TPU v7x, 32 devices: a whole 2x2x4 slice. The times are simulated.
32 devices in a mesh: blk: 16 (over z, y, x), rep: 2 (over core).
Axes of the slice: x: 2, y: 2, z: 4, core: 2. Of those that a mesh axis runs over, the one named last changes fastest.
Arguments:
- features: bfloat16 [16384, 128], P(('blk', 'rep')), may hold values from -6 to 6
- cotangent: bfloat16 [16384, 256], P(('blk', 'rep')), may hold values from -0.046875 to 0.046875
- self_weight: float32 [16384], P('blk'), may hold values from 0.2 to 1
- w_first: bfloat16 [128, 256], replicated, may hold values from -0.5 to 0.5
- b_first: float32 [256], replicated, may hold values from -4 to 4
- w_second: bfloat16 [256, 256], replicated, may hold values from -0.375 to 0.375
- block_row: int32 [16, 16, 12], P('blk', 'rep'), may hold values from 0 to 127, as said below
- block_col: int32 [16, 16, 12], P('blk', 'rep'), may hold values from 0 to 127, as said below
- block_slot: int32 [16, 16, 12], P('blk', 'rep'), may hold values from 0 to 11, as said below
- block_count: int32 [16, 16], P('blk', 'rep'), may hold values from 0 to 12, as said below
- block_values: bfloat16 [16, 16, 12, 128, 128], P('blk', 'rep'), as said below
Outputs:
- grad_w1: float32 [128, 256], replicated
- grad_b1: float32 [256], replicated
- grad_w2: float32 [256, 256], replicated
Inputs may be any that keep to these rules, and one draw needn't show every extreme that they name: `block_row`: entry k of partition p at distance d names a row block of partition p, from p * 8 to p * 8 + 7; entries with k >= block_count[p, d] are ignored. `block_col`: entry k of partition p at distance d names a column block of partition (p - d) mod 16; no block appears twice among counted entries; block (a, b) is counted if and only if block (b, a) is. `block_slot`: for each partition and distance the 12 slots form a permutation of 0 to 11. `block_count`: some partitions fill all 12 slots at some distance in every draw. `block_values`: the values of block (a, b) are the transpose of those of block (b, a); a block on the diagonal is symmetric.
All inputs are finite; a program needn't handle non-finite values.
Results may differ from a plain program's by a relative error of at most 0.00068.
Values may be sent and summed in bfloat16 or wider, within the bound.
No kernel may reach another device: no remote copies, remote signals or barrier semaphores. Data moves between devices by JAX's collectives and lax.ppermute only.
A program may use at most 64 MiB of HBM per device.

v0:
```python
import jax
import jax.numpy as jnp
from jax import lax
from jax.sharding import PartitionSpec as P


def passed_along(value, axis, steps):
    count = lax.axis_size(axis)
    pairs = [(source, (source + steps) % count) for source in range(count)]
    return lax.ppermute(value, axis, pairs)


def contribute(running, panel_now, position, tables):
    local_rows, local_cols, live_mask, ordered = tables
    row_ids = lax.dynamic_index_in_dim(local_rows, position, 0, keepdims=False)
    col_ids = lax.dynamic_index_in_dim(local_cols, position, 0, keepdims=False)
    live_now = lax.dynamic_index_in_dim(live_mask, position, 0, keepdims=False)
    blocks = lax.dynamic_index_in_dim(ordered, position, 0, keepdims=False)
    picked = jnp.take(panel_now, col_ids, axis=0)
    product = jnp.einsum("mab,mbf->maf", blocks, picked, preferred_element_type=jnp.float32)
    row_range = jnp.arange(panel_now.shape[0], dtype=jnp.int32)
    onehot = jnp.where(row_ids[None, :] == row_range[:, None], live_now[None, :], 0.0)
    return running + jnp.einsum("rm,maf->raf", onehot, product, precision=lax.Precision.HIGHEST)


def shards(
    features,
    cotangent,
    self_weight,
    w_first,
    b_first,
    w_second,
    block_row,
    block_col,
    block_slot,
    block_count,
    block_values,
):
    rep_index = lax.axis_index("rep")
    bit_count = lax.axis_size("rep").bit_length() - 1
    cycle_steps = block_values.shape[1]
    most_blocks = block_values.shape[2]
    block_size = block_values.shape[3]
    in_width = features.shape[1]
    hid_width = cotangent.shape[1]
    x_full, g_full = (
        lax.all_gather(features, "rep", axis=0, tiled=True),
        lax.all_gather(cotangent, "rep", axis=0, tiled=True),
    )
    rows_total = x_full.shape[0]
    row_blocks = rows_total // block_size
    live_mask = jnp.where(
        jnp.arange(most_blocks, dtype=jnp.int32)[None, :] < block_count[0][:, None], 1.0, 0.0
    ).astype(jnp.float32)
    ordered = jnp.take_along_axis(block_values[0], block_slot[0][:, :, None, None], axis=1)
    tables = (block_row[0] % row_blocks, block_col[0] % row_blocks, live_mask, ordered)
    x_panel = x_full.reshape(row_blocks, block_size, in_width)
    g_panel = g_full.reshape(row_blocks, block_size, hid_width)
    moving_x = x_panel
    for bit_level in range(bit_count):
        shifted_x = passed_along(moving_x, "blk", cycle_steps << bit_level)
        moving_x = jnp.where(rep_index >> bit_level & 1 == 1, shifted_x, moving_x)
    first_x = contribute(
        jnp.zeros((row_blocks, block_size, in_width), jnp.float32), moving_x, 0, tables
    )

    def walk_x(position, loop_state):
        held_panel, running = loop_state
        held_panel = passed_along(held_panel, "blk", 1)
        return (held_panel, contribute(running, held_panel, position, tables))

    total_x = lax.fori_loop(1, cycle_steps, walk_x, (moving_x, first_x))[1]
    moving_g = g_panel
    for bit_level in range(bit_count):
        shifted_g = passed_along(moving_g, "blk", cycle_steps << bit_level)
        moving_g = jnp.where(rep_index >> bit_level & 1 == 1, shifted_g, moving_g)
    first_g = contribute(
        jnp.zeros((row_blocks, block_size, hid_width), jnp.float32), moving_g, 0, tables
    )

    def walk_g(position, loop_state):
        held_panel, running = loop_state
        held_panel = passed_along(held_panel, "blk", 1)
        return (held_panel, contribute(running, held_panel, position, tables))

    total_g = lax.fori_loop(1, cycle_steps, walk_g, (moving_g, first_g))[1]
    part_x_all = total_x.reshape(rows_total, in_width)
    part_g_all = total_g.reshape(rows_total, hid_width)
    part_x, part_g = lax.psum((part_x_all, part_g_all), "rep")
    aggregated = (part_x + self_weight[:, None] * x_full.astype(jnp.float32)).astype(jnp.bfloat16)
    pre_act = jnp.dot(aggregated, w_first, preferred_element_type=jnp.float32) + b_first
    hidden = jax.nn.silu(pre_act).astype(jnp.bfloat16)
    back_agg = (part_g + self_weight[:, None] * g_full.astype(jnp.float32)).astype(jnp.bfloat16)
    grad_w2 = jnp.einsum("nh,nk->hk", hidden, back_agg, preferred_element_type=jnp.float32)
    squashed = jax.nn.sigmoid(pre_act)
    d_hidden = jnp.einsum("nk,hk->nh", back_agg, w_second, preferred_element_type=jnp.float32)
    grad_pre = (d_hidden * squashed * (1.0 + pre_act * (1.0 - squashed))).astype(jnp.bfloat16)
    grad_w1 = jnp.einsum("nf,nh->fh", aggregated, grad_pre, preferred_element_type=jnp.float32)
    grad_b1 = jnp.sum(grad_pre.astype(jnp.float32), axis=0)
    grad_w1, grad_b1, grad_w2 = lax.psum((grad_w1, grad_b1, grad_w2), "blk")
    return (grad_w1, grad_b1, grad_w2)


def solution(mesh):
    placed = (
        P(("blk", "rep"), None),
        P(("blk", "rep"), None),
        P("blk"),
        P(),
        P(),
        P(),
        P("blk", "rep", None),
        P("blk", "rep", None),
        P("blk", "rep", None),
        P("blk", "rep"),
        P("blk", "rep", None, None, None),
    )
    return jax.shard_map(
        shards, mesh=mesh, in_specs=placed, out_specs=(P(), P(), P()), check_vma=False
    )
```

profile of v0, /device:TPU:0, one launch (start us, length us, event | category | flops | bytes accessed | tf_op | source)
XLA Modules:
  0.0 490.2 jit_solution(18344005673973344078)
XLA Ops:
  7.2 4.4 all_gather.7
  11.6 3.7 collective-permute-start.3
  22.2 3.1 gather_fusion.2
  25.3 3.9 broadcast_select_fusion
  29.8 20.8 %collective-permute-done.2 = bf16[8,128,128]{2,1,0:T(8,128)(2,1)} collective-permute-done((bf16[8,128,128]{2,1,0:T(8,128)(2,1)S(1)}, bf16[8,128,128]{2,1,0:T(8,128)(2,1)}, u32[]{:S(2)}, u32[]{:S(2)}) %collective-permute-start.2) | collective-permute-done | bytes 262176 | tf_op jit(solution)/shard_map/ppermute | solution.py:10
  56.8 122.5 %while.34 = (s32[]{:T(128)}, bf16[8,128,128]{2,1,0:T(8,128)(2,1)}, f32[8,128,128]{2,0,1:T(8,128)}, s32[8,12]{1,0:T(8,128)S(1)}, f32[8,12]{1,0:T(8,128)S(1)}, /*i...) while((s32[]{:T(128)}, bf16[8,128,128]{2,1,0:T(8,128)(2,1)}, ...), condition=%wide.region_1.3_spmd, body=%wide.region_0.0_spmd.sunk | while | flops 69534992 | bytes 5771967 | solution.py:72
  58.4 11.3 %collective-permute-done = bf16[8,128,128]{2,1,0:T(8,128)(2,1)S(1)} collective-permute-done((bf16[8,128,128]{2,1,0:T(8,128)(2,1)}, bf16[8,128,128]{2,1,0:T(8,128)(2,1)S(1)}, u32[]{:S(2)}, u32[]{:S(2)}) %collective-permute-start) | collective-permute-done | bytes 262176 | tf_op jit(solution)/shard_map/while/body/eval_jaxpr/ppermute | solution.py:10
  72.5 2.9 convolution_add_fusion.3
  76.2 12.1 %collective-permute-done = bf16[8,128,128]{2,1,0:T(8,128)(2,1)S(1)} collective-permute-done((bf16[8,128,128]{2,1,0:T(8,128)(2,1)}, bf16[8,128,128]{2,1,0:T(8,128)(2,1)S(1)}, u32[]{:S(2)}, u32[]{:S(2)}) %collective-permute-start) | collective-permute-done | bytes 262176 | tf_op jit(solution)/shard_map/while/body/eval_jaxpr/ppermute | solution.py:10
  91.1 2.9 convolution_add_fusion.3
  94.8 11.2 %collective-permute-done = bf16[8,128,128]{2,1,0:T(8,128)(2,1)S(1)} collective-permute-done((bf16[8,128,128]{2,1,0:T(8,128)(2,1)}, bf16[8,128,128]{2,1,0:T(8,128)(2,1)S(1)}, u32[]{:S(2)}, u32[]{:S(2)}) %collective-permute-start) | collective-permute-done | bytes 262176 | tf_op jit(solution)/shard_map/while/body/eval_jaxpr/ppermute | solution.py:10
  108.9 2.9 convolution_add_fusion.3
  112.6 10.3 %collective-permute-done = bf16[8,128,128]{2,1,0:T(8,128)(2,1)S(1)} collective-permute-done((bf16[8,128,128]{2,1,0:T(8,128)(2,1)}, bf16[8,128,128]{2,1,0:T(8,128)(2,1)S(1)}, u32[]{:S(2)}, u32[]{:S(2)}) %collective-permute-start) | collective-permute-done | bytes 262176 | tf_op jit(solution)/shard_map/while/body/eval_jaxpr/ppermute | solution.py:10
  125.7 2.9 convolution_add_fusion.3
  129.4 10.1 %collective-permute-done = bf16[8,128,128]{2,1,0:T(8,128)(2,1)S(1)} collective-permute-done((bf16[8,128,128]{2,1,0:T(8,128)(2,1)}, bf16[8,128,128]{2,1,0:T(8,128)(2,1)S(1)}, u32[]{:S(2)}, u32[]{:S(2)}) %collective-permute-start) | collective-permute-done | bytes 262176 | tf_op jit(solution)/shard_map/while/body/eval_jaxpr/ppermute | solution.py:10
  142.4 2.9 convolution_add_fusion.3
  146.1 10.1 %collective-permute-done = bf16[8,128,128]{2,1,0:T(8,128)(2,1)S(1)} collective-permute-done((bf16[8,128,128]{2,1,0:T(8,128)(2,1)}, bf16[8,128,128]{2,1,0:T(8,128)(2,1)S(1)}, u32[]{:S(2)}, u32[]{:S(2)}) %collective-permute-start) | collective-permute-done | bytes 262176 | tf_op jit(solution)/shard_map/while/body/eval_jaxpr/ppermute | solution.py:10
  159.0 2.9 convolution_add_fusion.3
  162.7 10.1 %collective-permute-done = bf16[8,128,128]{2,1,0:T(8,128)(2,1)S(1)} collective-permute-done((bf16[8,128,128]{2,1,0:T(8,128)(2,1)}, bf16[8,128,128]{2,1,0:T(8,128)(2,1)S(1)}, u32[]{:S(2)}, u32[]{:S(2)}) %collective-permute-start) | collective-permute-done | bytes 262176 | tf_op jit(solution)/shard_map/while/body/eval_jaxpr/ppermute | solution.py:10
  175.7 2.9 convolution_add_fusion.3
  187.5 3.0 fusion.40
  190.5 154.2 %while.35 = (s32[]{:T(128)}, bf16[8,128,256]{2,1,0:T(8,128)(2,1)}, f32[8,128,256]{2,0,1:T(8,128)}, s32[8,12]{1,0:T(8,128)S(1)}, f32[8,12]{1,0:T(8,128)S(1)}, /*i...) while((s32[]{:T(128)}, bf16[8,128,256]{2,1,0:T(8,128)(2,1)}, ...), condition=%wide.region_4.7_spmd, body=%wide.region_3.6_spmd.sunk | while | flops 139068688 | bytes 19534584 | solution.py:86
  190.6 13.0 %collective-permute-done.1 = bf16[8,128,256]{2,1,0:T(8,128)(2,1)} collective-permute-done((bf16[8,128,256]{2,1,0:T(8,128)(2,1)}, bf16[8,128,256]{2,1,0:T(8,128)(2,1)}, u32[]{:S(2)}, u32[]{:S(2)}) %collective-permute-start.1) | collective-permute-done | bytes 524320 | tf_op jit(solution)/shard_map/while/body/eval_jaxpr/ppermute | solution.py:10
  212.6 13.0 %collective-permute-done.1 = bf16[8,128,256]{2,1,0:T(8,128)(2,1)} collective-permute-done((bf16[8,128,256]{2,1,0:T(8,128)(2,1)}, bf16[8,128,256]{2,1,0:T(8,128)(2,1)}, u32[]{:S(2)}, u32[]{:S(2)}) %collective-permute-start.1) | collective-permute-done | bytes 524320 | tf_op jit(solution)/shard_map/while/body/eval_jaxpr/ppermute | solution.py:10
  234.6 13.0 %collective-permute-done.1 = bf16[8,128,256]{2,1,0:T(8,128)(2,1)} collective-permute-done((bf16[8,128,256]{2,1,0:T(8,128)(2,1)}, bf16[8,128,256]{2,1,0:T(8,128)(2,1)}, u32[]{:S(2)}, u32[]{:S(2)}) %collective-permute-start.1) | collective-permute-done | bytes 524320 | tf_op jit(solution)/shard_map/while/body/eval_jaxpr/ppermute | solution.py:10
  256.7 13.0 %collective-permute-done.1 = bf16[8,128,256]{2,1,0:T(8,128)(2,1)} collective-permute-done((bf16[8,128,256]{2,1,0:T(8,128)(2,1)}, bf16[8,128,256]{2,1,0:T(8,128)(2,1)}, u32[]{:S(2)}, u32[]{:S(2)}) %collective-permute-start.1) | collective-permute-done | bytes 524320 | tf_op jit(solution)/shard_map/while/body/eval_jaxpr/ppermute | solution.py:10
  278.7 13.0 %collective-permute-done.1 = bf16[8,128,256]{2,1,0:T(8,128)(2,1)} collective-permute-done((bf16[8,128,256]{2,1,0:T(8,128)(2,1)}, bf16[8,128,256]{2,1,0:T(8,128)(2,1)}, u32[]{:S(2)}, u32[]{:S(2)}) %collective-permute-start.1) | collective-permute-done | bytes 524320 | tf_op jit(solution)/shard_map/while/body/eval_jaxpr/ppermute | solution.py:10
  300.7 13.0 %collective-permute-done.1 = bf16[8,128,256]{2,1,0:T(8,128)(2,1)} collective-permute-done((bf16[8,128,256]{2,1,0:T(8,128)(2,1)}, bf16[8,128,256]{2,1,0:T(8,128)(2,1)}, u32[]{:S(2)}, u32[]{:S(2)}) %collective-permute-start.1) | collective-permute-done | bytes 524320 | tf_op jit(solution)/shard_map/while/body/eval_jaxpr/ppermute | solution.py:10
  322.8 13.0 %collective-permute-done.1 = bf16[8,128,256]{2,1,0:T(8,128)(2,1)} collective-permute-done((bf16[8,128,256]{2,1,0:T(8,128)(2,1)}, bf16[8,128,256]{2,1,0:T(8,128)(2,1)}, u32[]{:S(2)}, u32[]{:S(2)}) %collective-permute-start.1) | collective-permute-done | bytes 524320 | tf_op jit(solution)/shard_map/while/body/eval_jaxpr/ppermute | solution.py:10
  347.4 16.4 %all-reduce.7.cloned.1.call-done = (f32[1024,128]{1,0:T(8,128)}, f32[1024,256]{1,0:T(8,128)}) async-done(((f32[1024,128]{1,0:T(8,128)}, f32[1024,256]{1,0:T(8,128)}), (f32[1024,128]{1,0:T(8,128)}, f32[1024,256]{1,0:T(8,128)})) %all-reduce.7.cloned.1.call-update) | async-done | bytes 1572880 | tf_op jit(solution)/shard_map/psum | solution.py:89
  369.7 42.8 %psum.38 = f32[256]{0:T(256)} all-reduce(f32[256]{0:T(256)S(1)} %get-tuple-element.397), channel_id=1, replica_groups=mesh['blk'=16,'rep'=2] {'blk'}, use_global_device_ids=true, to_apply=%region_8.11 | all-reduce | flops 256 | bytes 2048 | tf_op jit(solution)/shard_map/psum | solution.py:100
  412.5 67.7 %all-reduce.5.cloned.1.call-done = (f32[128,256]{1,0:T(8,128)}, f32[256,256]{1,0:T(8,128)}) async-done(((f32[128,256]{1,0:T(8,128)}, f32[256,256]{1,0:T(8,128)}), (f32[128,256]{1,0:T(8,128)}, f32[256,256]{1,0:T(8,128)})) %all-reduce.5.cloned.1.call-update) | async-done | bytes 393232 | tf_op jit(solution)/shard_map/psum | solution.py:100
  (201 shorter events, 122.6 us)
Async XLA Ops:
  7.2 15.0 %copy-start = (bf16[1,8,12,128,128]{4,3,2,1,0:T(8,128)(2,1)S(1)}, bf16[1,8,12,128,128]{4,3,2,1,0:T(8,128)(2,1)}, u32[]{:S(2)}) copy-start(bf16[1,8,12,128,128]{4,3,2,1,0:T(8,128)(2,1)} %param.29) | copy-start | bytes 9437188
  7.2 356.7 %all-reduce.7.cloned.1.call-start = ((), (), s32[]{:S(2)}) async-start(), calls=%async_computation.1 | async-start | bytes 3145728 | tf_op jit(solution)/shard_map/psum | solution.py:89
  11.6 169.7 %collective-permute-start.3 = (bf16[8,128,256]{2,1,0:T(8,128)(2,1)}, bf16[8,128,256]{2,1,0:T(8,128)(2,1)}, u32[]{:S(2)}, u32[]{:S(2)}) collective-permute-start(bf16[8,128,256]{2,1,0:T(8,128)(2,1)} %bitcast.24), channel_id=1, source_target_pairs={{0,16},{2,18},{4,20},{6,22},{8,24},{10,26},{12,28},{14,30},{16,0},... | collective-permute-start | bytes 1572872 | tf_op jit(solution)/shard_map/ppermute | solution.py:10
  17.6 33.0 %copy-start.3 = (bf16[1024,128]{1,0:T(8,128)(2,1)}, bf16[1024,128]{1,0:T(8,128)(2,1)S(1)}, u32[]{:S(2)}) copy-start(bf16[1024,128]{1,0:T(8,128)(2,1)S(1)} %all_gather.6) | copy-start | bytes 786436
  17.6 33.0 %collective-permute-start.2 = (bf16[8,128,128]{2,1,0:T(8,128)(2,1)S(1)}, bf16[8,128,128]{2,1,0:T(8,128)(2,1)}, u32[]{:S(2)}, u32[]{:S(2)}) collective-permute-start(bf16[8,128,128]{2,1,0:T(8,128)(2,1)S(1)} %bitcast.95), channel_id=1, source_target_pairs={{0,16},{2,18},{4,20},{6,22},{8,24},{10,26},{12,28},{14,30},{16,0},... | collective-permute-start | bytes 786440 | tf_op jit(solution)/shard_map/ppermute | solution.py:10
  56.8 12.9 %collective-permute-start = (bf16[8,128,128]{2,1,0:T(8,128)(2,1)}, bf16[8,128,128]{2,1,0:T(8,128)(2,1)S(1)}, u32[]{:S(2)}, u32[]{:S(2)}) collective-permute-start(bf16[8,128,128]{2,1,0:T(8,128)(2,1)} %get-tuple-element.504), channel_id=1, source_target_pairs={{0,2},{2,4},{4,6},{6,8},{8,10},{10,12},{12,14},{14,16},{16,18},{18... | collective-permute-start | bytes 786440 | tf_op jit(solution)/shard_map/while/body/eval_jaxpr/ppermute | solution.py:10
  76.1 12.1 %collective-permute-start = (bf16[8,128,128]{2,1,0:T(8,128)(2,1)}, bf16[8,128,128]{2,1,0:T(8,128)(2,1)S(1)}, u32[]{:S(2)}, u32[]{:S(2)}) collective-permute-start(bf16[8,128,128]{2,1,0:T(8,128)(2,1)} %get-tuple-element.504), channel_id=1, source_target_pairs={{0,2},{2,4},{4,6},{6,8},{8,10},{10,12},{12,14},{14,16},{16,18},{18... | collective-permute-start | bytes 786440 | tf_op jit(solution)/shard_map/while/body/eval_jaxpr/ppermute | solution.py:10
  94.8 11.3 %collective-permute-start = (bf16[8,128,128]{2,1,0:T(8,128)(2,1)}, bf16[8,128,128]{2,1,0:T(8,128)(2,1)S(1)}, u32[]{:S(2)}, u32[]{:S(2)}) collective-permute-start(bf16[8,128,128]{2,1,0:T(8,128)(2,1)} %get-tuple-element.504), channel_id=1, source_target_pairs={{0,2},{2,4},{4,6},{6,8},{8,10},{10,12},{12,14},{14,16},{16,18},{18... | collective-permute-start | bytes 786440 | tf_op jit(solution)/shard_map/while/body/eval_jaxpr/ppermute | solution.py:10
  112.5 10.4 %collective-permute-start = (bf16[8,128,128]{2,1,0:T(8,128)(2,1)}, bf16[8,128,128]{2,1,0:T(8,128)(2,1)S(1)}, u32[]{:S(2)}, u32[]{:S(2)}) collective-permute-start(bf16[8,128,128]{2,1,0:T(8,128)(2,1)} %get-tuple-element.504), channel_id=1, source_target_pairs={{0,2},{2,4},{4,6},{6,8},{8,10},{10,12},{12,14},{14,16},{16,18},{18... | collective-permute-start | bytes 786440 | tf_op jit(solution)/shard_map/while/body/eval_jaxpr/ppermute | solution.py:10
  129.4 10.2 %collective-permute-start = (bf16[8,128,128]{2,1,0:T(8,128)(2,1)}, bf16[8,128,128]{2,1,0:T(8,128)(2,1)S(1)}, u32[]{:S(2)}, u32[]{:S(2)}) collective-permute-start(bf16[8,128,128]{2,1,0:T(8,128)(2,1)} %get-tuple-element.504), channel_id=1, source_target_pairs={{0,2},{2,4},{4,6},{6,8},{8,10},{10,12},{12,14},{14,16},{16,18},{18... | collective-permute-start | bytes 786440 | tf_op jit(solution)/shard_map/while/body/eval_jaxpr/ppermute | solution.py:10
  146.0 10.2 %collective-permute-start = (bf16[8,128,128]{2,1,0:T(8,128)(2,1)}, bf16[8,128,128]{2,1,0:T(8,128)(2,1)S(1)}, u32[]{:S(2)}, u32[]{:S(2)}) collective-permute-start(bf16[8,128,128]{2,1,0:T(8,128)(2,1)} %get-tuple-element.504), channel_id=1, source_target_pairs={{0,2},{2,4},{4,6},{6,8},{8,10},{10,12},{12,14},{14,16},{16,18},{18... | collective-permute-start | bytes 786440 | tf_op jit(solution)/shard_map/while/body/eval_jaxpr/ppermute | solution.py:10
  162.7 10.2 %collective-permute-start = (bf16[8,128,128]{2,1,0:T(8,128)(2,1)}, bf16[8,128,128]{2,1,0:T(8,128)(2,1)S(1)}, u32[]{:S(2)}, u32[]{:S(2)}) collective-permute-start(bf16[8,128,128]{2,1,0:T(8,128)(2,1)} %get-tuple-element.504), channel_id=1, source_target_pairs={{0,2},{2,4},{4,6},{6,8},{8,10},{10,12},{12,14},{14,16},{16,18},{18... | collective-permute-start | bytes 786440 | tf_op jit(solution)/shard_map/while/body/eval_jaxpr/ppermute | solution.py:10
  179.3 6.5 %copy-start.7 = (pred[12]{0:T(512)(128)(4,1)S(1)}, pred[12]{0:T(512)(128)(4,1)}, u32[]{:S(2)}) copy-start(pred[12]{0:T(512)(128)(4,1)} %get-tuple-element.395) | copy-start | bytes 40
  181.3 6.2 %copy-start.8 = (f32[12]{0:T(128)S(1)}, f32[12]{0:T(128)}, u32[]{:S(2)}) copy-start(f32[12]{0:T(128)} %slice_bitcast_fusion.3) | copy-start | bytes 148
  181.3 6.2 %copy-start.9 = (s32[12]{0:T(128)S(1)}, s32[12]{0:T(128)}, u32[]{:S(2)}) copy-start(s32[12]{0:T(128)} %slice_bitcast_fusion.4) | copy-start | bytes 148
  190.5 13.1 %collective-permute-start.1 = (bf16[8,128,256]{2,1,0:T(8,128)(2,1)}, bf16[8,128,256]{2,1,0:T(8,128)(2,1)}, u32[]{:S(2)}, u32[]{:S(2)}) collective-permute-start(bf16[8,128,256]{2,1,0:T(8,128)(2,1)} %get-tuple-element.534), channel_id=1, source_target_pairs={{0,2},{2,4},{4,6},{6,8},{8,10},{10,12},{12,14},{14,16},{16,18},{18... | collective-permute-start | bytes 1572872 | tf_op jit(solution)/shard_map/while/body/eval_jaxpr/ppermute | solution.py:10
  210.3 2.3 copy-start.2
  212.5 13.1 %collective-permute-start.1 = (bf16[8,128,256]{2,1,0:T(8,128)(2,1)}, bf16[8,128,256]{2,1,0:T(8,128)(2,1)}, u32[]{:S(2)}, u32[]{:S(2)}) collective-permute-start(bf16[8,128,256]{2,1,0:T(8,128)(2,1)} %get-tuple-element.534), channel_id=1, source_target_pairs={{0,2},{2,4},{4,6},{6,8},{8,10},{10,12},{12,14},{14,16},{16,18},{18... | collective-permute-start | bytes 1572872 | tf_op jit(solution)/shard_map/while/body/eval_jaxpr/ppermute | solution.py:10
  232.3 2.3 copy-start.2
  234.6 13.1 %collective-permute-start.1 = (bf16[8,128,256]{2,1,0:T(8,128)(2,1)}, bf16[8,128,256]{2,1,0:T(8,128)(2,1)}, u32[]{:S(2)}, u32[]{:S(2)}) collective-permute-start(bf16[8,128,256]{2,1,0:T(8,128)(2,1)} %get-tuple-element.534), channel_id=1, source_target_pairs={{0,2},{2,4},{4,6},{6,8},{8,10},{10,12},{12,14},{14,16},{16,18},{18... | collective-permute-start | bytes 1572872 | tf_op jit(solution)/shard_map/while/body/eval_jaxpr/ppermute | solution.py:10
  254.3 2.3 copy-start.2
  256.6 13.1 %collective-permute-start.1 = (bf16[8,128,256]{2,1,0:T(8,128)(2,1)}, bf16[8,128,256]{2,1,0:T(8,128)(2,1)}, u32[]{:S(2)}, u32[]{:S(2)}) collective-permute-start(bf16[8,128,256]{2,1,0:T(8,128)(2,1)} %get-tuple-element.534), channel_id=1, source_target_pairs={{0,2},{2,4},{4,6},{6,8},{8,10},{10,12},{12,14},{14,16},{16,18},{18... | collective-permute-start | bytes 1572872 | tf_op jit(solution)/shard_map/while/body/eval_jaxpr/ppermute | solution.py:10
  276.4 2.3 copy-start.2
  278.6 13.1 %collective-permute-start.1 = (bf16[8,128,256]{2,1,0:T(8,128)(2,1)}, bf16[8,128,256]{2,1,0:T(8,128)(2,1)}, u32[]{:S(2)}, u32[]{:S(2)}) collective-permute-start(bf16[8,128,256]{2,1,0:T(8,128)(2,1)} %get-tuple-element.534), channel_id=1, source_target_pairs={{0,2},{2,4},{4,6},{6,8},{8,10},{10,12},{12,14},{14,16},{16,18},{18... | collective-permute-start | bytes 1572872 | tf_op jit(solution)/shard_map/while/body/eval_jaxpr/ppermute | solution.py:10
  298.4 2.3 copy-start.2
  300.7 13.1 %collective-permute-start.1 = (bf16[8,128,256]{2,1,0:T(8,128)(2,1)}, bf16[8,128,256]{2,1,0:T(8,128)(2,1)}, u32[]{:S(2)}, u32[]{:S(2)}) collective-permute-start(bf16[8,128,256]{2,1,0:T(8,128)(2,1)} %get-tuple-element.534), channel_id=1, source_target_pairs={{0,2},{2,4},{4,6},{6,8},{8,10},{10,12},{12,14},{14,16},{16,18},{18... | collective-permute-start | bytes 1572872 | tf_op jit(solution)/shard_map/while/body/eval_jaxpr/ppermute | solution.py:10
  322.7 13.1 %collective-permute-start.1 = (bf16[8,128,256]{2,1,0:T(8,128)(2,1)}, bf16[8,128,256]{2,1,0:T(8,128)(2,1)}, u32[]{:S(2)}, u32[]{:S(2)}) collective-permute-start(bf16[8,128,256]{2,1,0:T(8,128)(2,1)} %get-tuple-element.534), channel_id=1, source_target_pairs={{0,2},{2,4},{4,6},{6,8},{8,10},{10,12},{12,14},{14,16},{16,18},{18... | collective-permute-start | bytes 1572872 | tf_op jit(solution)/shard_map/while/body/eval_jaxpr/ppermute | solution.py:10
  344.7 19.1 %copy-start.4 = (bf16[1024,128]{1,0:T(8,128)(2,1)S(1)}, bf16[1024,128]{1,0:T(8,128)(2,1)}, u32[]{:S(2)}) copy-start(bf16[1024,128]{1,0:T(8,128)(2,1)} %copy-done.3) | copy-start | bytes 786436
  344.7 19.1 %copy-start.6 = (f32[1024]{0:T(1024)S(1)}, f32[1024]{0:T(1024)}, u32[]{:S(2)}) copy-start(f32[1024]{0:T(1024)} %param.21) | copy-start | bytes 12292
  344.7 21.9 %copy-start.5 = (bf16[128,256]{1,0:T(8,128)(2,1)S(1)}, bf16[128,256]{1,0:T(8,128)(2,1)}, u32[]{:S(2)}) copy-start(bf16[128,256]{1,0:T(8,128)(2,1)} %param.22) | copy-start | bytes 196612
  344.7 21.9 %copy-start.10 = (f32[256]{0:T(256)S(1)}, f32[256]{0:T(256)}, u32[]{:S(2)}) copy-start(f32[256]{0:T(256)} %param.23) | copy-start | bytes 3076
  347.4 132.8 %all-reduce.5.cloned.1.call-start = ((), (), s32[]{:S(2)}) async-start(), calls=%async_computation | async-start | bytes 786432 | tf_op jit(solution)/shard_map/psum | solution.py:100
  (10 other events, 18.5 us)
Sparse Core Ops, SparseCore 0:
  347.5 16.3 all-reduce.6
  370.6 109.5 all-reduce.4
where the time goes:
time: 492 us; the launch traced here: 490 us
  waiting for transfers between devices  271 us (55%)
  matrix products  70.8 us (14%)
  local copies, waits for them, and re-layouts  64.7 us (13%)
  blocking collectives  49.4 us (10%)
  between operations  14.2 us (3%)
  other arithmetic  13.7 us (3%)
  starting transfers between devices  5.42 us (1%)
    ppermute x16, waiting for transfers between devices, passed_along(): return lax.ppermute(value, axis, pairs)  187 us
    psum x1, waiting for transfers between devices, shards(): grad_w1, grad_b1, grad_w2 = lax.psum((grad_w1, grad_b1, grad_w2), 'blk')  67.7 us
    psum x1, blocking collectives, shards(): grad_w1, grad_b1, grad_w2 = lax.psum((grad_w1, grad_b1, grad_w2), 'blk')  42.8 us
    dot_general x16, matrix products, contribute(): jnp.einsum('rm,maf->raf', onehot, product, precision=lax.Precision.HIGHEST)  42.3 us
    gather x16, local copies, waits for them, and re-layouts, contribute(): picked = jnp.take(panel_now, col_ids, axis=0)  31.7 us
    dot_general x16, matrix products, contribute(): jnp.einsum('mab,mbf->maf', blocks, picked, preferred_element_type=jnp.flo...  25.6 us
    while x42, local copies, waits for them, and re-layouts  20.8 us
    psum x1, waiting for transfers between devices, shards(): part_x, part_g = lax.psum((part_x_all, part_g_all), 'rep')  16.4 us
  transfers between devices with their start and end apart: 18, of which 17 were waited for; matrix products, arithmetic and copies ran while one was open for 13% of the time, Pallas kernels for 0%

commit v1 on v0

--- a/solution.py
+++ b/solution.py
@@ -1,6 +1,10 @@
+import functools
+
 import jax
 import jax.numpy as jnp
 from jax import lax
+from jax.experimental import pallas as pl
+from jax.experimental.pallas import tpu as pltpu
 from jax.sharding import PartitionSpec as P
 
 
@@ -23,7 +27,7 @@
     return running + jnp.einsum("rm,maf->raf", onehot, product, precision=lax.Precision.HIGHEST)
 
 
-def shards(
+def walk_shards(
     features,
     cotangent,
     self_weight,
@@ -100,6 +104,320 @@
     grad_w1, grad_b1, grad_w2 = lax.psum((grad_w1, grad_b1, grad_w2), "blk")
     return (grad_w1, grad_b1, grad_w2)
 
+BF16, F32, I32 = jnp.bfloat16, jnp.float32, jnp.int32
+LANES = 128
+VMEM_SPEC = pl.BlockSpec(memory_space=pltpu.VMEM)
+SMEM_SPEC = pl.BlockSpec(memory_space=pltpu.SMEM)
+ANY_SPEC = pl.BlockSpec(memory_space=pl.ANY)
+
+
+def send(value, target):
+    pairs = []
+    for p in range(16):
+        for r in range(2):
+            to = target(p, r)
+            if to is not None:
+                pairs.append((p * 2 + r, to[0] * 2 + to[1]))
+    return lax.ppermute(value, ("blk", "rep"), pairs)
+
+
+def to_sibling(value):
+    return send(value, lambda p, r: (p, 1 - r))
+
+
+def first_way(value):
+    return send(value, lambda p, r: (p ^ (1 + r), r))
+
+
+def second_way(value):
+    return send(value, lambda p, r: (p ^ (2 - r), r))
+
+
+def z_pairs(value):
+    return send(value, lambda p, r: (p ^ 4, r))
+
+
+def z_middle(value):
+    return send(value, lambda p, r: (p ^ 12, r) if p // 4 in (1, 2) else None)
+
+
+def z_outward(value):
+    return send(value, lambda p, r: (p ^ 4, r) if p // 4 in (1, 2) else None)
+
+
+def assemble_kernel(place, feat, cot, got_tile, got_first, panel):
+    core = place[1]
+    half = feat.shape[0]
+    rolled = pltpu.roll(got_first[...].astype(F32), LANES // 2, 1).astype(BF16)
+    lane = lax.broadcasted_iota(I32, (half, LANES), 1)
+    mine = cot[:, :LANES]
+
+    @pl.when(core == 0)
+    def _():
+        panel[0:half, :] = feat[...]
+        panel[half : 2 * half, :] = got_tile[...]
+        panel[2 * half :, :] = jnp.where(lane < LANES // 2, mine, rolled)
+
+    @pl.when(core == 1)
+    def _():
+        panel[0:half, :] = got_tile[...]
+        panel[half : 2 * half, :] = cot[:, LANES:]
+        panel[2 * half :, :] = jnp.where(lane < LANES // 2, rolled, mine)
+
+
+def entry_of(place, kind):
+    step_one, step_two, slot = kind
+    p, core = place[0], place[1]
+    z, w = p >> 2, p & 3
+    if step_one:
+        w = w ^ (1 + core)
+    if step_two:
+        w = w ^ (2 - core)
+    upper = z >> 1
+    z = (z, z ^ 1, 2 - upper, 3 - 3 * upper)[slot]
+    d = (p - (z * 4 + w)) & 15
+    return (d >> 3) ^ core, d & 7
+
+
+def gather_kernel(kinds, first, last, place, table, start, own, other, *rest):
+    n = len(kinds)
+    panels, (out, acc, xbuf, abuf, sems) = rest[:n], rest[n:]
+    blocks = acc.shape[1]
+    size = acc.shape[2]
+    rows = blocks * size
+    half = rows // 2
+    where = [entry_of(place, kind) for kind in kinds]
+    if not first:
+        start_copy = pltpu.make_async_copy(start, acc, sems.at[2, 0])
+        start_copy.start()
+    for j in range(n):
+        away, dist = where[j]
+        pltpu.make_async_copy(panels[j], xbuf.at[j], sems.at[0, j]).start()
+
+        @pl.when(away == 0)
+        def _():
+            pltpu.make_async_copy(own.at[dist], abuf.at[j], sems.at[1, j]).start()
+
+        @pl.when(away != 0)
+        def _():
+            pltpu.make_async_copy(other.at[dist], abuf.at[j], sems.at[1, j]).start()
+
+    if not first:
+        start_copy.wait()
+    for j in range(n):
+        away, dist = where[j]
+        base = (away * 8 + dist) * 16
+        pltpu.make_async_copy(panels[j], xbuf.at[j], sems.at[0, j]).wait()
+        pltpu.make_async_copy(own.at[0], abuf.at[j], sems.at[1, j]).wait()
+        if first and j == 0:
+            for b in range(blocks):
+                weight = start[b * size : (b + 1) * size, :]
+                side, at = b // (blocks // 2), b % (blocks // 2)
+                acc[0, b] = weight * xbuf[0, b * size : (b + 1) * size, :].astype(F32)
+                acc[1 + side, b] = weight * xbuf[0, rows + at * size : rows + (at + 1) * size, :].astype(F32)
+                acc[2 - side, b] = jnp.zeros((size, LANES), F32)
+
+        def block(k, carry):
+            entry = table[base + k]
+            row, col, slot = entry & 7, (entry >> 3) & 7, entry >> 6
+            tile = xbuf[j, pl.ds(pl.multiple_of(col * size, size), size), :]
+            pack = xbuf[j, pl.ds(pl.multiple_of(rows + (col & 3) * size, size), size), :]
+            product = jnp.dot(
+                abuf[j, slot], jnp.concatenate([tile, pack], axis=1), preferred_element_type=F32
+            )
+            acc[0, row] += product[:, :LANES]
+            acc[1 + (col >> 2), row] += product[:, LANES:]
+            return carry
+
+        lax.fori_loop(0, table[base + 12], block, 0)
+    if last:
+        core = place[1]
+        lane = lax.broadcasted_iota(I32, (size, LANES), 1)
+        valid = (lane < LANES // 2) == (core == 0)
+        for b in range(blocks):
+            out[b * size : (b + 1) * size, :] = acc[0, b].astype(BF16)
+            joined = acc[1, b] + pltpu.roll(acc[2, b], LANES // 2, 1)
+            turned = pltpu.roll(joined, LANES // 2, 1)
+            both = jnp.where(core == 0, joined, turned)
+            out[rows + b * size : rows + (b + 1) * size, :] = jnp.where(valid, both, 0.0).astype(BF16)
+    else:
+        pltpu.make_async_copy(acc, out, sems.at[2, 0]).start()
+        pltpu.make_async_copy(acc, out, sems.at[2, 0]).wait()
+
+
+def gather_call(kinds, first, last, place, table, start, own, other, panels):
+    n = len(kinds)
+    most, size = own.shape[1], own.shape[2]
+    rows = panels[0].shape[0] * 2 // 3
+    blocks = rows // size
+    acc_shape = (3, blocks, size, LANES)
+    out = (
+        jax.ShapeDtypeStruct((2 * rows, LANES), BF16) if last else jax.ShapeDtypeStruct(acc_shape, F32)
+    )
+    return pl.pallas_call(
+        functools.partial(gather_kernel, kinds, first, last),
+        out_shape=out,
+        in_specs=[SMEM_SPEC, SMEM_SPEC, VMEM_SPEC if first else ANY_SPEC] + [ANY_SPEC] * (2 + n),
+        out_specs=VMEM_SPEC if last else ANY_SPEC,
+        scratch_shapes=[
+            pltpu.VMEM(acc_shape, F32),
+            pltpu.VMEM((n, panels[0].shape[0], LANES), BF16),
+            pltpu.VMEM((n, most, size, size), BF16),
+            pltpu.SemaphoreType.DMA((3, n)),
+        ],
+        compiler_params=pltpu.CompilerParams(vmem_limit_bytes=24 << 20),
+        cost_estimate=pl.CostEstimate(
+            flops=n * 6 * 2 * size * size * 2 * LANES, bytes_accessed=n * 800000, transcendentals=0
+        ),
+    )(place, table, start, own, other, *panels)
+
+
+def dense_kernel(place, mine, theirs, w_one, bias, w_two, out):
+    core = place[1]
+    rows = mine.shape[0] // 2
+    agg = jnp.where(core == 0, mine[:rows, :], theirs[:rows, :])
+    upper = jnp.where(core == 0, theirs[:rows, :], mine[:rows, :])
+    back = jnp.concatenate([mine[rows:, :] + theirs[rows:, :], upper], axis=1)
+    pre = jnp.dot(agg, w_one[...], preferred_element_type=F32) + bias[...]
+    squashed = 1.0 / (1.0 + jnp.exp(-pre))
+    hidden = (pre * squashed).astype(BF16)
+    d_hidden = lax.dot_general(back, w_two[...], (((1,), (1,)), ((), ())), preferred_element_type=F32)
+    grad_pre = (d_hidden * squashed * (1.0 + pre * (1.0 - squashed))).astype(BF16)
+    over_rows = (((0,), (0,)), ((), ()))
+    two = lax.dot_general(hidden, back, over_rows, preferred_element_type=F32)
+    one = lax.dot_general(agg, grad_pre, over_rows, preferred_element_type=F32)
+    bias_row = jnp.sum(grad_pre.astype(F32), axis=0, keepdims=True)
+    quarter = one.shape[0] // 4
+    corner = place[0] & 3
+    for piece in range(4):
+        at = piece ^ corner
+        span = slice(piece * quarter, (piece + 1) * quarter)
+        out[at, 0:quarter, :] = one[span, :]
+        out[at, quarter : 2 * quarter, :] = two[span, :LANES]
+        out[at, 2 * quarter : 3 * quarter, :] = two[span, LANES:]
+        out[at, 3 * quarter :, :] = jnp.broadcast_to(bias_row, (8, LANES))
+
+
+def spread_kernel(place, *refs):
+    pieces, (one, bias, two) = refs[:8], refs[8:]
+    core, corner = place[1], place[0] & 3
+    quarter = one.shape[0] // 4
+    for k in range(4):
+        rows = pl.ds(pl.multiple_of((k ^ corner) * quarter, quarter), quarter)
+        below = pl.ds(pl.multiple_of(4 * quarter + (k ^ corner) * quarter, quarter), quarter)
+        mine, theirs = pieces[k], pieces[4 + k]
+        low = jnp.where(core == 0, mine[...], theirs[...])
+        high = jnp.where(core == 0, theirs[...], mine[...])
+        one[rows, :LANES] = low[:quarter, :]
+        one[rows, LANES:] = high[:quarter, :]
+        two[rows, :LANES] = low[quarter : 2 * quarter, :]
+        two[rows, LANES:] = low[2 * quarter : 3 * quarter, :]
+        two[below, :LANES] = high[quarter : 2 * quarter, :]
+        two[below, LANES:] = high[2 * quarter : 3 * quarter, :]
+        if k == 0:
+            bias[:, :LANES] = low[3 * quarter : 3 * quarter + 1, :]
+            bias[:, LANES:] = high[3 * quarter : 3 * quarter + 1, :]
+
+
+def mesh_shards(
+    features,
+    cotangent,
+    self_weight,
+    w_first,
+    b_first,
+    w_second,
+    block_row,
+    block_col,
+    block_slot,
+    block_count,
+    block_values,
+):
+    p, r = lax.axis_index("blk"), lax.axis_index("rep")
+    place = jnp.stack([p, r]).astype(I32)
+    even = r == 0
+    half = features.shape[0]
+    rows = 2 * half
+    size = block_values.shape[3]
+    blocks = rows // size
+    hid = w_first.shape[1]
+
+    got_tile = to_sibling(jnp.where(even, cotangent[:, LANES:], features))
+    got_first = to_sibling(cotangent[:, :LANES])
+    panel = pl.pallas_call(
+        assemble_kernel,
+        out_shape=jax.ShapeDtypeStruct((3 * half, LANES), BF16),
+        in_specs=[SMEM_SPEC] + [VMEM_SPEC] * 4,
+        out_specs=VMEM_SPEC,
+    )(place, features, cotangent, got_tile, got_first)
+
+    own = block_values[0]
+    other = to_sibling(own)
+    entries = block_row[0] % blocks + blocks * (block_col[0] % blocks) + blocks * blocks * block_slot[0]
+    filler = jnp.zeros((entries.shape[0], 16 - entries.shape[1] - 1), I32)
+    own_table = jnp.concatenate([entries, block_count[0][:, None], filler], axis=1)
+    table = jnp.concatenate([own_table, to_sibling(own_table)], axis=0).reshape(-1)
+    weights = jnp.broadcast_to(self_weight[:, None], (rows, LANES))
+
+    middle = (p // 4 == 1) | (p // 4 == 2)
+
+    def quad(value):
+        one = first_way(value)
+        return [value, one, second_way(value), second_way(one)]
+
+    slot_a = z_pairs(panel)
+    near = z_middle(panel)
+    group_o = quad(panel)
+    far = z_middle(slot_a)
+    group_a = quad(slot_a)
+    slot_b = jnp.where(middle, near, z_outward(near))
+    group_b = quad(slot_b)
+    slot_c = jnp.where(middle, far, z_outward(far))
+    group_c = quad(slot_c)
+    ways = [(0, 0), (1, 0), (0, 1), (1, 1)]
+
+    def kinds(slot):
+        return [way + (slot,) for way in ways]
+
+    acc = gather_call(
+        tuple(kinds(0) + kinds(1)), True, False, place, table, weights, own, other, group_o + group_a
+    )
+    summed = gather_call(
+        tuple(kinds(2) + kinds(3)), False, True, place, table, acc, own, other, group_b + group_c
+    )
+    from_sibling = to_sibling(summed)
+
+    side = hid // 2
+    w_one = lax.dynamic_slice_in_dim(w_first, r * side, side, 1)
+    bias = lax.dynamic_slice_in_dim(b_first, r * side, side, 0)[None, :]
+    w_two = lax.dynamic_slice_in_dim(w_second, r * side, side, 0)
+    pieces = pl.pallas_call(
+        dense_kernel,
+        out_shape=jax.ShapeDtypeStruct((4, 3 * side // 4 + 8, LANES), F32),
+        in_specs=[SMEM_SPEC] + [VMEM_SPEC] * 5,
+        out_specs=VMEM_SPEC,
+    )(place, summed, from_sibling, w_one, bias, w_two)
+
+    def in_plane(value, k):
+        return send(value, lambda p, r: (p ^ k, r))
+
+    got = [in_plane(pieces[k], k) for k in (1, 2, 3)]
+    total = (pieces[0] + got[0]) + (got[1] + got[2])
+    across = [in_plane(total, 4 * k) for k in (1, 2, 3)]
+    total = (total + across[0]) + (across[1] + across[2])
+    full = [total] + [in_plane(total, k) for k in (1, 2, 3)]
+    back = [to_sibling(value) for value in full]
+    grad_w1, grad_b1, grad_w2 = pl.pallas_call(
+        spread_kernel,
+        out_shape=(
+            jax.ShapeDtypeStruct((side, hid), F32),
+            jax.ShapeDtypeStruct((1, hid), F32),
+            jax.ShapeDtypeStruct((hid, hid), F32),
+        ),
+        in_specs=[SMEM_SPEC] + [VMEM_SPEC] * 8,
+        out_specs=(VMEM_SPEC,) * 3,
+    )(place, *full, *back)
+    return (grad_w1, grad_b1.reshape(hid), grad_w2)
+
 
 def solution(mesh):
     placed = (
@@ -115,6 +433,7 @@
         P("blk", "rep"),
         P("blk", "rep", None, None, None),
     )
+    fits = mesh.shape["blk"] == 16 and mesh.shape["rep"] == 2
     return jax.shard_map(
-        shards, mesh=mesh, in_specs=placed, out_specs=(P(), P(), P()), check_vma=False
-    )
+        mesh_shards if fits else walk_shards, mesh=mesh, in_specs=placed, out_specs=(P(), P(), P()), check_vma=False
+    )

time: 492 us -> 140 us (0.28)
  waiting for transfers between devices: 271 us -> 50.6 us
  matrix products: 70.8 us -> 0 us
  blocking collectives: 49.4 us -> 0 us
  local copies, waits for them, and re-layouts: 64.7 us -> 16.8 us
  starting transfers between devices: 5.42 us -> 38.9 us
  Pallas kernels: 0 us -> 25.4 us
  between operations: 14.2 us -> 0.97 us
  other arithmetic: 13.7 us -> 6.01 us
    ppermute x16 -> x35, waiting for transfers between devices: 187 us -> 50.6 us  [send(): return lax.ppermute(value, ('blk', 'rep'), pairs)]
    psum x2 -> x0, waiting for transfers between devices: 84.1 us -> none  [the longest x1 67.7 us: shards(): grad_w1, grad_b1, grad_w2 = lax.psum((grad_w1, grad_b1, grad_w2), 'blk')]
    dot_general x36 -> x0, matrix products: 70.8 us -> none  [the longest x16 42.3 us: contribute(): jnp.einsum('rm,maf->raf', onehot, product, precision=lax.Precision.HIGHEST)]
    psum x1 -> x0, blocking collectives: 42.8 us -> none  [shards(): grad_w1, grad_b1, grad_w2 = lax.psum((grad_w1, grad_b1, grad_w2), 'blk')]
    gather x18 -> x0, local copies, waits for them, and re-layouts: 34.8 us -> none  [the longest x16 31.7 us: contribute(): picked = jnp.take(panel_now, col_ids, axis=0)]
    ppermute x16 -> x35, starting transfers between devices: 5.34 us -> 38.9 us  [send(): return lax.ppermute(value, ('blk', 'rep'), pairs)]
    pallas_call x0 -> x5, Pallas kernels: none -> 25.4 us  [the longest x2 19 us: gather_call(): pl.pallas_call(functools.partial(gather_kernel, kinds, first, last), out_...]
    while x44 -> x0, local copies, waits for them, and re-layouts: 25.3 us -> none
  transfers between devices with their start and end apart: 18 -> 35, of which waited for: 17 -> 19; matrix products, arithmetic and copies ran while one was open for 13% -> 6% of each run, Pallas kernels for 0% -> 8%
where the time goes in v1:
time: 140 us; the launch traced here: 139 us
  waiting for transfers between devices  50.6 us (36%)
  starting transfers between devices  38.9 us (28%)
  Pallas kernels  25.4 us (18%)
  local copies, waits for them, and re-layouts  16.8 us (12%)
  other arithmetic  6.01 us (4%)
    ppermute x35, waiting for transfers between devices, send(): return lax.ppermute(value, ('blk', 'rep'), pairs)  50.6 us
    ppermute x35, starting transfers between devices, send(): return lax.ppermute(value, ('blk', 'rep'), pairs)  38.9 us
    pallas_call x2, Pallas kernels, gather_call(): pl.pallas_call(functools.partial(gather_kernel, kinds, first, last), out_...  19 us
    unnamed x56, local copies, waits for them, and re-layouts  13.1 us
  transfers between devices with their start and end apart: 35, of which 19 were waited for; matrix products, arithmetic and copies ran while one was open for 6% of the time, Pallas kernels for 8%

profile of v1, /device:TPU:0, one launch (start us, length us, event | category | flops | bytes accessed | tf_op | source)
XLA Modules:
  0.0 138.6 jit_solution(13464456401780356958)
XLA Ops:
  3.4 3.4 %collective-permute-done.2.got_tile = bf16[512,128]{1,0:T(8,128)(2,1)} collective-permute-done((bf16[512,128]{1,0:T(8,128)(2,1)S(1)}, bf16[512,128]{1,0:T(8,128)(2,1)}, u32[]{:S(2)}, u32[]{:S(2)}) %collective-permute-start.2) | collective-permute-done | bytes 131104 | tf_op jit(solution)/shard_map/ppermute | solution.py:121
  7.0 2.0 %shard_map.130.rest_0_ = bf16[1536,128]{1,0:T(8,128)(2,1)} custom-call(s32[2]{0:T(128)} %pad_add_fusion.2.place, bf16[512,128]{1,0:T(8,128)(2,1)} %feat.1, bf16[512,256]{1,0:T(8,128)(2,1)} %cot.1, bf16[512,128]{1,0:T(8,128)(2,1)} %collective-permute-done.2.got_tile, bf16[512,128]{1,0:T(8,128)(2,1)} %collective-permute-done.3.got_first), custom_call_target="tpu_custom_call" | custom-call | tf_op jit(solution)/shard_map/pallas_call | solution.py:346
  9.0 2.9 %collective-permute-start.7 = (bf16[1536,128]{1,0:T(8,128)(2,1)}, bf16[1536,128]{1,0:T(8,128)(2,1)}, u32[]{:S(2)}, u32[]{:S(2)}) collective-permute-start(bf16[1536,128]{1,0:T(8,128)(2,1)} %shard_map.130.rest_0_), channel_id=1, source_target_pairs={{0,8},{1,9},{2,10},{3,11},{4,12},{5,13},{6,14},{7,15},{8,0},{9,1},... | collective-permute-start | bytes 1179656 | tf_op jit(solution)/shard_map/ppermute | solution.py:121
  13.4 8.3 %collective-permute-done.7.rest_4_ = bf16[1536,128]{1,0:T(8,128)(2,1)} collective-permute-done((bf16[1536,128]{1,0:T(8,128)(2,1)}, bf16[1536,128]{1,0:T(8,128)(2,1)}, u32[]{:S(2)}, u32[]{:S(2)}) %collective-permute-start.7) | collective-permute-done | bytes 393248 | tf_op jit(solution)/shard_map/ppermute | solution.py:121
  21.7 1.4 %collective-permute-start.16 = (bf16[1536,128]{1,0:T(8,128)(2,1)}, bf16[1536,128]{1,0:T(8,128)(2,1)}, u32[]{:S(2)}, u32[]{:S(2)}) collective-permute-start(bf16[1536,128]{1,0:T(8,128)(2,1)} %collective-permute-done.7.rest_4_), channel_id=1, source_target_pairs={{8,16},{9,17},{10,18},{11,19},{12,20},{13,21},{14,22},{15,23},{16,... | collective-permute-start | bytes 1179656 | tf_op jit(solution)/shard_map/ppermute | solution.py:121
  26.0 1.7 %collective-permute-start.4 = (bf16[1536,128]{1,0:T(8,128)(2,1)}, bf16[1536,128]{1,0:T(8,128)(2,1)S(1)}, u32[]{:S(2)}, u32[]{:S(2)}) collective-permute-start(bf16[1536,128]{1,0:T(8,128)(2,1)} %shard_map.130.rest_0_), channel_id=1, source_target_pairs={{0,2},{1,5},{2,0},{3,7},{4,6},{5,1},{6,4},{7,3},{8,10},{9,13},{10,... | collective-permute-start | bytes 1179656 | tf_op jit(solution)/shard_map/ppermute | solution.py:121
  27.7 1.5 %collective-permute-start.5 = (bf16[1536,128]{1,0:T(8,128)(2,1)}, bf16[1536,128]{1,0:T(8,128)(2,1)S(1)}, u32[]{:S(2)}, u32[]{:S(2)}) collective-permute-start(bf16[1536,128]{1,0:T(8,128)(2,1)} %shard_map.130.rest_0_), channel_id=1, source_target_pairs={{0,4},{1,3},{2,6},{3,1},{4,0},{5,7},{6,2},{7,5},{8,12},{9,11},{10,... | collective-permute-start | bytes 1179656 | tf_op jit(solution)/shard_map/ppermute | solution.py:121
  29.3 7.6 %collective-permute-done.12 = bf16[1536,128]{1,0:T(8,128)(2,1)} collective-permute-done((bf16[1536,128]{1,0:T(8,128)(2,1)}, bf16[1536,128]{1,0:T(8,128)(2,1)}, u32[]{:S(2)}, u32[]{:S(2)}) %collective-permute-start.12) | collective-permute-done | bytes 393248 | tf_op jit(solution)/shard_map/ppermute | solution.py:121
  38.2 1.8 %broadcast_select_fusion.1.rest_0_ = bf16[1536,128]{1,0:T(8,128)(2,1)} fusion(bf16[1536,128]{1,0:T(8,128)(2,1)} %collective-permute-done.11, bf16[1536,128]{1,0:T(8,128)(2,1)} %collective-permute-done.12, pred[]{:T(512)S(6)} %or.3), kind=kLoop, calls=%fused_computation.1 | loop fusion | flops 196608 | bytes 1179649 | tf_op jit(solution)/shard_map/jit(_where)/select_n | solution.py:372
  40.0 1.5 %collective-permute-start.8 = (bf16[1536,128]{1,0:T(8,128)(2,1)}, bf16[1536,128]{1,0:T(8,128)(2,1)S(1)}, u32[]{:S(2)}, u32[]{:S(2)}) collective-permute-start(bf16[1536,128]{1,0:T(8,128)(2,1)} %collective-permute-done.7.rest_4_), channel_id=1, source_target_pairs={{0,2},{1,5},{2,0},{3,7},{4,6},{5,1},{6,4},{7,3},{8,10},{9,13},{10,... | collective-permute-start | bytes 1179656 | tf_op jit(solution)/shard_map/ppermute | solution.py:121
  41.5 6.9 %collective-permute-done.17 = bf16[1536,128]{1,0:T(8,128)(2,1)S(1)} collective-permute-done((bf16[1536,128]{1,0:T(8,128)(2,1)}, bf16[1536,128]{1,0:T(8,128)(2,1)S(1)}, u32[]{:S(2)}, u32[]{:S(2)}) %collective-permute-start.17) | collective-permute-done | bytes 393248 | tf_op jit(solution)/shard_map/ppermute | solution.py:121
  48.4 1.5 %collective-permute-start.9 = (bf16[1536,128]{1,0:T(8,128)(2,1)}, bf16[1536,128]{1,0:T(8,128)(2,1)S(1)}, u32[]{:S(2)}, u32[]{:S(2)}) collective-permute-start(bf16[1536,128]{1,0:T(8,128)(2,1)} %collective-permute-done.7.rest_4_), channel_id=1, source_target_pairs={{0,4},{1,3},{2,6},{3,1},{4,0},{5,7},{6,2},{7,5},{8,12},{9,11},{10,... | collective-permute-start | bytes 1179656 | tf_op jit(solution)/shard_map/ppermute | solution.py:121
  52.0 1.5 %collective-permute-start.10 = (bf16[1536,128]{1,0:T(8,128)(2,1)S(1)}, bf16[1536,128]{1,0:T(8,128)(2,1)S(1)}, u32[]{:S(2)}, u32[]{:S(2)}) collective-permute-start(bf16[1536,128]{1,0:T(8,128)(2,1)S(1)} %collective-permute-done.8.rest_5_), channel_id=1, source_target_pairs={{0,4},{1,3},{2,6},{3,1},{4,0},{5,7},{6,2},{7,5},{8,12},{9,11},{10,... | collective-permute-start | bytes 1179656 | tf_op jit(solution)/shard_map/ppermute | solution.py:121
  55.1 1.5 %collective-permute-start.13 = (bf16[1536,128]{1,0:T(8,128)(2,1)}, bf16[1536,128]{1,0:T(8,128)(2,1)}, u32[]{:S(2)}, u32[]{:S(2)}) collective-permute-start(bf16[1536,128]{1,0:T(8,128)(2,1)} %broadcast_select_fusion.1.rest_0_), channel_id=1, source_target_pairs={{0,2},{1,5},{2,0},{3,7},{4,6},{5,1},{6,4},{7,3},{8,10},{9,13},{10,... | collective-permute-start | bytes 1179656 | tf_op jit(solution)/shard_map/ppermute | solution.py:121
  56.6 1.5 %collective-permute-done.9.rest_6_ = bf16[1536,128]{1,0:T(8,128)(2,1)S(1)} collective-permute-done((bf16[1536,128]{1,0:T(8,128)(2,1)}, bf16[1536,128]{1,0:T(8,128)(2,1)S(1)}, u32[]{:S(2)}, u32[]{:S(2)}) %collective-permute-start.9) | collective-permute-done | bytes 393248 | tf_op jit(solution)/shard_map/ppermute | solution.py:121
  58.9 2.5 %collective-permute-start.18 = (bf16[1536,128]{1,0:T(8,128)(2,1)}, bf16[1536,128]{1,0:T(8,128)(2,1)}, u32[]{:S(2)}, u32[]{:S(2)}) collective-permute-start(bf16[1536,128]{1,0:T(8,128)(2,1)} %broadcast_select_fusion.rest_4_), channel_id=1, source_target_pairs={{0,2},{1,5},{2,0},{3,7},{4,6},{5,1},{6,4},{7,3},{8,10},{9,13},{10,... | collective-permute-start | bytes 1179656 | tf_op jit(solution)/shard_map/ppermute | solution.py:121
  61.4 5.2 %collective-permute-done.6.rest_3_ = bf16[1536,128]{1,0:T(8,128)(2,1)S(1)} collective-permute-done((bf16[1536,128]{1,0:T(8,128)(2,1)S(1)}, bf16[1536,128]{1,0:T(8,128)(2,1)S(1)}, u32[]{:S(2)}, u32[]{:S(2)}) %collective-permute-start.6) | collective-permute-done | bytes 393248 | tf_op jit(solution)/shard_map/ppermute | solution.py:121
  67.3 1.5 %collective-permute-start.14 = (bf16[1536,128]{1,0:T(8,128)(2,1)}, bf16[1536,128]{1,0:T(8,128)(2,1)}, u32[]{:S(2)}, u32[]{:S(2)}) collective-permute-start(bf16[1536,128]{1,0:T(8,128)(2,1)} %broadcast_select_fusion.1.rest_0_), channel_id=1, source_target_pairs={{0,4},{1,3},{2,6},{3,1},{4,0},{5,7},{6,2},{7,5},{8,12},{9,11},{10,... | collective-permute-start | bytes 1179656 | tf_op jit(solution)/shard_map/ppermute | solution.py:121
  68.8 4.4 %collective-permute-done.10.rest_7_ = bf16[1536,128]{1,0:T(8,128)(2,1)S(1)} collective-permute-done((bf16[1536,128]{1,0:T(8,128)(2,1)S(1)}, bf16[1536,128]{1,0:T(8,128)(2,1)S(1)}, u32[]{:S(2)}, u32[]{:S(2)}) %collective-permute-start.10) | collective-permute-done | bytes 393248 | tf_op jit(solution)/shard_map/ppermute | solution.py:121
  74.0 1.5 %collective-permute-start.19 = (bf16[1536,128]{1,0:T(8,128)(2,1)}, bf16[1536,128]{1,0:T(8,128)(2,1)}, u32[]{:S(2)}, u32[]{:S(2)}) collective-permute-start(bf16[1536,128]{1,0:T(8,128)(2,1)} %broadcast_select_fusion.rest_4_), channel_id=1, source_target_pairs={{0,4},{1,3},{2,6},{3,1},{4,0},{5,7},{6,2},{7,5},{8,12},{9,11},{10,... | collective-permute-start | bytes 1179656 | tf_op jit(solution)/shard_map/ppermute | solution.py:121
  76.0 1.5 %collective-permute-start.20 = (bf16[1536,128]{1,0:T(8,128)(2,1)}, bf16[1536,128]{1,0:T(8,128)(2,1)}, u32[]{:S(2)}, u32[]{:S(2)}) collective-permute-start(bf16[1536,128]{1,0:T(8,128)(2,1)} %collective-permute-done.18.rest_5_), channel_id=1, source_target_pairs={{0,4},{1,3},{2,6},{3,1},{4,0},{5,7},{6,2},{7,5},{8,12},{9,11},{10,... | collective-permute-start | bytes 1179656 | tf_op jit(solution)/shard_map/ppermute | solution.py:121
  84.9 9.7 %shard_map.131.start = f32[3,8,128,128]{3,2,1,0:T(8,128)S(1)} custom-call(s32[2]{0:T(128)S(1)} %copy-done.15, s32[256]{0:T(256)S(1)} %reshape.15.table, f32[1024,128]{1,0:T(8,128)S(1)} %broadcast_in_dim.4.start, bf16[8,12,128,128]{3,2,1,0:T(8,128)(2,1)S(1)} %bitcast.30, bf16[8,12,128,128]{3,2,1,0:T(8,128)(2,1)} %collective-permute-done.1.other, ...), custom_call_target="tpu_custom_call" | custom-call | flops 402653184 | bytes 6400000 | tf_op jit(solution)/shard_map/pallas_call | solution.py:257
  94.6 9.3 %shard_map.132.mine = bf16[2048,128]{1,0:T(8,128)(2,1)} custom-call(s32[2]{0:T(128)S(1)} %copy-done.15, s32[256]{0:T(256)S(1)} %reshape.15.table, f32[3,8,128,128]{3,2,1,0:T(8,128)S(1)} %shard_map.131.start, bf16[8,12,128,128]{3,2,1,0:T(8,128)(2,1)S(1)} %bitcast.31, bf16[8,12,128,128]{3,2,1,0:T(8,128)(2,1)} %collective-permute-done.1.other, ...), custom_call_target="tpu_custom_call" | custom-call | flops 402653184 | bytes 6400000 | tf_op jit(solution)/shard_map/pallas_call | solution.py:257
  107.0 2.6 %shard_map.133 = f32[4,104,128]{2,1,0:T(8,128)} custom-call(s32[2]{0:T(128)} %pad_add_fusion.2.place, bf16[2048,128]{1,0:T(8,128)(2,1)} %shard_map.132.mine, bf16[2048,128]{1,0:T(8,128)(2,1)} %copy-done.16, bf16[128,128]{1,0:T(8,128)(2,1)} %constant_dynamic-slice_fusion.1.w_one, f32[1,128]{1,0:T(1,128)} %dynamic-slice_bitcast_fusion.bias, ...), custom_call_target="tpu_custom_call" | custom-call | tf_op jit(solution)/shard_map/pallas_call | solution.py:393
  111.8 1.4 %collective-permute-start.23 = (f32[104,128]{1,0:T(8,128)S(1)}, f32[104,128]{1,0:T(8,128)S(1)}, u32[]{:S(2)}, u32[]{:S(2)}) collective-permute-start(f32[104,128]{1,0:T(8,128)S(1)} %get-tuple-element.12), channel_id=1, source_target_pairs={{0,4},{1,5},{2,6},{3,7},{4,0},{5,1},{6,2},{7,3},{8,12},{9,13},{10,... | collective-permute-start | bytes 159752 | tf_op jit(solution)/shard_map/ppermute | solution.py:121
  115.9 2.3 %collective-permute-done.24 = f32[104,128]{1,0:T(8,128)S(1)} collective-permute-done((f32[104,128]{1,0:T(8,128)S(1)}, f32[104,128]{1,0:T(8,128)S(1)}, u32[]{:S(2)}, u32[]{:S(2)}) %collective-permute-start.24) | collective-permute-done | bytes 53280 | tf_op jit(solution)/shard_map/ppermute | solution.py:121
  119.1 2.5 %collective-permute-start.25 = (f32[104,128]{1,0:T(8,128)S(1)}, f32[104,128]{1,0:T(8,128)S(1)}, u32[]{:S(2)}, u32[]{:S(2)}) collective-permute-start(f32[104,128]{1,0:T(8,128)S(1)} %fusion.1), channel_id=1, source_target_pairs={{0,8},{1,9},{2,10},{3,11},{4,12},{5,13},{6,14},{7,15},{8,0},{9,1},... | collective-permute-start | bytes 159752 | tf_op jit(solution)/shard_map/ppermute | solution.py:121
  121.6 2.4 %collective-permute-start.27 = (f32[104,128]{1,0:T(8,128)S(1)}, f32[104,128]{1,0:T(8,128)S(1)}, u32[]{:S(2)}, u32[]{:S(2)}) collective-permute-start(f32[104,128]{1,0:T(8,128)S(1)} %fusion.1), channel_id=1, source_target_pairs={{0,24},{1,25},{2,26},{3,27},{4,28},{5,29},{6,30},{7,31},{8,16},{9,... | collective-permute-start | bytes 159752 | tf_op jit(solution)/shard_map/ppermute | solution.py:121
  124.0 2.9 %collective-permute-done.26 = f32[104,128]{1,0:T(8,128)S(1)} collective-permute-done((f32[104,128]{1,0:T(8,128)S(1)}, f32[104,128]{1,0:T(8,128)S(1)}, u32[]{:S(2)}, u32[]{:S(2)}) %collective-permute-start.26) | collective-permute-done | bytes 53280 | tf_op jit(solution)/shard_map/ppermute | solution.py:121
  127.7 2.0 %collective-permute-start.28 = (f32[104,128]{1,0:T(8,128)S(1)}, f32[104,128]{1,0:T(8,128)S(1)}, u32[]{:S(2)}, u32[]{:S(2)}) collective-permute-start(f32[104,128]{1,0:T(8,128)S(1)} %add_add_fusion.refs_0_), channel_id=1, source_target_pairs={{0,2},{1,3},{2,0},{3,1},{4,6},{5,7},{6,4},{7,5},{8,10},{9,11},{10,... | collective-permute-start | bytes 159752 | tf_op jit(solution)/shard_map/ppermute | solution.py:121
  131.9 1.9 %collective-permute-done.29.refs_2_ = f32[104,128]{1,0:T(8,128)S(1)} collective-permute-done((f32[104,128]{1,0:T(8,128)S(1)}, f32[104,128]{1,0:T(8,128)S(1)}, u32[]{:S(2)}, u32[]{:S(2)}) %collective-permute-start.29) | collective-permute-done | bytes 53280 | tf_op jit(solution)/shard_map/ppermute | solution.py:121
  136.8 1.8 %shard_map.134 = (f32[128,256]{1,0:T(8,128)}, f32[1,256]{1,0:T(1,128)}, f32[256,256]{1,0:T(8,128)}) custom-call(s32[2]{0:T(128)} %pad_add_fusion.2.place, f32[104,128]{1,0:T(8,128)} %copy-done.17, f32[104,128]{1,0:T(8,128)} %copy-done.18, f32[104,128]{1,0:T(8,128)} %copy-done.19, f32[104,128]{1,0:T(8,128)} %copy-done.20, f32[104,128]{1,0:T(8,128)} %copy-done.21, ...), custom_call_target="tpu_custom_call" | custom-call | tf_op jit(solution)/shard_map/pallas_call | solution.py:409
  (116 shorter events, 36.9 us)
Async XLA Ops:
  0.7 77.0 %collective-permute-start.1 = (bf16[8,12,128,128]{3,2,1,0:T(8,128)(2,1)}, bf16[8,12,128,128]{3,2,1,0:T(8,128)(2,1)}, u32[]{:S(2)}, u32[]{:S(2)}) collective-permute-start(bf16[8,12,128,128]{3,2,1,0:T(8,128)(2,1)} %bitcast.29), channel_id=1, source_target_pairs={{0,1},{1,0},{2,3},{3,2},{4,5},{5,4},{6,7},{7,6},{8,9},{9,8},{10,11... | collective-permute-start | bytes 9437192 | tf_op jit(solution)/shard_map/ppermute | solution.py:121
  2.2 4.5 %collective-permute-start.2 = (bf16[512,128]{1,0:T(8,128)(2,1)S(1)}, bf16[512,128]{1,0:T(8,128)(2,1)}, u32[]{:S(2)}, u32[]{:S(2)}) collective-permute-start(bf16[512,128]{1,0:T(8,128)(2,1)S(1)} %get-tuple-element.10), channel_id=1, source_target_pairs={{0,1},{1,0},{2,3},{3,2},{4,5},{5,4},{6,7},{7,6},{8,9},{9,8},{10,11... | collective-permute-start | bytes 393224 | tf_op jit(solution)/shard_map/ppermute | solution.py:121
  2.5 4.5 %collective-permute-start.3 = (bf16[512,128]{1,0:T(8,128)(2,1)S(1)}, bf16[512,128]{1,0:T(8,128)(2,1)}, u32[]{:S(2)}, u32[]{:S(2)}) collective-permute-start(bf16[512,128]{1,0:T(8,128)(2,1)S(1)} %get-tuple-element.9), channel_id=1, source_target_pairs={{0,1},{1,0},{2,3},{3,2},{4,5},{5,4},{6,7},{7,6},{8,9},{9,8},{10,11... | collective-permute-start | bytes 393224 | tf_op jit(solution)/shard_map/ppermute | solution.py:121
  9.0 12.7 %collective-permute-start.7 = (bf16[1536,128]{1,0:T(8,128)(2,1)}, bf16[1536,128]{1,0:T(8,128)(2,1)}, u32[]{:S(2)}, u32[]{:S(2)}) collective-permute-start(bf16[1536,128]{1,0:T(8,128)(2,1)} %shard_map.130.rest_0_), channel_id=1, source_target_pairs={{0,8},{1,9},{2,10},{3,11},{4,12},{5,13},{6,14},{7,15},{8,0},{9,1},... | collective-permute-start | bytes 1179656 | tf_op jit(solution)/shard_map/ppermute | solution.py:121
  12.0 11.2 %collective-permute-start.11 = (bf16[1536,128]{1,0:T(8,128)(2,1)}, bf16[1536,128]{1,0:T(8,128)(2,1)}, u32[]{:S(2)}, u32[]{:S(2)}) collective-permute-start(bf16[1536,128]{1,0:T(8,128)(2,1)} %shard_map.130.rest_0_), channel_id=1, source_target_pairs={{8,16},{9,17},{10,18},{11,19},{12,20},{13,21},{14,22},{15,23},{16,... | collective-permute-start | bytes 1179656 | tf_op jit(solution)/shard_map/ppermute | solution.py:121
  21.7 6.0 %collective-permute-start.16 = (bf16[1536,128]{1,0:T(8,128)(2,1)}, bf16[1536,128]{1,0:T(8,128)(2,1)}, u32[]{:S(2)}, u32[]{:S(2)}) collective-permute-start(bf16[1536,128]{1,0:T(8,128)(2,1)} %collective-permute-done.7.rest_4_), channel_id=1, source_target_pairs={{8,16},{9,17},{10,18},{11,19},{12,20},{13,21},{14,22},{15,23},{16,... | collective-permute-start | bytes 1179656 | tf_op jit(solution)/shard_map/ppermute | solution.py:121
  23.1 13.7 %collective-permute-start.12 = (bf16[1536,128]{1,0:T(8,128)(2,1)}, bf16[1536,128]{1,0:T(8,128)(2,1)}, u32[]{:S(2)}, u32[]{:S(2)}) collective-permute-start(bf16[1536,128]{1,0:T(8,128)(2,1)} %collective-permute-done.11), channel_id=1, source_target_pairs={{8,0},{9,1},{10,2},{11,3},{12,4},{13,5},{14,6},{15,7},{16,24},{17,... | collective-permute-start | bytes 1179656 | tf_op jit(solution)/shard_map/ppermute | solution.py:121
  26.0 14.0 %collective-permute-start = (s32[8,16]{1,0:T(8,128)S(1)}, s32[8,16]{1,0:T(8,128)S(1)}, u32[]{:S(2)}, u32[]{:S(2)}) collective-permute-start(s32[8,16]{1,0:T(8,128)S(1)} %pad_add_fusion.1), channel_id=1, source_target_pairs={{0,1},{1,0},{2,3},{3,2},{4,5},{5,4},{6,7},{7,6},{8,9},{9,8},{10,11... | collective-permute-start | bytes 1544 | tf_op jit(solution)/shard_map/ppermute | solution.py:121
  26.0 24.7 %collective-permute-start.4 = (bf16[1536,128]{1,0:T(8,128)(2,1)}, bf16[1536,128]{1,0:T(8,128)(2,1)S(1)}, u32[]{:S(2)}, u32[]{:S(2)}) collective-permute-start(bf16[1536,128]{1,0:T(8,128)(2,1)} %shard_map.130.rest_0_), channel_id=1, source_target_pairs={{0,2},{1,5},{2,0},{3,7},{4,6},{5,1},{6,4},{7,3},{8,10},{9,13},{10,... | collective-permute-start | bytes 1179656 | tf_op jit(solution)/shard_map/ppermute | solution.py:121
  27.7 26.6 %collective-permute-start.5 = (bf16[1536,128]{1,0:T(8,128)(2,1)}, bf16[1536,128]{1,0:T(8,128)(2,1)S(1)}, u32[]{:S(2)}, u32[]{:S(2)}) collective-permute-start(bf16[1536,128]{1,0:T(8,128)(2,1)} %shard_map.130.rest_0_), channel_id=1, source_target_pairs={{0,4},{1,3},{2,6},{3,1},{4,0},{5,7},{6,2},{7,5},{8,12},{9,11},{10,... | collective-permute-start | bytes 1179656 | tf_op jit(solution)/shard_map/ppermute | solution.py:121
  36.9 11.5 %collective-permute-start.17 = (bf16[1536,128]{1,0:T(8,128)(2,1)}, bf16[1536,128]{1,0:T(8,128)(2,1)S(1)}, u32[]{:S(2)}, u32[]{:S(2)}) collective-permute-start(bf16[1536,128]{1,0:T(8,128)(2,1)} %collective-permute-done.16), channel_id=1, source_target_pairs={{8,0},{9,1},{10,2},{11,3},{12,4},{13,5},{14,6},{15,7},{16,24},{17,... | collective-permute-start | bytes 1179656 | tf_op jit(solution)/shard_map/ppermute | solution.py:121
  40.0 12.1 %collective-permute-start.8 = (bf16[1536,128]{1,0:T(8,128)(2,1)}, bf16[1536,128]{1,0:T(8,128)(2,1)S(1)}, u32[]{:S(2)}, u32[]{:S(2)}) collective-permute-start(bf16[1536,128]{1,0:T(8,128)(2,1)} %collective-permute-done.7.rest_4_), channel_id=1, source_target_pairs={{0,2},{1,5},{2,0},{3,7},{4,6},{5,1},{6,4},{7,3},{8,10},{9,13},{10,... | collective-permute-start | bytes 1179656 | tf_op jit(solution)/shard_map/ppermute | solution.py:121
  48.4 9.7 %collective-permute-start.9 = (bf16[1536,128]{1,0:T(8,128)(2,1)}, bf16[1536,128]{1,0:T(8,128)(2,1)S(1)}, u32[]{:S(2)}, u32[]{:S(2)}) collective-permute-start(bf16[1536,128]{1,0:T(8,128)(2,1)} %collective-permute-done.7.rest_4_), channel_id=1, source_target_pairs={{0,4},{1,3},{2,6},{3,1},{4,0},{5,7},{6,2},{7,5},{8,12},{9,11},{10,... | collective-permute-start | bytes 1179656 | tf_op jit(solution)/shard_map/ppermute | solution.py:121
  50.7 15.8 %collective-permute-start.6 = (bf16[1536,128]{1,0:T(8,128)(2,1)S(1)}, bf16[1536,128]{1,0:T(8,128)(2,1)S(1)}, u32[]{:S(2)}, u32[]{:S(2)}) collective-permute-start(bf16[1536,128]{1,0:T(8,128)(2,1)S(1)} %collective-permute-done.4.rest_1_), channel_id=1, source_target_pairs={{0,4},{1,3},{2,6},{3,1},{4,0},{5,7},{6,2},{7,5},{8,12},{9,11},{10,... | collective-permute-start | bytes 1179656 | tf_op jit(solution)/shard_map/ppermute | solution.py:121
  52.0 21.2 %collective-permute-start.10 = (bf16[1536,128]{1,0:T(8,128)(2,1)S(1)}, bf16[1536,128]{1,0:T(8,128)(2,1)S(1)}, u32[]{:S(2)}, u32[]{:S(2)}) collective-permute-start(bf16[1536,128]{1,0:T(8,128)(2,1)S(1)} %collective-permute-done.8.rest_5_), channel_id=1, source_target_pairs={{0,4},{1,3},{2,6},{3,1},{4,0},{5,7},{6,2},{7,5},{8,12},{9,11},{10,... | collective-permute-start | bytes 1179656 | tf_op jit(solution)/shard_map/ppermute | solution.py:121
  55.1 20.4 %collective-permute-start.13 = (bf16[1536,128]{1,0:T(8,128)(2,1)}, bf16[1536,128]{1,0:T(8,128)(2,1)}, u32[]{:S(2)}, u32[]{:S(2)}) collective-permute-start(bf16[1536,128]{1,0:T(8,128)(2,1)} %broadcast_select_fusion.1.rest_0_), channel_id=1, source_target_pairs={{0,2},{1,5},{2,0},{3,7},{4,6},{5,1},{6,4},{7,3},{8,10},{9,13},{10,... | collective-permute-start | bytes 1179656 | tf_op jit(solution)/shard_map/ppermute | solution.py:121
  58.9 17.1 %collective-permute-start.18 = (bf16[1536,128]{1,0:T(8,128)(2,1)}, bf16[1536,128]{1,0:T(8,128)(2,1)}, u32[]{:S(2)}, u32[]{:S(2)}) collective-permute-start(bf16[1536,128]{1,0:T(8,128)(2,1)} %broadcast_select_fusion.rest_4_), channel_id=1, source_target_pairs={{0,2},{1,5},{2,0},{3,7},{4,6},{5,1},{6,4},{7,3},{8,10},{9,13},{10,... | collective-permute-start | bytes 1179656 | tf_op jit(solution)/shard_map/ppermute | solution.py:121
  67.3 27.3 %collective-permute-start.14 = (bf16[1536,128]{1,0:T(8,128)(2,1)}, bf16[1536,128]{1,0:T(8,128)(2,1)}, u32[]{:S(2)}, u32[]{:S(2)}) collective-permute-start(bf16[1536,128]{1,0:T(8,128)(2,1)} %broadcast_select_fusion.1.rest_0_), channel_id=1, source_target_pairs={{0,4},{1,3},{2,6},{3,1},{4,0},{5,7},{6,2},{7,5},{8,12},{9,11},{10,... | collective-permute-start | bytes 1179656 | tf_op jit(solution)/shard_map/ppermute | solution.py:121
  74.0 20.6 %collective-permute-start.19 = (bf16[1536,128]{1,0:T(8,128)(2,1)}, bf16[1536,128]{1,0:T(8,128)(2,1)}, u32[]{:S(2)}, u32[]{:S(2)}) collective-permute-start(bf16[1536,128]{1,0:T(8,128)(2,1)} %broadcast_select_fusion.rest_4_), channel_id=1, source_target_pairs={{0,4},{1,3},{2,6},{3,1},{4,0},{5,7},{6,2},{7,5},{8,12},{9,11},{10,... | collective-permute-start | bytes 1179656 | tf_op jit(solution)/shard_map/ppermute | solution.py:121
  75.5 19.1 %collective-permute-start.15 = (bf16[1536,128]{1,0:T(8,128)(2,1)}, bf16[1536,128]{1,0:T(8,128)(2,1)}, u32[]{:S(2)}, u32[]{:S(2)}) collective-permute-start(bf16[1536,128]{1,0:T(8,128)(2,1)} %collective-permute-done.13.rest_1_), channel_id=1, source_target_pairs={{0,4},{1,3},{2,6},{3,1},{4,0},{5,7},{6,2},{7,5},{8,12},{9,11},{10,... | collective-permute-start | bytes 1179656 | tf_op jit(solution)/shard_map/ppermute | solution.py:121
  76.0 18.6 %collective-permute-start.20 = (bf16[1536,128]{1,0:T(8,128)(2,1)}, bf16[1536,128]{1,0:T(8,128)(2,1)}, u32[]{:S(2)}, u32[]{:S(2)}) collective-permute-start(bf16[1536,128]{1,0:T(8,128)(2,1)} %collective-permute-done.18.rest_5_), channel_id=1, source_target_pairs={{0,4},{1,3},{2,6},{3,1},{4,0},{5,7},{6,2},{7,5},{8,12},{9,11},{10,... | collective-permute-start | bytes 1179656 | tf_op jit(solution)/shard_map/ppermute | solution.py:121
  110.4 4.2 %collective-permute-start.22 = (f32[104,128]{1,0:T(8,128)S(1)}, f32[104,128]{1,0:T(8,128)S(1)}, u32[]{:S(2)}, u32[]{:S(2)}) collective-permute-start(f32[104,128]{1,0:T(8,128)S(1)} %get-tuple-element.13), channel_id=1, source_target_pairs={{0,2},{1,3},{2,0},{3,1},{4,6},{5,7},{6,4},{7,5},{8,10},{9,11},{10,... | collective-permute-start | bytes 159752 | tf_op jit(solution)/shard_map/ppermute | solution.py:121
  111.8 4.1 %collective-permute-start.23 = (f32[104,128]{1,0:T(8,128)S(1)}, f32[104,128]{1,0:T(8,128)S(1)}, u32[]{:S(2)}, u32[]{:S(2)}) collective-permute-start(f32[104,128]{1,0:T(8,128)S(1)} %get-tuple-element.12), channel_id=1, source_target_pairs={{0,4},{1,5},{2,6},{3,7},{4,0},{5,1},{6,2},{7,3},{8,12},{9,13},{10,... | collective-permute-start | bytes 159752 | tf_op jit(solution)/shard_map/ppermute | solution.py:121
  113.2 5.0 %collective-permute-start.24 = (f32[104,128]{1,0:T(8,128)S(1)}, f32[104,128]{1,0:T(8,128)S(1)}, u32[]{:S(2)}, u32[]{:S(2)}) collective-permute-start(f32[104,128]{1,0:T(8,128)S(1)} %get-tuple-element.11), channel_id=1, source_target_pairs={{0,6},{1,7},{2,4},{3,5},{4,2},{5,3},{6,0},{7,1},{8,14},{9,15},{10,... | collective-permute-start | bytes 159752 | tf_op jit(solution)/shard_map/ppermute | solution.py:121
  119.1 5.0 %collective-permute-start.25 = (f32[104,128]{1,0:T(8,128)S(1)}, f32[104,128]{1,0:T(8,128)S(1)}, u32[]{:S(2)}, u32[]{:S(2)}) collective-permute-start(f32[104,128]{1,0:T(8,128)S(1)} %fusion.1), channel_id=1, source_target_pairs={{0,8},{1,9},{2,10},{3,11},{4,12},{5,13},{6,14},{7,15},{8,0},{9,1},... | collective-permute-start | bytes 159752 | tf_op jit(solution)/shard_map/ppermute | solution.py:121
  121.6 5.3 %collective-permute-start.26 = (f32[104,128]{1,0:T(8,128)S(1)}, f32[104,128]{1,0:T(8,128)S(1)}, u32[]{:S(2)}, u32[]{:S(2)}) collective-permute-start(f32[104,128]{1,0:T(8,128)S(1)} %fusion.1), channel_id=1, source_target_pairs={{0,16},{1,17},{2,18},{3,19},{4,20},{5,21},{6,22},{7,23},{8,24},{9,... | collective-permute-start | bytes 159752 | tf_op jit(solution)/shard_map/ppermute | solution.py:121
  121.6 6.0 %collective-permute-start.27 = (f32[104,128]{1,0:T(8,128)S(1)}, f32[104,128]{1,0:T(8,128)S(1)}, u32[]{:S(2)}, u32[]{:S(2)}) collective-permute-start(f32[104,128]{1,0:T(8,128)S(1)} %fusion.1), channel_id=1, source_target_pairs={{0,24},{1,25},{2,26},{3,27},{4,28},{5,29},{6,30},{7,31},{8,16},{9,... | collective-permute-start | bytes 159752 | tf_op jit(solution)/shard_map/ppermute | solution.py:121
  127.7 4.2 %collective-permute-start.28 = (f32[104,128]{1,0:T(8,128)S(1)}, f32[104,128]{1,0:T(8,128)S(1)}, u32[]{:S(2)}, u32[]{:S(2)}) collective-permute-start(f32[104,128]{1,0:T(8,128)S(1)} %add_add_fusion.refs_0_), channel_id=1, source_target_pairs={{0,2},{1,3},{2,0},{3,1},{4,6},{5,7},{6,4},{7,5},{8,10},{9,11},{10,... | collective-permute-start | bytes 159752 | tf_op jit(solution)/shard_map/ppermute | solution.py:121
  129.7 4.1 %collective-permute-start.29 = (f32[104,128]{1,0:T(8,128)S(1)}, f32[104,128]{1,0:T(8,128)S(1)}, u32[]{:S(2)}, u32[]{:S(2)}) collective-permute-start(f32[104,128]{1,0:T(8,128)S(1)} %add_add_fusion.refs_0_), channel_id=1, source_target_pairs={{0,4},{1,5},{2,6},{3,7},{4,0},{5,1},{6,2},{7,3},{8,12},{9,13},{10,... | collective-permute-start | bytes 159752 | tf_op jit(solution)/shard_map/ppermute | solution.py:121
  129.8 5.0 %collective-permute-start.30 = (f32[104,128]{1,0:T(8,128)S(1)}, f32[104,128]{1,0:T(8,128)S(1)}, u32[]{:S(2)}, u32[]{:S(2)}) collective-permute-start(f32[104,128]{1,0:T(8,128)S(1)} %add_add_fusion.refs_0_), channel_id=1, source_target_pairs={{0,6},{1,7},{2,4},{3,5},{4,2},{5,3},{6,0},{7,1},{8,14},{9,15},{10,... | collective-permute-start | bytes 159752 | tf_op jit(solution)/shard_map/ppermute | solution.py:121
  131.2 3.7 %collective-permute-start.31 = (f32[104,128]{1,0:T(8,128)S(1)}, f32[104,128]{1,0:T(8,128)S(1)}, u32[]{:S(2)}, u32[]{:S(2)}) collective-permute-start(f32[104,128]{1,0:T(8,128)S(1)} %add_add_fusion.refs_0_), channel_id=1, source_target_pairs={{0,1},{1,0},{2,3},{3,2},{4,5},{5,4},{6,7},{7,6},{8,9},{9,8},{10,11... | collective-permute-start | bytes 159752 | tf_op jit(solution)/shard_map/ppermute | solution.py:121
  131.9 3.0 %collective-permute-start.32 = (f32[104,128]{1,0:T(8,128)S(1)}, f32[104,128]{1,0:T(8,128)S(1)}, u32[]{:S(2)}, u32[]{:S(2)}) collective-permute-start(f32[104,128]{1,0:T(8,128)S(1)} %collective-permute-done.28.refs_1_), channel_id=1, source_target_pairs={{0,1},{1,0},{2,3},{3,2},{4,5},{5,4},{6,7},{7,6},{8,9},{9,8},{10,11... | collective-permute-start | bytes 159752 | tf_op jit(solution)/shard_map/ppermute | solution.py:121
  (31 other events, 390.5 us)

commit v2 on v1

--- a/solution.py
+++ b/solution.py
@@ -108,7 +108,7 @@
 LANES = 128
 VMEM_SPEC = pl.BlockSpec(memory_space=pltpu.VMEM)
 SMEM_SPEC = pl.BlockSpec(memory_space=pltpu.SMEM)
-ANY_SPEC = pl.BlockSpec(memory_space=pl.ANY)
+HBM_SPEC = pl.BlockSpec(memory_space=pltpu.HBM)
 
 
 def send(value, target):
@@ -145,29 +145,37 @@
     return send(value, lambda p, r: (p ^ 4, r) if p // 4 in (1, 2) else None)
 
 
-def assemble_kernel(place, feat, cot, got_tile, got_first, panel):
-    core = place[1]
-    half = feat.shape[0]
-    rolled = pltpu.roll(got_first[...].astype(F32), LANES // 2, 1).astype(BF16)
-    lane = lax.broadcasted_iota(I32, (half, LANES), 1)
-    mine = cot[:, :LANES]
+def pack_kernel(feat, cot, row, col, slot, count, mine, give, table):
+    core = lax.axis_index("rep")
+    listed = (row[...] & 7) + 8 * (col[...] & 7) + 64 * slot[...]
+    dists, most = listed.shape
+    table[:dists, :most] = listed
+    table[dists : dists + 1, :dists] = count[...]
+    half, deep = feat.shape[0], feat.shape[0] // 2
+    lane = lax.broadcasted_iota(I32, (deep, LANES), 1)
+    above, below = cot[:deep, :LANES], cot[deep:, :LANES]
+    above_turned = pltpu.roll(above.astype(F32), LANES // 2, 1).astype(BF16)
+    below_turned = pltpu.roll(below.astype(F32), LANES // 2, 1).astype(BF16)
+    low = jnp.where(lane < LANES // 2, above, below_turned)
+    high = jnp.where(lane < LANES // 2, above_turned, below)
 
     @pl.when(core == 0)
     def _():
-        panel[0:half, :] = feat[...]
-        panel[half : 2 * half, :] = got_tile[...]
-        panel[2 * half :, :] = jnp.where(lane < LANES // 2, mine, rolled)
+        mine[:half, :] = feat[...]
+        mine[half:, :] = low
+        give[:half, :] = cot[:, LANES:]
+        give[half:, :] = high
 
     @pl.when(core == 1)
     def _():
-        panel[0:half, :] = got_tile[...]
-        panel[half : 2 * half, :] = cot[:, LANES:]
-        panel[2 * half :, :] = jnp.where(lane < LANES // 2, rolled, mine)
-
-
-def entry_of(place, kind):
+        mine[:half, :] = cot[:, LANES:]
+        mine[half:, :] = high
+        give[:half, :] = feat[...]
+        give[half:, :] = low
+
+
+def entry_of(p, core, kind):
     step_one, step_two, slot = kind
-    p, core = place[0], place[1]
     z, w = p >> 2, p & 3
     if step_one:
         w = w ^ (1 + core)
@@ -179,59 +187,84 @@
     return (d >> 3) ^ core, d & 7
 
 
-def gather_kernel(kinds, first, last, place, table, start, own, other, *rest):
+UNROLL = 4
+FLOPS = 300000000
+
+
+def gather_kernel(kinds, near, own_table, other_table, start, own, other, *rest):
     n = len(kinds)
-    panels, (out, acc, xbuf, abuf, sems) = rest[:n], rest[n:]
-    blocks = acc.shape[1]
+    first, last = kinds[0] == (0, 0, 0), kinds[-1] == (1, 1, 3)
+    sources, acc, rest = rest[:n], rest[n], rest[n + 1 :]
+    if last:
+        out, rest = rest[0], rest[1:]
+    abuf, table, sems = rest[:3]
+    panels = sources if near else [rest[3].at[j] for j in range(n)]
+    most = abuf.shape[1]
+    blocks = acc.shape[1] - 1
     size = acc.shape[2]
-    rows = blocks * size
-    half = rows // 2
-    where = [entry_of(place, kind) for kind in kinds]
-    if not first:
-        start_copy = pltpu.make_async_copy(start, acc, sems.at[2, 0])
-        start_copy.start()
+    part = sources[0].shape[0] // 2
+    deep = part * 2 // 3
+    core = lax.axis_index("rep")
+    where = [entry_of(lax.axis_index("blk"), core, kind) for kind in kinds]
     for j in range(n):
         away, dist = where[j]
-        pltpu.make_async_copy(panels[j], xbuf.at[j], sems.at[0, j]).start()
+        if not near:
+            pltpu.make_async_copy(sources[j], panels[j], sems.at[1, j]).start()
 
         @pl.when(away == 0)
         def _():
-            pltpu.make_async_copy(own.at[dist], abuf.at[j], sems.at[1, j]).start()
+            pltpu.make_async_copy(own.at[dist], abuf.at[j], sems.at[0, j]).start()
 
         @pl.when(away != 0)
         def _():
-            pltpu.make_async_copy(other.at[dist], abuf.at[j], sems.at[1, j]).start()
-
-    if not first:
-        start_copy.wait()
+            pltpu.make_async_copy(other.at[dist], abuf.at[j], sems.at[0, j]).start()
+
+    def spot(col):
+        side = ((col >> 2) ^ core) * part
+        return (
+            pl.ds(pl.multiple_of(side + (col & 3) * size, size), size),
+            pl.ds(pl.multiple_of(side + deep + (col & 1) * size, size), size),
+            (col >> 1) & 1,
+        )
+
+    dists = own.shape[0]
     for j in range(n):
         away, dist = where[j]
-        base = (away * 8 + dist) * 16
-        pltpu.make_async_copy(panels[j], xbuf.at[j], sems.at[0, j]).wait()
-        pltpu.make_async_copy(own.at[0], abuf.at[j], sems.at[1, j]).wait()
+        for k in range(most):
+            table[j, k] = jnp.where(away == 0, own_table[dist, k], other_table[dist, k])
+        table[j, most] = jnp.where(away == 0, own_table[dists, dist], other_table[dists, dist])
+    for j in range(n):
+        count = table[j, most]
+        if not near:
+            pltpu.make_async_copy(sources[j], panels[j], sems.at[1, j]).wait()
         if first and j == 0:
             for b in range(blocks):
-                weight = start[b * size : (b + 1) * size, :]
-                side, at = b // (blocks // 2), b % (blocks // 2)
-                acc[0, b] = weight * xbuf[0, b * size : (b + 1) * size, :].astype(F32)
-                acc[1 + side, b] = weight * xbuf[0, rows + at * size : rows + (at + 1) * size, :].astype(F32)
-                acc[2 - side, b] = jnp.zeros((size, LANES), F32)
-
-        def block(k, carry):
-            entry = table[base + k]
-            row, col, slot = entry & 7, (entry >> 3) & 7, entry >> 6
-            tile = xbuf[j, pl.ds(pl.multiple_of(col * size, size), size), :]
-            pack = xbuf[j, pl.ds(pl.multiple_of(rows + (col & 3) * size, size), size), :]
-            product = jnp.dot(
-                abuf[j, slot], jnp.concatenate([tile, pack], axis=1), preferred_element_type=F32
-            )
-            acc[0, row] += product[:, :LANES]
-            acc[1 + (col >> 2), row] += product[:, LANES:]
+                weight = jnp.transpose(jnp.broadcast_to(start[b : b + 1, :], (size, LANES)))
+                tile, pack, _ = spot(b)
+                lanes = (b >> 1) & 1
+                acc[0, b] = weight * panels[0][tile, :].astype(F32)
+                acc[1 + lanes, b] = weight * panels[0][pack, :].astype(F32)
+                acc[2 - lanes, b] = jnp.zeros((size, LANES), F32)
+        pltpu.make_async_copy(own.at[0], abuf.at[j], sems.at[0, j]).wait()
+
+        def step(g, carry):
+            found = []
+            for i in range(UNROLL):
+                k = g * UNROLL + i
+                entry = table[j, jnp.minimum(k, most - 1)]
+                tile, pack, lanes = spot((entry >> 3) & 7)
+                row = jnp.where(k < count, entry & 7, blocks)
+                right = jnp.concatenate([panels[j][tile, :], panels[j][pack, :]], axis=1)
+                product = jnp.dot(abuf[j, entry >> 6], right, preferred_element_type=F32)
+                found.append((row, lanes, product))
+            for row, lanes, product in found:
+                acc[0, row] += product[:, :LANES]
+                acc[1 + lanes, row] += product[:, LANES:]
             return carry
 
-        lax.fori_loop(0, table[base + 12], block, 0)
+        lax.fori_loop(0, (count + UNROLL - 1) // UNROLL, step, 0)
     if last:
-        core = place[1]
+        rows = blocks * size
         lane = lax.broadcasted_iota(I32, (size, LANES), 1)
         valid = (lane < LANES // 2) == (core == 0)
         for b in range(blocks):
@@ -240,62 +273,61 @@
             turned = pltpu.roll(joined, LANES // 2, 1)
             both = jnp.where(core == 0, joined, turned)
             out[rows + b * size : rows + (b + 1) * size, :] = jnp.where(valid, both, 0.0).astype(BF16)
-    else:
-        pltpu.make_async_copy(acc, out, sems.at[2, 0]).start()
-        pltpu.make_async_copy(acc, out, sems.at[2, 0]).wait()
-
-
-def gather_call(kinds, first, last, place, table, start, own, other, panels):
+
+
+def gather_call(kinds, near, tables, start, own, other, panels):
     n = len(kinds)
+    first, last = kinds[0] == (0, 0, 0), kinds[-1] == (1, 1, 3)
     most, size = own.shape[1], own.shape[2]
     rows = panels[0].shape[0] * 2 // 3
-    blocks = rows // size
-    acc_shape = (3, blocks, size, LANES)
-    out = (
-        jax.ShapeDtypeStruct((2 * rows, LANES), BF16) if last else jax.ShapeDtypeStruct(acc_shape, F32)
-    )
+    sums = jax.ShapeDtypeStruct((3, rows // size + 1, size, LANES), F32)
+    outs = (sums, jax.ShapeDtypeStruct((2 * rows, LANES), BF16)) if last else (sums,)
     return pl.pallas_call(
-        functools.partial(gather_kernel, kinds, first, last),
-        out_shape=out,
-        in_specs=[SMEM_SPEC, SMEM_SPEC, VMEM_SPEC if first else ANY_SPEC] + [ANY_SPEC] * (2 + n),
-        out_specs=VMEM_SPEC if last else ANY_SPEC,
+        functools.partial(gather_kernel, kinds, near),
+        out_shape=outs,
+        in_specs=[SMEM_SPEC, SMEM_SPEC, VMEM_SPEC, HBM_SPEC, HBM_SPEC]
+        + [VMEM_SPEC if near else HBM_SPEC] * n,
+        out_specs=(VMEM_SPEC,) * len(outs),
+        input_output_aliases={} if first else {2: 0},
         scratch_shapes=[
-            pltpu.VMEM(acc_shape, F32),
-            pltpu.VMEM((n, panels[0].shape[0], LANES), BF16),
             pltpu.VMEM((n, most, size, size), BF16),
-            pltpu.SemaphoreType.DMA((3, n)),
-        ],
-        compiler_params=pltpu.CompilerParams(vmem_limit_bytes=24 << 20),
-        cost_estimate=pl.CostEstimate(
-            flops=n * 6 * 2 * size * size * 2 * LANES, bytes_accessed=n * 800000, transcendentals=0
-        ),
-    )(place, table, start, own, other, *panels)
-
-
-def dense_kernel(place, mine, theirs, w_one, bias, w_two, out):
+            pltpu.SMEM((n, most + 1), I32),
+            pltpu.SemaphoreType.DMA((2, n)),
+        ]
+        + ([] if near else [pltpu.VMEM((n,) + panels[0].shape, BF16)]),
+        compiler_params=pltpu.CompilerParams(vmem_limit_bytes=16 << 20),
+        cost_estimate=pl.CostEstimate(flops=n * FLOPS, bytes_accessed=n * 800000, transcendentals=0),
+    )(*tables, start, own, other, *panels)
+
+
+def dense_kernel(place, mine, theirs, w_first, b_first, w_second, *rest):
+    outs, (one, two) = rest[:4], rest[4:]
     core = place[1]
+    side = one.shape[1]
+    ours = pl.ds(pl.multiple_of(core * side, side), side)
     rows = mine.shape[0] // 2
     agg = jnp.where(core == 0, mine[:rows, :], theirs[:rows, :])
     upper = jnp.where(core == 0, theirs[:rows, :], mine[:rows, :])
     back = jnp.concatenate([mine[rows:, :] + theirs[rows:, :], upper], axis=1)
-    pre = jnp.dot(agg, w_one[...], preferred_element_type=F32) + bias[...]
+    pre = jnp.dot(agg, w_first[:, ours], preferred_element_type=F32) + b_first[:, ours]
     squashed = 1.0 / (1.0 + jnp.exp(-pre))
     hidden = (pre * squashed).astype(BF16)
-    d_hidden = lax.dot_general(back, w_two[...], (((1,), (1,)), ((), ())), preferred_element_type=F32)
+    d_hidden = lax.dot_general(
+        back, w_second[ours, :], (((1,), (1,)), ((), ())), preferred_element_type=F32
+    )
     grad_pre = (d_hidden * squashed * (1.0 + pre * (1.0 - squashed))).astype(BF16)
     over_rows = (((0,), (0,)), ((), ()))
-    two = lax.dot_general(hidden, back, over_rows, preferred_element_type=F32)
-    one = lax.dot_general(agg, grad_pre, over_rows, preferred_element_type=F32)
+    two[...] = lax.dot_general(hidden, back, over_rows, preferred_element_type=F32)
+    one[...] = lax.dot_general(agg, grad_pre, over_rows, preferred_element_type=F32)
     bias_row = jnp.sum(grad_pre.astype(F32), axis=0, keepdims=True)
     quarter = one.shape[0] // 4
     corner = place[0] & 3
-    for piece in range(4):
-        at = piece ^ corner
-        span = slice(piece * quarter, (piece + 1) * quarter)
-        out[at, 0:quarter, :] = one[span, :]
-        out[at, quarter : 2 * quarter, :] = two[span, :LANES]
-        out[at, 2 * quarter : 3 * quarter, :] = two[span, LANES:]
-        out[at, 3 * quarter :, :] = jnp.broadcast_to(bias_row, (8, LANES))
+    for k in range(4):
+        span = pl.ds(pl.multiple_of((k ^ corner) * quarter, quarter), quarter)
+        outs[k][0:quarter, :] = one[span, :]
+        outs[k][quarter : 2 * quarter, :] = two[span, :LANES]
+        outs[k][2 * quarter : 3 * quarter, :] = two[span, LANES:]
+        outs[k][3 * quarter :, :] = jnp.broadcast_to(bias_row, (8, LANES))
 
 
 def spread_kernel(place, *refs):
@@ -334,68 +366,71 @@
 ):
     p, r = lax.axis_index("blk"), lax.axis_index("rep")
     place = jnp.stack([p, r]).astype(I32)
-    even = r == 0
     half = features.shape[0]
     rows = 2 * half
     size = block_values.shape[3]
     blocks = rows // size
     hid = w_first.shape[1]
 
-    got_tile = to_sibling(jnp.where(even, cotangent[:, LANES:], features))
-    got_first = to_sibling(cotangent[:, :LANES])
-    panel = pl.pallas_call(
-        assemble_kernel,
-        out_shape=jax.ShapeDtypeStruct((3 * half, LANES), BF16),
-        in_specs=[SMEM_SPEC] + [VMEM_SPEC] * 4,
-        out_specs=VMEM_SPEC,
-    )(place, features, cotangent, got_tile, got_first)
-
-    own = block_values[0]
-    other = to_sibling(own)
-    entries = block_row[0] % blocks + blocks * (block_col[0] % blocks) + blocks * blocks * block_slot[0]
-    filler = jnp.zeros((entries.shape[0], 16 - entries.shape[1] - 1), I32)
-    own_table = jnp.concatenate([entries, block_count[0][:, None], filler], axis=1)
-    table = jnp.concatenate([own_table, to_sibling(own_table)], axis=0).reshape(-1)
-    weights = jnp.broadcast_to(self_weight[:, None], (rows, LANES))
+    mine, give, own_table = pl.pallas_call(
+        pack_kernel,
+        out_shape=(jax.ShapeDtypeStruct((3 * half // 2, LANES), BF16),) * 2
+        + (jax.ShapeDtypeStruct((2 * block_row.shape[1], LANES), I32),),
+        in_specs=[VMEM_SPEC] * 6,
+        out_specs=(VMEM_SPEC,) * 3,
+    )(features, cotangent, block_row[0], block_col[0], block_slot[0], block_count)
+    panel = jnp.concatenate([mine, to_sibling(give)], axis=0)
+
+    own = pltpu.with_memory_space_constraint(block_values[0], pltpu.HBM)
+    other = pltpu.with_memory_space_constraint(to_sibling(own), pltpu.HBM)
+    tables = (own_table, to_sibling(own_table))
+    weights = self_weight.reshape(blocks, size)
 
     middle = (p // 4 == 1) | (p // 4 == 2)
 
-    def quad(value):
-        one = first_way(value)
-        return [value, one, second_way(value), second_way(one)]
-
-    slot_a = z_pairs(panel)
-    near = z_middle(panel)
-    group_o = quad(panel)
-    far = z_middle(slot_a)
-    group_a = quad(slot_a)
-    slot_b = jnp.where(middle, near, z_outward(near))
-    group_b = quad(slot_b)
-    slot_c = jnp.where(middle, far, z_outward(far))
-    group_c = quad(slot_c)
-    ways = [(0, 0), (1, 0), (0, 1), (1, 1)]
-
-    def kinds(slot):
-        return [way + (slot,) for way in ways]
-
-    acc = gather_call(
-        tuple(kinds(0) + kinds(1)), True, False, place, table, weights, own, other, group_o + group_a
-    )
-    summed = gather_call(
-        tuple(kinds(2) + kinds(3)), False, True, place, table, acc, own, other, group_b + group_c
-    )
+    def named(name, move, value, *after):
+        if after:
+            value = lax.optimization_barrier((value,) + after)[0]
+        with jax.named_scope(name):
+            return move(value)
+
+    def products(name, start, work, near=False):
+        kinds = tuple(kind for kind, _ in work)
+        with jax.named_scope(name):
+            return gather_call(kinds, near, tables, start, own, other, [panel for _, panel in work])
+
+    one_o = named("TuO", first_way, panel)
+    two_o = named("TvO", second_way, panel)
+    slot_a = named("TP1", z_pairs, panel)
+    near = named("TP2", z_middle, panel)
+    both_o = named("TvuO", second_way, one_o)
+    far = named("TP3b", z_middle, slot_a, one_o)
+    one_a = named("TuA", first_way, slot_a, two_o)
+    slot_b = jnp.where(middle, near, named("TP3a", z_outward, near, one_o))
+    two_a = named("TvA", z_pairs, two_o, slot_b)
+    (acc,) = products("TK0", weights, [((0, 0, 0), panel), ((1, 0, 0), one_o), ((0, 1, 0), two_o)])
+    one_b = named("TuB", first_way, slot_b, both_o, one_a)
+    two_b = named("TvB", second_way, slot_b, one_a, acc)
+    slot_c = jnp.where(middle, far, named("TP4", z_outward, far))
+    both_b = named("TvuB", second_way, one_b)
+    (acc,) = products("TK1", acc, [((1, 1, 0), both_o), ((0, 0, 1), slot_a), ((1, 0, 1), one_a), ((0, 0, 2), slot_b)])
+    both_a = named("TvuA", z_pairs, both_o, two_a)
+    one_c = named("TuC", first_way, slot_c, two_b, acc)
+    two_c = named("TvC", second_way, slot_c, both_b)
+    (acc,) = products("TK2", acc, [((0, 1, 1), two_a), ((1, 0, 2), one_b), ((0, 1, 2), two_b)])
+    both_c = named("TvuC", second_way, one_c, acc)
+    (acc,) = products("TK3", acc, [((1, 1, 1), both_a), ((1, 1, 2), both_b), ((0, 0, 3), slot_c), ((1, 0, 3), one_c), ((0, 1, 3), two_c)], True)
+    _, summed = products("TK4", acc, [((1, 1, 3), both_c)], True)
     from_sibling = to_sibling(summed)
 
     side = hid // 2
-    w_one = lax.dynamic_slice_in_dim(w_first, r * side, side, 1)
-    bias = lax.dynamic_slice_in_dim(b_first, r * side, side, 0)[None, :]
-    w_two = lax.dynamic_slice_in_dim(w_second, r * side, side, 0)
     pieces = pl.pallas_call(
         dense_kernel,
-        out_shape=jax.ShapeDtypeStruct((4, 3 * side // 4 + 8, LANES), F32),
+        out_shape=(jax.ShapeDtypeStruct((3 * side // 4 + 8, LANES), F32),) * 4,
         in_specs=[SMEM_SPEC] + [VMEM_SPEC] * 5,
-        out_specs=VMEM_SPEC,
-    )(place, summed, from_sibling, w_one, bias, w_two)
+        out_specs=(VMEM_SPEC,) * 4,
+        scratch_shapes=[pltpu.VMEM((side, side), F32), pltpu.VMEM((side, hid), F32)],
+    )(place, summed, from_sibling, w_first, b_first[None, :], w_second)
 
     def in_plane(value, k):
         return send(value, lambda p, r: (p ^ k, r))

time: 140 us -> 113 us (0.81)
  local copies, waits for them, and re-layouts: 16.8 us -> 2.44 us
  starting transfers between devices: 38.9 us -> 34 us
  other arithmetic: 6.01 us -> 1.55 us
  waiting for transfers between devices: 50.6 us -> 48.8 us
    unnamed x56 -> x25, local copies, waits for them, and re-layouts: 13.1 us -> 2.42 us
    ppermute x35 -> x34, starting transfers between devices: 38.9 us -> 34 us  [send(): return lax.ppermute(value, ('blk', 'rep'), pairs)]
    select_n x2, other arithmetic: 2.62 us -> 0.09 us  [the longest x1 0.04 us: mesh_shards(): slot_b = jnp.where(middle, near, named('TP3a', z_outward, near, one_o))]
    ppermute x35 -> x34, waiting for transfers between devices: 50.6 us -> 48.8 us  [send(): return lax.ppermute(value, ('blk', 'rep'), pairs)]
    pallas_call x4 -> x7, Pallas kernels: 23.6 us -> 22.9 us  [the longest x5 18.5 us: gather_call(): pl.pallas_call(functools.partial(gather_kernel, kinds, near), out_shape=o...]
  transfers between devices with their start and end apart: 35 -> 34, of which waited for: 19 -> 21; matrix products, arithmetic and copies ran while one was open for 6% -> 1% of each run, Pallas kernels for 8% -> 15%
where the time goes in v2:
time: 113 us; the launch traced here: 112 us
  waiting for transfers between devices  48.8 us (43%)
  starting transfers between devices  34 us (30%)
  Pallas kernels  24.7 us (22%)
  local copies, waits for them, and re-layouts  2.44 us (2%)
  other arithmetic  1.55 us (1%)
    ppermute x34, waiting for transfers between devices, send(): return lax.ppermute(value, ('blk', 'rep'), pairs)  48.8 us
    ppermute x34, starting transfers between devices, send(): return lax.ppermute(value, ('blk', 'rep'), pairs)  34 us
    pallas_call x5, Pallas kernels, gather_call(): pl.pallas_call(functools.partial(gather_kernel, kinds, near), out_shape=o...  18.5 us
    pallas_call x1, Pallas kernels, mesh_shards(): pl.pallas_call(dense_kernel, out_shape=(jax.ShapeDtypeStruct((3 * side //...  2.59 us
    unnamed x25, local copies, waits for them, and re-layouts  2.42 us
  transfers between devices with their start and end apart: 34, of which 21 were waited for; matrix products, arithmetic and copies ran while one was open for 1% of the time, Pallas kernels for 15%

profile of v2, /device:TPU:0, one launch (start us, length us, event | category | flops | bytes accessed | tf_op | source)
XLA Modules:
  0.0 112.4 jit_solution(5431486505661654173)
XLA Ops:
  1.2 1.9 %shard_map.130 = (bf16[768,128]{1,0:T(8,128)(2,1)}, bf16[768,128]{1,0:T(8,128)(2,1)}, s32[16,128]{1,0:T(8,128)}) custom-call(bf16[512,128]{1,0:T(8,128)(2,1)} %feat.1, bf16[512,256]{1,0:T(8,128)(2,1)} %cot.1, s32[8,12]{1,0:T(8,128)} %bitcast.16, s32[8,12]{1,0:T(8,128)} %bitcast.17, s32[8,12]{1,0:T(8,128)} %bitcast.18, s32[1,8]{1,0:T(1,128)} %count.1), custom_call_target="tpu_custom_call" | custom-call | tf_op jit(solution)/shard_map/pallas_call | solution.py:375
  4.1 2.9 %collective-permute-done.2 = bf16[768,128]{1,0:T(8,128)(2,1)S(1)} collective-permute-done((bf16[768,128]{1,0:T(8,128)(2,1)}, bf16[768,128]{1,0:T(8,128)(2,1)S(1)}, u32[]{:S(2)}, u32[]{:S(2)}) %collective-permute-start.2) | collective-permute-done | bytes 196640 | tf_op jit(solution)/shard_map/ppermute | solution.py:121
  7.0 2.9 %collective-permute-start.3 = (bf16[1536,128]{1,0:T(8,128)(2,1)S(1)}, bf16[1536,128]{1,0:T(8,128)(2,1)S(1)}, u32[]{:S(2)}, u32[]{:S(2)}) collective-permute-start(bf16[1536,128]{1,0:T(8,128)(2,1)S(1)} %constant_dynamic-update-slice_fusion.rest_0_), channel_id=1, source_target_pairs={{0,2},{1,5},{2,0},{3,7},{4,6},{5,1},{6,4},{7,3},{8,10},{9,13},{10,... | collective-permute-start | bytes 1179656 | tf_op jit(solution)/shard_map/TuO/ppermute | solution.py:121
  10.6 1.6 %collective-permute-start.4 = (bf16[1536,128]{1,0:T(8,128)(2,1)S(1)}, bf16[1536,128]{1,0:T(8,128)(2,1)S(1)}, u32[]{:S(2)}, u32[]{:S(2)}) collective-permute-start(bf16[1536,128]{1,0:T(8,128)(2,1)S(1)} %constant_dynamic-update-slice_fusion.rest_0_), channel_id=1, source_target_pairs={{0,4},{1,3},{2,6},{3,1},{4,0},{5,7},{6,2},{7,5},{8,12},{9,11},{10,... | collective-permute-start | bytes 1179656 | tf_op jit(solution)/shard_map/TvO/ppermute | solution.py:121
  12.2 4.4 %collective-permute-start.6 = (bf16[1536,128]{1,0:T(8,128)(2,1)S(1)}, bf16[1536,128]{1,0:T(8,128)(2,1)S(1)}, u32[]{:S(2)}, u32[]{:S(2)}) collective-permute-start(bf16[1536,128]{1,0:T(8,128)(2,1)S(1)} %constant_dynamic-update-slice_fusion.rest_0_), channel_id=1, source_target_pairs={{0,8},{1,9},{2,10},{3,11},{4,12},{5,13},{6,14},{7,15},{8,0},{9,1},... | collective-permute-start | bytes 1179656 | tf_op jit(solution)/shard_map/TP1/ppermute | solution.py:121
  16.5 1.7 %collective-permute-done.3.rest_1_ = bf16[1536,128]{1,0:T(8,128)(2,1)S(1)} collective-permute-done((bf16[1536,128]{1,0:T(8,128)(2,1)S(1)}, bf16[1536,128]{1,0:T(8,128)(2,1)S(1)}, u32[]{:S(2)}, u32[]{:S(2)}) %collective-permute-start.3) | collective-permute-done | bytes 393248 | tf_op jit(solution)/shard_map/TuO/ppermute | solution.py:121
  18.2 1.3 %collective-permute-start.9 = (bf16[1536,128]{1,0:T(8,128)(2,1)S(1)}, bf16[1536,128]{1,0:T(8,128)(2,1)S(1)}, u32[]{:S(2)}, u32[]{:S(2)}) collective-permute-start(bf16[1536,128]{1,0:T(8,128)(2,1)S(1)} %collective-permute-done.8), channel_id=1, source_target_pairs={{8,0},{9,1},{10,2},{11,3},{12,4},{13,5},{14,6},{15,7},{16,24},{17,... | collective-permute-start | bytes 1179656 | tf_op jit(solution)/shard_map/TP3a/ppermute | solution.py:121
  19.6 5.6 %collective-permute-done.6.rest_1_ = bf16[1536,128]{1,0:T(8,128)(2,1)S(1)} collective-permute-done((bf16[1536,128]{1,0:T(8,128)(2,1)S(1)}, bf16[1536,128]{1,0:T(8,128)(2,1)S(1)}, u32[]{:S(2)}, u32[]{:S(2)}) %collective-permute-start.6) | collective-permute-done | bytes 393248 | tf_op jit(solution)/shard_map/TP1/ppermute | solution.py:121
  27.1 6.7 %collective-permute-done.9 = bf16[1536,128]{1,0:T(8,128)(2,1)S(1)} collective-permute-done((bf16[1536,128]{1,0:T(8,128)(2,1)S(1)}, bf16[1536,128]{1,0:T(8,128)(2,1)S(1)}, u32[]{:S(2)}, u32[]{:S(2)}) %collective-permute-start.9) | collective-permute-done | bytes 393248 | tf_op jit(solution)/shard_map/TP3a/ppermute | solution.py:121
  33.9 1.9 %collective-permute-done.7.rest_2_ = bf16[1536,128]{1,0:T(8,128)(2,1)S(1)} collective-permute-done((bf16[1536,128]{1,0:T(8,128)(2,1)S(1)}, bf16[1536,128]{1,0:T(8,128)(2,1)S(1)}, u32[]{:S(2)}, u32[]{:S(2)}) %collective-permute-start.7) | collective-permute-done | bytes 393248 | tf_op jit(solution)/shard_map/TuA/ppermute | solution.py:121
  36.4 1.3 %collective-permute-start.16 = (bf16[1536,128]{1,0:T(8,128)(2,1)S(1)}, bf16[1536,128]{1,0:T(8,128)(2,1)S(1)}, u32[]{:S(2)}, u32[]{:S(2)}) collective-permute-start(bf16[1536,128]{1,0:T(8,128)(2,1)S(1)} %collective-permute-done.15), channel_id=1, source_target_pairs={{8,0},{9,1},{10,2},{11,3},{12,4},{13,5},{14,6},{15,7},{16,24},{17,... | collective-permute-start | bytes 1179656 | tf_op jit(solution)/shard_map/TP4/ppermute | solution.py:121
  37.8 2.8 %collective-permute-start.10 = (bf16[1536,128]{1,0:T(8,128)(2,1)S(1)}, bf16[1536,128]{1,0:T(8,128)(2,1)S(1)}, u32[]{:S(2)}, u32[]{:S(2)}) collective-permute-start(bf16[1536,128]{1,0:T(8,128)(2,1)S(1)} %collective-permute-done.4.rest_2_), channel_id=1, source_target_pairs={{0,8},{1,9},{2,10},{3,11},{4,12},{5,13},{6,14},{7,15},{8,0},{9,1},... | collective-permute-start | bytes 1179656 | tf_op jit(solution)/shard_map/TvA/ppermute | solution.py:121
  40.6 3.0 %collective-permute-done.11.rest_1_ = bf16[1536,128]{1,0:T(8,128)(2,1)S(1)} collective-permute-done((bf16[1536,128]{1,0:T(8,128)(2,1)S(1)}, bf16[1536,128]{1,0:T(8,128)(2,1)S(1)}, u32[]{:S(2)}, u32[]{:S(2)}) %collective-permute-start.11) | collective-permute-done | bytes 393248 | tf_op jit(solution)/shard_map/TuB/ppermute | solution.py:121
  43.5 1.5 %collective-permute-start.14 = (bf16[1536,128]{1,0:T(8,128)(2,1)S(1)}, bf16[1536,128]{1,0:T(8,128)(2,1)S(1)}, u32[]{:S(2)}, u32[]{:S(2)}) collective-permute-start(bf16[1536,128]{1,0:T(8,128)(2,1)S(1)} %collective-permute-done.11.rest_1_), channel_id=1, source_target_pairs={{0,4},{1,3},{2,6},{3,1},{4,0},{5,7},{6,2},{7,5},{8,12},{9,11},{10,... | collective-permute-start | bytes 1179656 | tf_op jit(solution)/shard_map/TvuB/ppermute | solution.py:121
  45.1 4.0 %TK0.1.start = f32[3,9,128,128]{3,2,1,0:T(8,128)S(1)} custom-call(s32[16,128]{1,0:T(8,128)S(1)} %copy-done.1, s32[16,128]{1,0:T(8,128)S(1)} %collective-permute-done.other_table, f32[8,128]{1,0:T(8,128)S(1)} %bitcast.9, bf16[8,12,128,128]{3,2,1,0:T(8,128)(2,1)} %bitcast.11, bf16[8,12,128,128]{3,2,1,0:T(8,128)(2,1)} %collective-permute-done.1.other, ...), custom_call_target="tpu_custom_call" | custom-call | flops 900000000 | bytes 2400000 | tf_op jit(solution)/shard_map/TK0/pallas_call | solution.py:285
  50.3 3.3 %TK1.1.start = f32[3,9,128,128]{3,2,1,0:T(8,128)S(1)} custom-call(s32[16,128]{1,0:T(8,128)S(1)} %copy-done.1, s32[16,128]{1,0:T(8,128)S(1)} %collective-permute-done.other_table, f32[3,9,128,128]{3,2,1,0:T(8,128)S(1)} %TK0.1.start, bf16[8,12,128,128]{3,2,1,0:T(8,128)(2,1)} %bitcast.12, ...), custom_call_target="tpu_custom_call", output_to_operand_aliasing={{}: (2, {})} | custom-call | flops 1200000000 | bytes 3200000 | tf_op jit(solution)/shard_map/TK1/pallas_call | solution.py:285
  53.6 4.1 %collective-permute-done.12.rest_2_ = bf16[1536,128]{1,0:T(8,128)(2,1)S(1)} collective-permute-done((bf16[1536,128]{1,0:T(8,128)(2,1)S(1)}, bf16[1536,128]{1,0:T(8,128)(2,1)S(1)}, u32[]{:S(2)}, u32[]{:S(2)}) %collective-permute-start.12) | collective-permute-done | bytes 393248 | tf_op jit(solution)/shard_map/TvB/ppermute | solution.py:121
  58.2 1.6 %collective-permute-start.13 = (bf16[1536,128]{1,0:T(8,128)(2,1)S(1)}, bf16[1536,128]{1,0:T(8,128)(2,1)S(1)}, u32[]{:S(2)}, u32[]{:S(2)}) collective-permute-start(bf16[1536,128]{1,0:T(8,128)(2,1)S(1)} %collective-permute-done.5.rest_0_), channel_id=1, source_target_pairs={{0,8},{1,9},{2,10},{3,11},{4,12},{5,13},{6,14},{7,15},{8,0},{9,1},... | collective-permute-start | bytes 1179656 | tf_op jit(solution)/shard_map/TvuA/ppermute | solution.py:121
  60.6 3.6 %TK2.1.start = f32[3,9,128,128]{3,2,1,0:T(8,128)S(1)} custom-call(s32[16,128]{1,0:T(8,128)S(1)} %copy-done.1, s32[16,128]{1,0:T(8,128)S(1)} %collective-permute-done.other_table, f32[3,9,128,128]{3,2,1,0:T(8,128)S(1)} %TK1.1.start, bf16[8,12,128,128]{3,2,1,0:T(8,128)(2,1)} %bitcast.13, ...), custom_call_target="tpu_custom_call", output_to_operand_aliasing={{}: (2, {})} | custom-call | flops 900000000 | bytes 2400000 | tf_op jit(solution)/shard_map/TK2/pallas_call | solution.py:285
  64.1 5.6 %collective-permute-done.17.rest_3_ = bf16[1536,128]{1,0:T(8,128)(2,1)S(1)} collective-permute-done((bf16[1536,128]{1,0:T(8,128)(2,1)S(1)}, bf16[1536,128]{1,0:T(8,128)(2,1)S(1)}, u32[]{:S(2)}, u32[]{:S(2)}) %collective-permute-start.17) | collective-permute-done | bytes 393248 | tf_op jit(solution)/shard_map/TuC/ppermute | solution.py:121
  69.7 4.4 %TK3.1.start = f32[3,9,128,128]{3,2,1,0:T(8,128)S(1)} custom-call(s32[16,128]{1,0:T(8,128)S(1)} %copy-done.1, s32[16,128]{1,0:T(8,128)S(1)} %collective-permute-done.other_table, f32[3,9,128,128]{3,2,1,0:T(8,128)S(1)} %TK2.1.start, bf16[8,12,128,128]{3,2,1,0:T(8,128)(2,1)} %bitcast.14, ...), custom_call_target="tpu_custom_call", output_to_operand_aliasing={{}: (2, {})} | custom-call | flops 1500000000 | bytes 4000000 | tf_op jit(solution)/shard_map/TK3/pallas_call | solution.py:285
  74.2 3.3 %collective-permute-done.19.rest_0_ = bf16[1536,128]{1,0:T(8,128)(2,1)S(1)} collective-permute-done((bf16[1536,128]{1,0:T(8,128)(2,1)S(1)}, bf16[1536,128]{1,0:T(8,128)(2,1)S(1)}, u32[]{:S(2)}, u32[]{:S(2)}) %collective-permute-start.19) | collective-permute-done | bytes 393248 | tf_op jit(solution)/shard_map/TvuC/ppermute | solution.py:121
  77.5 3.1 %TK4.1 = (f32[3,9,128,128]{3,2,1,0:T(8,128)S(1)}, bf16[2048,128]{1,0:T(8,128)(2,1)S(1)}) custom-call(s32[16,128]{1,0:T(8,128)S(1)} %copy-done.1, s32[16,128]{1,0:T(8,128)S(1)} %collective-permute-done.other_table, f32[3,9,128,128]{3,2,1,0:T(8,128)S(1)} %TK3.1.start, bf16[8,12,128,128]{3,2,1,0:T(8,128)(2,1)} %bitcast.15, ...), custom_call_target="tpu_custom_call", output_to_operand_aliasing={{0}: (2, {})} | custom-call | flops 300000000 | bytes 800000 | tf_op jit(solution)/shard_map/TK4/pallas_call | solution.py:285
  83.4 2.6 %shard_map.131 = (f32[104,128]{1,0:T(8,128)}, f32[104,128]{1,0:T(8,128)}, f32[104,128]{1,0:T(8,128)}, f32[104,128]{1,0:T(8,128)}) custom-call(s32[2]{0:T(128)} %pad_add_fusion.place, bf16[2048,128]{1,0:T(8,128)(2,1)} %copy-done, bf16[2048,128]{1,0:T(8,128)(2,1)} %copy-done.3, bf16[128,256]{1,0:T(8,128)(2,1)} %w_first.1, f32[1,256]{1,0:T(1,128)} %bitcast.19, ...), custom_call_target="tpu_custom_call" | custom-call | tf_op jit(solution)/shard_map/pallas_call | solution.py:427
  86.0 3.4 %collective-permute-start.23 = (f32[104,128]{1,0:T(8,128)}, f32[104,128]{1,0:T(8,128)S(1)}, u32[]{:S(2)}, u32[]{:S(2)}) collective-permute-start(f32[104,128]{1,0:T(8,128)} %get-tuple-element.41), channel_id=1, source_target_pairs={{0,6},{1,7},{2,4},{3,5},{4,2},{5,3},{6,0},{7,1},{8,14},{9,15},{10,... | collective-permute-start | bytes 159752 | tf_op jit(solution)/shard_map/ppermute | solution.py:121
  92.6 1.6 %collective-permute-start.24 = (f32[104,128]{1,0:T(8,128)S(1)}, f32[104,128]{1,0:T(8,128)S(1)}, u32[]{:S(2)}, u32[]{:S(2)}) collective-permute-start(f32[104,128]{1,0:T(8,128)S(1)} %add_add_fusion.1), channel_id=1, source_target_pairs={{0,8},{1,9},{2,10},{3,11},{4,12},{5,13},{6,14},{7,15},{8,0},{9,1},... | collective-permute-start | bytes 159752 | tf_op jit(solution)/shard_map/ppermute | solution.py:121
  95.3 1.8 %collective-permute-start.26 = (f32[104,128]{1,0:T(8,128)S(1)}, f32[104,128]{1,0:T(8,128)S(1)}, u32[]{:S(2)}, u32[]{:S(2)}) collective-permute-start(f32[104,128]{1,0:T(8,128)S(1)} %add_add_fusion.1), channel_id=1, source_target_pairs={{0,24},{1,25},{2,26},{3,27},{4,28},{5,29},{6,30},{7,31},{8,16},{9,... | collective-permute-start | bytes 159752 | tf_op jit(solution)/shard_map/ppermute | solution.py:121
  97.1 2.7 %collective-permute-done.25 = f32[104,128]{1,0:T(8,128)S(1)} collective-permute-done((f32[104,128]{1,0:T(8,128)S(1)}, f32[104,128]{1,0:T(8,128)S(1)}, u32[]{:S(2)}, u32[]{:S(2)}) %collective-permute-start.25) | collective-permute-done | bytes 53280 | tf_op jit(solution)/shard_map/ppermute | solution.py:121
  99.8 1.5 %collective-permute-done.26 = f32[104,128]{1,0:T(8,128)S(1)} collective-permute-done((f32[104,128]{1,0:T(8,128)S(1)}, f32[104,128]{1,0:T(8,128)S(1)}, u32[]{:S(2)}, u32[]{:S(2)}) %collective-permute-start.26) | collective-permute-done | bytes 53280 | tf_op jit(solution)/shard_map/ppermute | solution.py:121
  102.0 1.7 %collective-permute-start.28 = (f32[104,128]{1,0:T(8,128)S(1)}, f32[104,128]{1,0:T(8,128)S(1)}, u32[]{:S(2)}, u32[]{:S(2)}) collective-permute-start(f32[104,128]{1,0:T(8,128)S(1)} %add_add_fusion.refs_0_), channel_id=1, source_target_pairs={{0,4},{1,5},{2,6},{3,7},{4,0},{5,1},{6,2},{7,3},{8,12},{9,13},{10,... | collective-permute-start | bytes 159752 | tf_op jit(solution)/shard_map/ppermute | solution.py:121
  106.1 2.6 %collective-permute-done.29.refs_3_ = f32[104,128]{1,0:T(8,128)S(1)} collective-permute-done((f32[104,128]{1,0:T(8,128)S(1)}, f32[104,128]{1,0:T(8,128)S(1)}, u32[]{:S(2)}, u32[]{:S(2)}) %collective-permute-start.29) | collective-permute-done | bytes 53280 | tf_op jit(solution)/shard_map/ppermute | solution.py:121
  110.6 1.8 %shard_map.132 = (f32[128,256]{1,0:T(8,128)}, f32[1,256]{1,0:T(1,128)}, f32[256,256]{1,0:T(8,128)}) custom-call(s32[2]{0:T(128)} %pad_add_fusion.place, f32[104,128]{1,0:T(8,128)} %copy-done.4, f32[104,128]{1,0:T(8,128)} %copy-done.5, f32[104,128]{1,0:T(8,128)} %copy-done.6, f32[104,128]{1,0:T(8,128)} %copy-done.7, f32[104,128]{1,0:T(8,128)} %copy-done.8, ...), custom_call_target="tpu_custom_call" | custom-call | tf_op jit(solution)/shard_map/pallas_call | solution.py:444
  (75 shorter events, 19.4 us)
Async XLA Ops:
  0.6 44.4 %collective-permute-start.1 = (bf16[8,12,128,128]{3,2,1,0:T(8,128)(2,1)}, bf16[8,12,128,128]{3,2,1,0:T(8,128)(2,1)}, u32[]{:S(2)}, u32[]{:S(2)}) collective-permute-start(bf16[8,12,128,128]{3,2,1,0:T(8,128)(2,1)} %bitcast.10), channel_id=1, source_target_pairs={{0,1},{1,0},{2,3},{3,2},{4,5},{5,4},{6,7},{7,6},{8,9},{9,8},{10,11... | collective-permute-start | bytes 9437192 | tf_op jit(solution)/shard_map/ppermute | solution.py:121
  3.1 3.9 %collective-permute-start.2 = (bf16[768,128]{1,0:T(8,128)(2,1)}, bf16[768,128]{1,0:T(8,128)(2,1)S(1)}, u32[]{:S(2)}, u32[]{:S(2)}) collective-permute-start(bf16[768,128]{1,0:T(8,128)(2,1)} %get-tuple-element.26), channel_id=1, source_target_pairs={{0,1},{1,0},{2,3},{3,2},{4,5},{5,4},{6,7},{7,6},{8,9},{9,8},{10,11... | collective-permute-start | bytes 589832 | tf_op jit(solution)/shard_map/ppermute | solution.py:121
  7.0 11.3 %collective-permute-start.3 = (bf16[1536,128]{1,0:T(8,128)(2,1)S(1)}, bf16[1536,128]{1,0:T(8,128)(2,1)S(1)}, u32[]{:S(2)}, u32[]{:S(2)}) collective-permute-start(bf16[1536,128]{1,0:T(8,128)(2,1)S(1)} %constant_dynamic-update-slice_fusion.rest_0_), channel_id=1, source_target_pairs={{0,2},{1,5},{2,0},{3,7},{4,6},{5,1},{6,4},{7,3},{8,10},{9,13},{10,... | collective-permute-start | bytes 1179656 | tf_op jit(solution)/shard_map/TuO/ppermute | solution.py:121
  9.9 8.3 %collective-permute-start.8 = (bf16[1536,128]{1,0:T(8,128)(2,1)S(1)}, bf16[1536,128]{1,0:T(8,128)(2,1)S(1)}, u32[]{:S(2)}, u32[]{:S(2)}) collective-permute-start(bf16[1536,128]{1,0:T(8,128)(2,1)S(1)} %constant_dynamic-update-slice_fusion.rest_0_), channel_id=1, source_target_pairs={{8,16},{9,17},{10,18},{11,19},{12,20},{13,21},{14,22},{15,23},{16,... | collective-permute-start | bytes 1179656 | tf_op jit(solution)/shard_map/TP2/ppermute | solution.py:121
  10.6 9.0 %collective-permute-start.4 = (bf16[1536,128]{1,0:T(8,128)(2,1)S(1)}, bf16[1536,128]{1,0:T(8,128)(2,1)S(1)}, u32[]{:S(2)}, u32[]{:S(2)}) collective-permute-start(bf16[1536,128]{1,0:T(8,128)(2,1)S(1)} %constant_dynamic-update-slice_fusion.rest_0_), channel_id=1, source_target_pairs={{0,4},{1,3},{2,6},{3,1},{4,0},{5,7},{6,2},{7,5},{8,12},{9,11},{10,... | collective-permute-start | bytes 1179656 | tf_op jit(solution)/shard_map/TvO/ppermute | solution.py:121
  12.2 12.9 %collective-permute-start.6 = (bf16[1536,128]{1,0:T(8,128)(2,1)S(1)}, bf16[1536,128]{1,0:T(8,128)(2,1)S(1)}, u32[]{:S(2)}, u32[]{:S(2)}) collective-permute-start(bf16[1536,128]{1,0:T(8,128)(2,1)S(1)} %constant_dynamic-update-slice_fusion.rest_0_), channel_id=1, source_target_pairs={{0,8},{1,9},{2,10},{3,11},{4,12},{5,13},{6,14},{7,15},{8,0},{9,1},... | collective-permute-start | bytes 1179656 | tf_op jit(solution)/shard_map/TP1/ppermute | solution.py:121
  18.2 15.6 %collective-permute-start.9 = (bf16[1536,128]{1,0:T(8,128)(2,1)S(1)}, bf16[1536,128]{1,0:T(8,128)(2,1)S(1)}, u32[]{:S(2)}, u32[]{:S(2)}) collective-permute-start(bf16[1536,128]{1,0:T(8,128)(2,1)S(1)} %collective-permute-done.8), channel_id=1, source_target_pairs={{8,0},{9,1},{10,2},{11,3},{12,4},{13,5},{14,6},{15,7},{16,24},{17,... | collective-permute-start | bytes 1179656 | tf_op jit(solution)/shard_map/TP3a/ppermute | solution.py:121
  25.1 10.7 %collective-permute-start.7 = (bf16[1536,128]{1,0:T(8,128)(2,1)S(1)}, bf16[1536,128]{1,0:T(8,128)(2,1)S(1)}, u32[]{:S(2)}, u32[]{:S(2)}) collective-permute-start(bf16[1536,128]{1,0:T(8,128)(2,1)S(1)} %collective-permute-done.6.rest_1_), channel_id=1, source_target_pairs={{0,2},{1,5},{2,0},{3,7},{4,6},{5,1},{6,4},{7,3},{8,10},{9,13},{10,... | collective-permute-start | bytes 1179656 | tf_op jit(solution)/shard_map/TuA/ppermute | solution.py:121
  25.6 10.8 %collective-permute-start.15 = (bf16[1536,128]{1,0:T(8,128)(2,1)S(1)}, bf16[1536,128]{1,0:T(8,128)(2,1)S(1)}, u32[]{:S(2)}, u32[]{:S(2)}) collective-permute-start(bf16[1536,128]{1,0:T(8,128)(2,1)S(1)} %collective-permute-done.6.rest_1_), channel_id=1, source_target_pairs={{8,16},{9,17},{10,18},{11,19},{12,20},{13,21},{14,22},{15,23},{16,... | collective-permute-start | bytes 1179656 | tf_op jit(solution)/shard_map/TP3b/ppermute | solution.py:121
  26.3 9.4 %collective-permute-start.5 = (bf16[1536,128]{1,0:T(8,128)(2,1)S(1)}, bf16[1536,128]{1,0:T(8,128)(2,1)S(1)}, u32[]{:S(2)}, u32[]{:S(2)}) collective-permute-start(bf16[1536,128]{1,0:T(8,128)(2,1)S(1)} %collective-permute-done.3.rest_1_), channel_id=1, source_target_pairs={{0,4},{1,3},{2,6},{3,1},{4,0},{5,7},{6,2},{7,5},{8,12},{9,11},{10,... | collective-permute-start | bytes 1179656 | tf_op jit(solution)/shard_map/TvuO/ppermute | solution.py:121
  35.8 7.8 %collective-permute-start.11 = (bf16[1536,128]{1,0:T(8,128)(2,1)S(1)}, bf16[1536,128]{1,0:T(8,128)(2,1)S(1)}, u32[]{:S(2)}, u32[]{:S(2)}) collective-permute-start(bf16[1536,128]{1,0:T(8,128)(2,1)S(1)} %broadcast_select_fusion.1.rest_3_), channel_id=1, source_target_pairs={{0,2},{1,5},{2,0},{3,7},{4,6},{5,1},{6,4},{7,3},{8,10},{9,13},{10,... | collective-permute-start | bytes 1179656 | tf_op jit(solution)/shard_map/TuB/ppermute | solution.py:121
  36.4 13.8 %collective-permute-start.16 = (bf16[1536,128]{1,0:T(8,128)(2,1)S(1)}, bf16[1536,128]{1,0:T(8,128)(2,1)S(1)}, u32[]{:S(2)}, u32[]{:S(2)}) collective-permute-start(bf16[1536,128]{1,0:T(8,128)(2,1)S(1)} %collective-permute-done.15), channel_id=1, source_target_pairs={{8,0},{9,1},{10,2},{11,3},{12,4},{13,5},{14,6},{15,7},{16,24},{17,... | collective-permute-start | bytes 1179656 | tf_op jit(solution)/shard_map/TP4/ppermute | solution.py:121
  37.7 7.4 %collective-permute-start = (s32[16,128]{1,0:T(8,128)S(1)}, s32[16,128]{1,0:T(8,128)S(1)}, u32[]{:S(2)}, u32[]{:S(2)}) collective-permute-start(s32[16,128]{1,0:T(8,128)S(1)} %copy-done.1), channel_id=1, source_target_pairs={{0,1},{1,0},{2,3},{3,2},{4,5},{5,4},{6,7},{7,6},{8,9},{9,8},{10,11... | collective-permute-start | bytes 24584 | tf_op jit(solution)/shard_map/ppermute | solution.py:121
  37.8 20.4 %collective-permute-start.10 = (bf16[1536,128]{1,0:T(8,128)(2,1)S(1)}, bf16[1536,128]{1,0:T(8,128)(2,1)S(1)}, u32[]{:S(2)}, u32[]{:S(2)}) collective-permute-start(bf16[1536,128]{1,0:T(8,128)(2,1)S(1)} %collective-permute-done.4.rest_2_), channel_id=1, source_target_pairs={{0,8},{1,9},{2,10},{3,11},{4,12},{5,13},{6,14},{7,15},{8,0},{9,1},... | collective-permute-start | bytes 1179656 | tf_op jit(solution)/shard_map/TvA/ppermute | solution.py:121
  43.5 16.2 %collective-permute-start.14 = (bf16[1536,128]{1,0:T(8,128)(2,1)S(1)}, bf16[1536,128]{1,0:T(8,128)(2,1)S(1)}, u32[]{:S(2)}, u32[]{:S(2)}) collective-permute-start(bf16[1536,128]{1,0:T(8,128)(2,1)S(1)} %collective-permute-done.11.rest_1_), channel_id=1, source_target_pairs={{0,4},{1,3},{2,6},{3,1},{4,0},{5,7},{6,2},{7,5},{8,12},{9,11},{10,... | collective-permute-start | bytes 1179656 | tf_op jit(solution)/shard_map/TvuB/ppermute | solution.py:121
  49.1 8.6 %collective-permute-start.12 = (bf16[1536,128]{1,0:T(8,128)(2,1)S(1)}, bf16[1536,128]{1,0:T(8,128)(2,1)S(1)}, u32[]{:S(2)}, u32[]{:S(2)}) collective-permute-start(bf16[1536,128]{1,0:T(8,128)(2,1)S(1)} %broadcast_select_fusion.1.rest_3_), channel_id=1, source_target_pairs={{0,4},{1,3},{2,6},{3,1},{4,0},{5,7},{6,2},{7,5},{8,12},{9,11},{10,... | collective-permute-start | bytes 1179656 | tf_op jit(solution)/shard_map/TvB/ppermute | solution.py:121
  57.7 12.0 %collective-permute-start.17 = (bf16[1536,128]{1,0:T(8,128)(2,1)S(1)}, bf16[1536,128]{1,0:T(8,128)(2,1)S(1)}, u32[]{:S(2)}, u32[]{:S(2)}) collective-permute-start(bf16[1536,128]{1,0:T(8,128)(2,1)S(1)} %broadcast_select_fusion.rest_2_), channel_id=1, source_target_pairs={{0,2},{1,5},{2,0},{3,7},{4,6},{5,1},{6,4},{7,3},{8,10},{9,13},{10,... | collective-permute-start | bytes 1179656 | tf_op jit(solution)/shard_map/TuC/ppermute | solution.py:121
  58.2 11.6 %collective-permute-start.13 = (bf16[1536,128]{1,0:T(8,128)(2,1)S(1)}, bf16[1536,128]{1,0:T(8,128)(2,1)S(1)}, u32[]{:S(2)}, u32[]{:S(2)}) collective-permute-start(bf16[1536,128]{1,0:T(8,128)(2,1)S(1)} %collective-permute-done.5.rest_0_), channel_id=1, source_target_pairs={{0,8},{1,9},{2,10},{3,11},{4,12},{5,13},{6,14},{7,15},{8,0},{9,1},... | collective-permute-start | bytes 1179656 | tf_op jit(solution)/shard_map/TvuA/ppermute | solution.py:121
  59.8 10.0 %collective-permute-start.18 = (bf16[1536,128]{1,0:T(8,128)(2,1)S(1)}, bf16[1536,128]{1,0:T(8,128)(2,1)S(1)}, u32[]{:S(2)}, u32[]{:S(2)}) collective-permute-start(bf16[1536,128]{1,0:T(8,128)(2,1)S(1)} %broadcast_select_fusion.rest_2_), channel_id=1, source_target_pairs={{0,4},{1,3},{2,6},{3,1},{4,0},{5,7},{6,2},{7,5},{8,12},{9,11},{10,... | collective-permute-start | bytes 1179656 | tf_op jit(solution)/shard_map/TvC/ppermute | solution.py:121
  69.7 7.8 %collective-permute-start.19 = (bf16[1536,128]{1,0:T(8,128)(2,1)S(1)}, bf16[1536,128]{1,0:T(8,128)(2,1)S(1)}, u32[]{:S(2)}, u32[]{:S(2)}) collective-permute-start(bf16[1536,128]{1,0:T(8,128)(2,1)S(1)} %collective-permute-done.17.rest_3_), channel_id=1, source_target_pairs={{0,4},{1,3},{2,6},{3,1},{4,0},{5,7},{6,2},{7,5},{8,12},{9,11},{10,... | collective-permute-start | bytes 1179656 | tf_op jit(solution)/shard_map/TvuC/ppermute | solution.py:121
  86.0 4.6 %collective-permute-start.21 = (f32[104,128]{1,0:T(8,128)}, f32[104,128]{1,0:T(8,128)S(1)}, u32[]{:S(2)}, u32[]{:S(2)}) collective-permute-start(f32[104,128]{1,0:T(8,128)} %get-tuple-element.39), channel_id=1, source_target_pairs={{0,2},{1,3},{2,0},{3,1},{4,6},{5,7},{6,4},{7,5},{8,10},{9,11},{10,... | collective-permute-start | bytes 159752 | tf_op jit(solution)/shard_map/ppermute | solution.py:121
  86.0 5.0 %collective-permute-start.22 = (f32[104,128]{1,0:T(8,128)}, f32[104,128]{1,0:T(8,128)S(1)}, u32[]{:S(2)}, u32[]{:S(2)}) collective-permute-start(f32[104,128]{1,0:T(8,128)} %get-tuple-element.40), channel_id=1, source_target_pairs={{0,4},{1,5},{2,6},{3,7},{4,0},{5,1},{6,2},{7,3},{8,12},{9,13},{10,... | collective-permute-start | bytes 159752 | tf_op jit(solution)/shard_map/ppermute | solution.py:121
  86.0 5.7 %collective-permute-start.23 = (f32[104,128]{1,0:T(8,128)}, f32[104,128]{1,0:T(8,128)S(1)}, u32[]{:S(2)}, u32[]{:S(2)}) collective-permute-start(f32[104,128]{1,0:T(8,128)} %get-tuple-element.41), channel_id=1, source_target_pairs={{0,6},{1,7},{2,4},{3,5},{4,2},{5,3},{6,0},{7,1},{8,14},{9,15},{10,... | collective-permute-start | bytes 159752 | tf_op jit(solution)/shard_map/ppermute | solution.py:121
  92.6 4.5 %collective-permute-start.24 = (f32[104,128]{1,0:T(8,128)S(1)}, f32[104,128]{1,0:T(8,128)S(1)}, u32[]{:S(2)}, u32[]{:S(2)}) collective-permute-start(f32[104,128]{1,0:T(8,128)S(1)} %add_add_fusion.1), channel_id=1, source_target_pairs={{0,8},{1,9},{2,10},{3,11},{4,12},{5,13},{6,14},{7,15},{8,0},{9,1},... | collective-permute-start | bytes 159752 | tf_op jit(solution)/shard_map/ppermute | solution.py:121
  94.2 5.6 %collective-permute-start.25 = (f32[104,128]{1,0:T(8,128)S(1)}, f32[104,128]{1,0:T(8,128)S(1)}, u32[]{:S(2)}, u32[]{:S(2)}) collective-permute-start(f32[104,128]{1,0:T(8,128)S(1)} %add_add_fusion.1), channel_id=1, source_target_pairs={{0,16},{1,17},{2,18},{3,19},{4,20},{5,21},{6,22},{7,23},{8,24},{9,... | collective-permute-start | bytes 159752 | tf_op jit(solution)/shard_map/ppermute | solution.py:121
  95.3 6.0 %collective-permute-start.26 = (f32[104,128]{1,0:T(8,128)S(1)}, f32[104,128]{1,0:T(8,128)S(1)}, u32[]{:S(2)}, u32[]{:S(2)}) collective-permute-start(f32[104,128]{1,0:T(8,128)S(1)} %add_add_fusion.1), channel_id=1, source_target_pairs={{0,24},{1,25},{2,26},{3,27},{4,28},{5,29},{6,30},{7,31},{8,16},{9,... | collective-permute-start | bytes 159752 | tf_op jit(solution)/shard_map/ppermute | solution.py:121
  101.3 4.2 %collective-permute-start.27 = (f32[104,128]{1,0:T(8,128)S(1)}, f32[104,128]{1,0:T(8,128)S(1)}, u32[]{:S(2)}, u32[]{:S(2)}) collective-permute-start(f32[104,128]{1,0:T(8,128)S(1)} %add_add_fusion.refs_0_), channel_id=1, source_target_pairs={{0,2},{1,3},{2,0},{3,1},{4,6},{5,7},{6,4},{7,5},{8,10},{9,11},{10,... | collective-permute-start | bytes 159752 | tf_op jit(solution)/shard_map/ppermute | solution.py:121
  102.0 4.1 %collective-permute-start.28 = (f32[104,128]{1,0:T(8,128)S(1)}, f32[104,128]{1,0:T(8,128)S(1)}, u32[]{:S(2)}, u32[]{:S(2)}) collective-permute-start(f32[104,128]{1,0:T(8,128)S(1)} %add_add_fusion.refs_0_), channel_id=1, source_target_pairs={{0,4},{1,5},{2,6},{3,7},{4,0},{5,1},{6,2},{7,3},{8,12},{9,13},{10,... | collective-permute-start | bytes 159752 | tf_op jit(solution)/shard_map/ppermute | solution.py:121
  103.6 5.0 %collective-permute-start.29 = (f32[104,128]{1,0:T(8,128)S(1)}, f32[104,128]{1,0:T(8,128)S(1)}, u32[]{:S(2)}, u32[]{:S(2)}) collective-permute-start(f32[104,128]{1,0:T(8,128)S(1)} %add_add_fusion.refs_0_), channel_id=1, source_target_pairs={{0,6},{1,7},{2,4},{3,5},{4,2},{5,3},{6,0},{7,1},{8,14},{9,15},{10,... | collective-permute-start | bytes 159752 | tf_op jit(solution)/shard_map/ppermute | solution.py:121
  104.9 3.8 %collective-permute-start.30 = (f32[104,128]{1,0:T(8,128)S(1)}, f32[104,128]{1,0:T(8,128)S(1)}, u32[]{:S(2)}, u32[]{:S(2)}) collective-permute-start(f32[104,128]{1,0:T(8,128)S(1)} %add_add_fusion.refs_0_), channel_id=1, source_target_pairs={{0,1},{1,0},{2,3},{3,2},{4,5},{5,4},{6,7},{7,6},{8,9},{9,8},{10,11... | collective-permute-start | bytes 159752 | tf_op jit(solution)/shard_map/ppermute | solution.py:121
  105.5 3.2 %collective-permute-start.31 = (f32[104,128]{1,0:T(8,128)S(1)}, f32[104,128]{1,0:T(8,128)S(1)}, u32[]{:S(2)}, u32[]{:S(2)}) collective-permute-start(f32[104,128]{1,0:T(8,128)S(1)} %collective-permute-done.27.refs_1_), channel_id=1, source_target_pairs={{0,1},{1,0},{2,3},{3,2},{4,5},{5,4},{6,7},{7,6},{8,9},{9,8},{10,11... | collective-permute-start | bytes 159752 | tf_op jit(solution)/shard_map/ppermute | solution.py:121
  106.1 2.6 %collective-permute-start.32 = (f32[104,128]{1,0:T(8,128)S(1)}, f32[104,128]{1,0:T(8,128)S(1)}, u32[]{:S(2)}, u32[]{:S(2)}) collective-permute-start(f32[104,128]{1,0:T(8,128)S(1)} %collective-permute-done.28.refs_2_), channel_id=1, source_target_pairs={{0,1},{1,0},{2,3},{3,2},{4,5},{5,4},{6,7},{7,6},{8,9},{9,8},{10,11... | collective-permute-start | bytes 159752 | tf_op jit(solution)/shard_map/ppermute | solution.py:121
  (14 other events, 107.5 us)

commit v3 on v2

--- a/solution.py
+++ b/solution.py
@@ -121,6 +121,14 @@
     return lax.ppermute(value, ("blk", "rep"), pairs)
 
 
+def in_hbm(value):
+    return pltpu.with_memory_space_constraint(value, pltpu.HBM)
+
+
+def in_vmem(value):
+    return pltpu.with_memory_space_constraint(value, pltpu.VMEM)
+
+
 def to_sibling(value):
     return send(value, lambda p, r: (p, 1 - r))
 
@@ -145,33 +153,40 @@
     return send(value, lambda p, r: (p ^ 4, r) if p // 4 in (1, 2) else None)
 
 
-def pack_kernel(feat, cot, row, col, slot, count, mine, give, table):
+def pack_kernel(away, feat, cot, out):
     core = lax.axis_index("rep")
-    listed = (row[...] & 7) + 8 * (col[...] & 7) + 64 * slot[...]
-    dists, most = listed.shape
-    table[:dists, :most] = listed
-    table[dists : dists + 1, :dists] = count[...]
+    core = 1 - core if away else core
     half, deep = feat.shape[0], feat.shape[0] // 2
     lane = lax.broadcasted_iota(I32, (deep, LANES), 1)
     above, below = cot[:deep, :LANES], cot[deep:, :LANES]
-    above_turned = pltpu.roll(above.astype(F32), LANES // 2, 1).astype(BF16)
-    below_turned = pltpu.roll(below.astype(F32), LANES // 2, 1).astype(BF16)
-    low = jnp.where(lane < LANES // 2, above, below_turned)
-    high = jnp.where(lane < LANES // 2, above_turned, below)
+
+    def turned(value):
+        return pltpu.roll(value.astype(F32), LANES // 2, 1).astype(BF16)
 
     @pl.when(core == 0)
     def _():
-        mine[:half, :] = feat[...]
-        mine[half:, :] = low
-        give[:half, :] = cot[:, LANES:]
-        give[half:, :] = high
+        out[:half, :] = feat[...]
+        out[half : half + deep, :] = jnp.where(lane < LANES // 2, above, turned(below))
 
     @pl.when(core == 1)
     def _():
-        mine[:half, :] = cot[:, LANES:]
-        mine[half:, :] = high
-        give[:half, :] = feat[...]
-        give[half:, :] = low
+        out[:half, :] = cot[:, LANES:]
+        out[half : half + deep, :] = jnp.where(lane < LANES // 2, turned(above), below)
+
+
+def pack_call(away, rows, features, cotangent):
+    return pl.pallas_call(
+        functools.partial(pack_kernel, away),
+        out_shape=pltpu.VMEM((rows, LANES), BF16),
+        in_specs=[VMEM_SPEC] * 2,
+        out_specs=VMEM_SPEC,
+    )(features, cotangent)
+
+
+def table_kernel(row, col, slot, count, after, table):
+    dists, most = row.shape
+    table[:dists, :most] = (row[...] & 7) + 8 * (col[...] & 7) + 64 * slot[...]
+    table[dists : dists + 1, :dists] = count[...]
 
 
 def entry_of(p, core, kind):
@@ -277,11 +292,14 @@
 
 def gather_call(kinds, near, tables, start, own, other, panels):
     n = len(kinds)
+    if near:
+        panels = [in_vmem(panel) for panel in panels]
     first, last = kinds[0] == (0, 0, 0), kinds[-1] == (1, 1, 3)
     most, size = own.shape[1], own.shape[2]
     rows = panels[0].shape[0] * 2 // 3
-    sums = jax.ShapeDtypeStruct((3, rows // size + 1, size, LANES), F32)
-    outs = (sums, jax.ShapeDtypeStruct((2 * rows, LANES), BF16)) if last else (sums,)
+    sums = pltpu.VMEM((3, rows // size + 1, size, LANES), F32)
+    outs = (sums, pltpu.VMEM((2 * rows, LANES), BF16)) if last else (sums,)
+    start = start if first else in_vmem(start)
     return pl.pallas_call(
         functools.partial(gather_kernel, kinds, near),
         out_shape=outs,
@@ -300,9 +318,9 @@
     )(*tables, start, own, other, *panels)
 
 
-def dense_kernel(place, mine, theirs, w_first, b_first, w_second, *rest):
+def dense_kernel(mine, theirs, w_first, b_first, w_second, *rest):
     outs, (one, two) = rest[:4], rest[4:]
-    core = place[1]
+    core = lax.axis_index("rep")
     side = one.shape[1]
     ours = pl.ds(pl.multiple_of(core * side, side), side)
     rows = mine.shape[0] // 2
@@ -321,7 +339,7 @@
     one[...] = lax.dot_general(agg, grad_pre, over_rows, preferred_element_type=F32)
     bias_row = jnp.sum(grad_pre.astype(F32), axis=0, keepdims=True)
     quarter = one.shape[0] // 4
-    corner = place[0] & 3
+    corner = lax.axis_index("blk") & 3
     for k in range(4):
         span = pl.ds(pl.multiple_of((k ^ corner) * quarter, quarter), quarter)
         outs[k][0:quarter, :] = one[span, :]
@@ -330,9 +348,9 @@
         outs[k][3 * quarter :, :] = jnp.broadcast_to(bias_row, (8, LANES))
 
 
-def spread_kernel(place, *refs):
+def spread_kernel(*refs):
     pieces, (one, bias, two) = refs[:8], refs[8:]
-    core, corner = place[1], place[0] & 3
+    core, corner = lax.axis_index("rep"), lax.axis_index("blk") & 3
     quarter = one.shape[0] // 4
     for k in range(4):
         rows = pl.ds(pl.multiple_of((k ^ corner) * quarter, quarter), quarter)
@@ -364,26 +382,29 @@
     block_count,
     block_values,
 ):
-    p, r = lax.axis_index("blk"), lax.axis_index("rep")
-    place = jnp.stack([p, r]).astype(I32)
+    p = lax.axis_index("blk")
     half = features.shape[0]
     rows = 2 * half
     size = block_values.shape[3]
     blocks = rows // size
     hid = w_first.shape[1]
 
-    mine, give, own_table = pl.pallas_call(
-        pack_kernel,
-        out_shape=(jax.ShapeDtypeStruct((3 * half // 2, LANES), BF16),) * 2
-        + (jax.ShapeDtypeStruct((2 * block_row.shape[1], LANES), I32),),
-        in_specs=[VMEM_SPEC] * 6,
-        out_specs=(VMEM_SPEC,) * 3,
-    )(features, cotangent, block_row[0], block_col[0], block_slot[0], block_count)
-    panel = jnp.concatenate([mine, to_sibling(give)], axis=0)
-
-    own = pltpu.with_memory_space_constraint(block_values[0], pltpu.HBM)
-    other = pltpu.with_memory_space_constraint(to_sibling(own), pltpu.HBM)
+    give = pack_call(True, 3 * half // 2, features, cotangent)
+    got = to_sibling(give)
+    panel = pack_call(False, 3 * half, features, cotangent)
+    panel = lax.dynamic_update_slice(panel, got, (3 * half // 2, 0))
+
+    own = in_hbm(block_values[0])
+    held, panel = lax.optimization_barrier((own, panel))
+    other = in_hbm(to_sibling(held))
+    own_table = pl.pallas_call(
+        table_kernel,
+        out_shape=jax.ShapeDtypeStruct((2 * block_row.shape[1], LANES), I32),
+        in_specs=[VMEM_SPEC] * 4 + [HBM_SPEC],
+        out_specs=VMEM_SPEC,
+    )(block_row[0], block_col[0], block_slot[0], block_count, panel)
     tables = (own_table, to_sibling(own_table))
+    later = lax.optimization_barrier((panel, own_table))[0]
     weights = self_weight.reshape(blocks, size)
 
     middle = (p // 4 == 1) | (p // 4 == 2)
@@ -399,38 +420,39 @@
         with jax.named_scope(name):
             return gather_call(kinds, near, tables, start, own, other, [panel for _, panel in work])
 
+    slot_a = named("TP1", z_pairs, panel)
     one_o = named("TuO", first_way, panel)
     two_o = named("TvO", second_way, panel)
-    slot_a = named("TP1", z_pairs, panel)
-    near = named("TP2", z_middle, panel)
+    near = named("TP2", z_middle, later)
     both_o = named("TvuO", second_way, one_o)
     far = named("TP3b", z_middle, slot_a, one_o)
     one_a = named("TuA", first_way, slot_a, two_o)
-    slot_b = jnp.where(middle, near, named("TP3a", z_outward, near, one_o))
-    two_a = named("TvA", z_pairs, two_o, slot_b)
-    (acc,) = products("TK0", weights, [((0, 0, 0), panel), ((1, 0, 0), one_o), ((0, 1, 0), two_o)])
-    one_b = named("TuB", first_way, slot_b, both_o, one_a)
-    two_b = named("TvB", second_way, slot_b, one_a, acc)
-    slot_c = jnp.where(middle, far, named("TP4", z_outward, far))
+    slot_b = jnp.where(middle, near, named("TP3a", z_outward, near, slot_a))
+    two_a = named("TvA", second_way, slot_a, one_a)
+    (first_acc,) = products("TK0", weights, [((0, 0, 0), panel), ((1, 0, 0), one_o), ((0, 1, 0), two_o)])
+    one_b = named("TuB", first_way, slot_b, one_a, other)
+    two_b = named("TvB", second_way, slot_b, one_a, two_a, first_acc)
+    (acc,) = products("TK1", first_acc, [((1, 1, 0), both_o), ((0, 0, 1), slot_a), ((1, 0, 1), one_a), ((1, 0, 2), one_b)])
+    slot_c = named("TP4", z_outward, far, both_o, one_a)
+    slot_c = jnp.where(middle, lax.optimization_barrier((far, acc))[0], slot_c)
     both_b = named("TvuB", second_way, one_b)
-    (acc,) = products("TK1", acc, [((1, 1, 0), both_o), ((0, 0, 1), slot_a), ((1, 0, 1), one_a), ((0, 0, 2), slot_b)])
-    both_a = named("TvuA", z_pairs, both_o, two_a)
-    one_c = named("TuC", first_way, slot_c, two_b, acc)
-    two_c = named("TvC", second_way, slot_c, both_b)
-    (acc,) = products("TK2", acc, [((0, 1, 1), two_a), ((1, 0, 2), one_b), ((0, 1, 2), two_b)])
+    both_a = named("TvuA", z_pairs, both_o, two_b)
+    one_c = named("TuC", first_way, slot_c)
+    two_c = named("TvC", second_way, slot_c, two_b)
+    (acc,) = products("TK2", acc, [((0, 1, 1), two_a), ((0, 0, 2), slot_b), ((0, 1, 2), two_b)])
     both_c = named("TvuC", second_way, one_c, acc)
     (acc,) = products("TK3", acc, [((1, 1, 1), both_a), ((1, 1, 2), both_b), ((0, 0, 3), slot_c), ((1, 0, 3), one_c), ((0, 1, 3), two_c)], True)
     _, summed = products("TK4", acc, [((1, 1, 3), both_c)], True)
-    from_sibling = to_sibling(summed)
+    from_sibling = in_vmem(to_sibling(summed))
 
     side = hid // 2
     pieces = pl.pallas_call(
         dense_kernel,
-        out_shape=(jax.ShapeDtypeStruct((3 * side // 4 + 8, LANES), F32),) * 4,
-        in_specs=[SMEM_SPEC] + [VMEM_SPEC] * 5,
+        out_shape=(pltpu.VMEM((3 * side // 4 + 8, LANES), F32),) * 4,
+        in_specs=[VMEM_SPEC] * 5,
         out_specs=(VMEM_SPEC,) * 4,
         scratch_shapes=[pltpu.VMEM((side, side), F32), pltpu.VMEM((side, hid), F32)],
-    )(place, summed, from_sibling, w_first, b_first[None, :], w_second)
+    )(in_vmem(summed), from_sibling, w_first, b_first[None, :], w_second)
 
     def in_plane(value, k):
         return send(value, lambda p, r: (p ^ k, r))
@@ -440,7 +462,8 @@
     across = [in_plane(total, 4 * k) for k in (1, 2, 3)]
     total = (total + across[0]) + (across[1] + across[2])
     full = [total] + [in_plane(total, k) for k in (1, 2, 3)]
-    back = [to_sibling(value) for value in full]
+    back = [in_vmem(to_sibling(value)) for value in full]
+    full = [in_vmem(value) for value in full]
     grad_w1, grad_b1, grad_w2 = pl.pallas_call(
         spread_kernel,
         out_shape=(
@@ -448,9 +471,9 @@
             jax.ShapeDtypeStruct((1, hid), F32),
             jax.ShapeDtypeStruct((hid, hid), F32),
         ),
-        in_specs=[SMEM_SPEC] + [VMEM_SPEC] * 8,
+        in_specs=[VMEM_SPEC] * 8,
         out_specs=(VMEM_SPEC,) * 3,
-    )(place, *full, *back)
+    )(*full, *back)
     return (grad_w1, grad_b1.reshape(hid), grad_w2)
 
 

time: 113 us -> 102 us (0.903)
  waiting for transfers between devices: 48.8 us -> 33.9 us
  starting transfers between devices: 34 us -> 41.3 us
  Pallas kernels: 24.7 us -> 23 us
  other arithmetic: 1.55 us -> 0.12 us
    ppermute x34, waiting for transfers between devices: 48.8 us -> 33.9 us  [send(): return lax.ppermute(value, ('blk', 'rep'), pairs)]
    ppermute x34, starting transfers between devices: 34 us -> 41.3 us  [send(): return lax.ppermute(value, ('blk', 'rep'), pairs)]
    pallas_call x5, Pallas kernels: 18.5 us -> 17 us  [gather_call(): pl.pallas_call(functools.partial(gather_kernel, kinds, near), out_shape=o...]
    pallas_call x2 -> x4, Pallas kernels: 4.48 us -> 5.2 us  [the longest x2 2.25 us: pack_call(): pl.pallas_call(functools.partial(pack_kernel, away), out_shape=pltpu.VMEM...]
    unnamed x25 -> x8, local copies, waits for them, and re-layouts: 2.42 us -> 1.7 us
  transfers between devices with their start and end apart: 34 -> 34, of which waited for: 21 -> 20; matrix products, arithmetic and copies ran while one was open for 1% -> 0% of each run, Pallas kernels for 15% -> 16%
where the time goes in v3:
time: 102 us; the launch traced here: 101 us
  starting transfers between devices  41.3 us (40%)
  waiting for transfers between devices  33.9 us (33%)
  Pallas kernels  23 us (23%)
  local copies, waits for them, and re-layouts  1.73 us (2%)
    ppermute x34, starting transfers between devices, send(): return lax.ppermute(value, ('blk', 'rep'), pairs)  41.3 us
    ppermute x34, waiting for transfers between devices, send(): return lax.ppermute(value, ('blk', 'rep'), pairs)  33.9 us
    pallas_call x5, Pallas kernels, gather_call(): pl.pallas_call(functools.partial(gather_kernel, kinds, near), out_shape=o...  17 us
    pallas_call x2, Pallas kernels, pack_call(): pl.pallas_call(functools.partial(pack_kernel, away), out_shape=pltpu.VMEM...  2.25 us
  transfers between devices with their start and end apart: 34, of which 20 were waited for; matrix products, arithmetic and copies ran while one was open for 0% of the time, Pallas kernels for 16%

profile of v3, /device:TPU:0, one launch (start us, length us, event | category | flops | bytes accessed | tf_op | source)
XLA Modules:
  0.0 100.9 jit_solution(16400019992819094952)
XLA Ops:
  3.8 2.8 %collective-permute-start.6 = (bf16[1536,128]{1,0:T(8,128)(2,1)S(1)}, bf16[1536,128]{1,0:T(8,128)(2,1)S(1)}, u32[]{:S(2)}, u32[]{:S(2)}) collective-permute-start(bf16[1536,128]{1,0:T(8,128)(2,1)S(1)} %constant_dynamic-update-slice_fusion.after.rest_0_), channel_id=1, source_target_pairs={{0,8},{1,9},{2,10},{3,11},{4,12},{5,13},{6,14},{7,15},{8,0},{9,1},... | collective-permute-start | bytes 1179656 | tf_op jit(solution)/shard_map/TP1/ppermute | solution.py:121
  6.6 1.5 %collective-permute-start.4 = (bf16[1536,128]{1,0:T(8,128)(2,1)S(1)}, bf16[1536,128]{1,0:T(8,128)(2,1)S(1)}, u32[]{:S(2)}, u32[]{:S(2)}) collective-permute-start(bf16[1536,128]{1,0:T(8,128)(2,1)S(1)} %constant_dynamic-update-slice_fusion.after.rest_0_), channel_id=1, source_target_pairs={{0,4},{1,3},{2,6},{3,1},{4,0},{5,7},{6,2},{7,5},{8,12},{9,11},{10,... | collective-permute-start | bytes 1179656 | tf_op jit(solution)/shard_map/TvO/ppermute | solution.py:121
  8.1 1.3 %shard_map.132.own_table = s32[16,128]{1,0:T(8,128)} custom-call(s32[8,12]{1,0:T(8,128)} %bitcast.14, s32[8,12]{1,0:T(8,128)} %bitcast.15, s32[8,12]{1,0:T(8,128)} %bitcast.16, s32[1,8]{1,0:T(1,128)} %count.1, bf16[1536,128]{1,0:T(8,128)(2,1)} %copy-done), custom_call_target="tpu_custom_call" | custom-call | tf_op jit(solution)/shard_map/pallas_call | solution.py:400
  10.2 1.6 %collective-permute-start.3 = (bf16[1536,128]{1,0:T(8,128)(2,1)}, bf16[1536,128]{1,0:T(8,128)(2,1)S(1)}, u32[]{:S(2)}, u32[]{:S(2)}) collective-permute-start(bf16[1536,128]{1,0:T(8,128)(2,1)} %copy-done), channel_id=1, source_target_pairs={{0,2},{1,5},{2,0},{3,7},{4,6},{5,1},{6,4},{7,3},{8,10},{9,13},{10,... | collective-permute-start | bytes 1179656 | tf_op jit(solution)/shard_map/TuO/ppermute | solution.py:121
  11.7 4.5 %collective-permute-done.6.rest_1_ = bf16[1536,128]{1,0:T(8,128)(2,1)S(1)} collective-permute-done((bf16[1536,128]{1,0:T(8,128)(2,1)S(1)}, bf16[1536,128]{1,0:T(8,128)(2,1)S(1)}, u32[]{:S(2)}, u32[]{:S(2)}) %collective-permute-start.6) | collective-permute-done | bytes 393248 | tf_op jit(solution)/shard_map/TP1/ppermute | solution.py:121
  16.2 2.2 %collective-permute-start.7 = (bf16[1536,128]{1,0:T(8,128)(2,1)S(1)}, bf16[1536,128]{1,0:T(8,128)(2,1)S(1)}, u32[]{:S(2)}, u32[]{:S(2)}) collective-permute-start(bf16[1536,128]{1,0:T(8,128)(2,1)S(1)} %collective-permute-done.6.rest_1_), channel_id=1, source_target_pairs={{0,2},{1,5},{2,0},{3,7},{4,6},{5,1},{6,4},{7,3},{8,10},{9,13},{10,... | collective-permute-start | bytes 1179656 | tf_op jit(solution)/shard_map/TuA/ppermute | solution.py:121
  20.5 1.6 %collective-permute-start.5 = (bf16[1536,128]{1,0:T(8,128)(2,1)S(1)}, bf16[1536,128]{1,0:T(8,128)(2,1)S(1)}, u32[]{:S(2)}, u32[]{:S(2)}) collective-permute-start(bf16[1536,128]{1,0:T(8,128)(2,1)S(1)} %collective-permute-done.3.rest_1_), channel_id=1, source_target_pairs={{0,4},{1,3},{2,6},{3,1},{4,0},{5,7},{6,2},{7,5},{8,12},{9,11},{10,... | collective-permute-start | bytes 1179656 | tf_op jit(solution)/shard_map/TvuO/ppermute | solution.py:121
  22.0 4.6 %collective-permute-done.7.rest_2_ = bf16[1536,128]{1,0:T(8,128)(2,1)S(1)} collective-permute-done((bf16[1536,128]{1,0:T(8,128)(2,1)S(1)}, bf16[1536,128]{1,0:T(8,128)(2,1)S(1)}, u32[]{:S(2)}, u32[]{:S(2)}) %collective-permute-start.7) | collective-permute-done | bytes 393248 | tf_op jit(solution)/shard_map/TuA/ppermute | solution.py:121
  26.7 1.5 %collective-permute-start.11 = (bf16[1536,128]{1,0:T(8,128)(2,1)S(1)}, bf16[1536,128]{1,0:T(8,128)(2,1)S(1)}, u32[]{:S(2)}, u32[]{:S(2)}) collective-permute-start(bf16[1536,128]{1,0:T(8,128)(2,1)S(1)} %collective-permute-done.6.rest_1_), channel_id=1, source_target_pairs={{0,4},{1,3},{2,6},{3,1},{4,0},{5,7},{6,2},{7,5},{8,12},{9,11},{10,... | collective-permute-start | bytes 1179656 | tf_op jit(solution)/shard_map/TvA/ppermute | solution.py:121
  28.2 5.2 %collective-permute-done.9 = bf16[1536,128]{1,0:T(8,128)(2,1)S(1)} collective-permute-done((bf16[1536,128]{1,0:T(8,128)(2,1)S(1)}, bf16[1536,128]{1,0:T(8,128)(2,1)S(1)}, u32[]{:S(2)}, u32[]{:S(2)}) %collective-permute-start.9) | collective-permute-done | bytes 393248 | tf_op jit(solution)/shard_map/TP3a/ppermute | solution.py:121
  34.9 1.9 %collective-permute-start.1 = (s32[16,128]{1,0:T(8,128)}, s32[16,128]{1,0:T(8,128)S(1)}, u32[]{:S(2)}, u32[]{:S(2)}) collective-permute-start(s32[16,128]{1,0:T(8,128)} %shard_map.132.own_table), channel_id=1, source_target_pairs={{0,1},{1,0},{2,3},{3,2},{4,5},{5,4},{6,7},{7,6},{8,9},{9,8},{10,11... | collective-permute-start | bytes 24584 | tf_op jit(solution)/shard_map/ppermute | solution.py:121
  39.4 3.8 %TK0.1.start = f32[3,9,128,128]{3,2,1,0:T(8,128)S(1)} custom-call(s32[16,128]{1,0:T(8,128)S(1)} %copy-done.2, s32[16,128]{1,0:T(8,128)S(1)} %collective-permute-done.1.other_table, f32[8,128]{1,0:T(8,128)S(1)} %bitcast.7, bf16[8,12,128,128]{3,2,1,0:T(8,128)(2,1)} %bitcast.9, bf16[8,12,128,128]{3,2,1,0:T(8,128)(2,1)} %collective-permute-done.2.other, ...), custom_call_target="tpu_custom_call" | custom-call | flops 900000000 | bytes 2400000 | tf_op jit(solution)/shard_map/TK0/pallas_call | solution.py:303
  43.3 1.3 %collective-permute-start.12 = (bf16[1536,128]{1,0:T(8,128)(2,1)S(1)}, bf16[1536,128]{1,0:T(8,128)(2,1)S(1)}, u32[]{:S(2)}, u32[]{:S(2)}) collective-permute-start(bf16[1536,128]{1,0:T(8,128)(2,1)S(1)} %broadcast_select_fusion.1.rest_1_), channel_id=1, source_target_pairs={{0,4},{1,3},{2,6},{3,1},{4,0},{5,7},{6,2},{7,5},{8,12},{9,11},{10,... | collective-permute-start | bytes 1179656 | tf_op jit(solution)/shard_map/TvB/ppermute | solution.py:121
  44.6 3.6 %TK1.1.start = f32[3,9,128,128]{3,2,1,0:T(8,128)S(1)} custom-call(s32[16,128]{1,0:T(8,128)S(1)} %copy-done.2, s32[16,128]{1,0:T(8,128)S(1)} %collective-permute-done.1.other_table, f32[3,9,128,128]{3,2,1,0:T(8,128)S(1)} %TK0.1.start, bf16[8,12,128,128]{3,2,1,0:T(8,128)(2,1)} %bitcast.10, ...), custom_call_target="tpu_custom_call", output_to_operand_aliasing={{}: (2, {})} | custom-call | flops 1200000000 | bytes 3200000 | tf_op jit(solution)/shard_map/TK1/pallas_call | solution.py:303
  48.3 2.2 %collective-permute-start.17 = (bf16[1536,128]{1,0:T(8,128)(2,1)S(1)}, bf16[1536,128]{1,0:T(8,128)(2,1)S(1)}, u32[]{:S(2)}, u32[]{:S(2)}) collective-permute-start(bf16[1536,128]{1,0:T(8,128)(2,1)S(1)} %broadcast_select_fusion.rest_2_), channel_id=1, source_target_pairs={{0,2},{1,5},{2,0},{3,7},{4,6},{5,1},{6,4},{7,3},{8,10},{9,13},{10,... | collective-permute-start | bytes 1179656 | tf_op jit(solution)/shard_map/TuC/ppermute | solution.py:121
  52.4 3.1 %collective-permute-start.13 = (bf16[1536,128]{1,0:T(8,128)(2,1)S(1)}, bf16[1536,128]{1,0:T(8,128)(2,1)S(1)}, u32[]{:S(2)}, u32[]{:S(2)}) collective-permute-start(bf16[1536,128]{1,0:T(8,128)(2,1)S(1)} %collective-permute-done.5.rest_0_), channel_id=1, source_target_pairs={{0,8},{1,9},{2,10},{3,11},{4,12},{5,13},{6,14},{7,15},{8,0},{9,1},... | collective-permute-start | bytes 1179656 | tf_op jit(solution)/shard_map/TvuA/ppermute | solution.py:121
  55.5 2.8 %TK2.1.start = f32[3,9,128,128]{3,2,1,0:T(8,128)S(1)} custom-call(s32[16,128]{1,0:T(8,128)S(1)} %copy-done.2, s32[16,128]{1,0:T(8,128)S(1)} %collective-permute-done.1.other_table, f32[3,9,128,128]{3,2,1,0:T(8,128)S(1)} %TK1.1.start, bf16[8,12,128,128]{3,2,1,0:T(8,128)(2,1)} %bitcast.11, ...), custom_call_target="tpu_custom_call", output_to_operand_aliasing={{}: (2, {})} | custom-call | flops 900000000 | bytes 2400000 | tf_op jit(solution)/shard_map/TK2/pallas_call | solution.py:303
  58.3 1.7 %collective-permute-done.17.rest_3_ = bf16[1536,128]{1,0:T(8,128)(2,1)S(1)} collective-permute-done((bf16[1536,128]{1,0:T(8,128)(2,1)S(1)}, bf16[1536,128]{1,0:T(8,128)(2,1)S(1)}, u32[]{:S(2)}, u32[]{:S(2)}) %collective-permute-start.17) | collective-permute-done | bytes 393248 | tf_op jit(solution)/shard_map/TuC/ppermute | solution.py:121
  60.9 2.6 %collective-permute-done.13.rest_0_ = bf16[1536,128]{1,0:T(8,128)(2,1)S(1)} collective-permute-done((bf16[1536,128]{1,0:T(8,128)(2,1)S(1)}, bf16[1536,128]{1,0:T(8,128)(2,1)S(1)}, u32[]{:S(2)}, u32[]{:S(2)}) %collective-permute-start.13) | collective-permute-done | bytes 393248 | tf_op jit(solution)/shard_map/TvuA/ppermute | solution.py:121
  63.9 3.7 %TK3.1.start = f32[3,9,128,128]{3,2,1,0:T(8,128)S(1)} custom-call(s32[16,128]{1,0:T(8,128)S(1)} %copy-done.2, s32[16,128]{1,0:T(8,128)S(1)} %collective-permute-done.1.other_table, f32[3,9,128,128]{3,2,1,0:T(8,128)S(1)} %TK2.1.start, bf16[8,12,128,128]{3,2,1,0:T(8,128)(2,1)} %bitcast.12, ...), custom_call_target="tpu_custom_call", output_to_operand_aliasing={{}: (2, {})} | custom-call | flops 1500000000 | bytes 4000000 | tf_op jit(solution)/shard_map/TK3/pallas_call | solution.py:303
  68.1 3.1 %TK4.1 = (f32[3,9,128,128]{3,2,1,0:T(8,128)S(1)}, bf16[2048,128]{1,0:T(8,128)(2,1)S(1)}) custom-call(s32[16,128]{1,0:T(8,128)S(1)} %copy-done.2, s32[16,128]{1,0:T(8,128)S(1)} %collective-permute-done.1.other_table, f32[3,9,128,128]{3,2,1,0:T(8,128)S(1)} %TK3.1.start, bf16[8,12,128,128]{3,2,1,0:T(8,128)(2,1)} %bitcast.13, ...), custom_call_target="tpu_custom_call", output_to_operand_aliasing={{0}: (2, {})} | custom-call | flops 300000000 | bytes 800000 | tf_op jit(solution)/shard_map/TK4/pallas_call | solution.py:303
  71.9 1.5 %collective-permute-done.20.theirs = bf16[2048,128]{1,0:T(8,128)(2,1)S(1)} collective-permute-done((bf16[2048,128]{1,0:T(8,128)(2,1)S(1)}, bf16[2048,128]{1,0:T(8,128)(2,1)S(1)}, u32[]{:S(2)}, u32[]{:S(2)}) %collective-permute-start.20) | collective-permute-done | bytes 524320 | tf_op jit(solution)/shard_map/ppermute | solution.py:121
  73.5 1.6 %shard_map.133 = (f32[104,128]{1,0:T(8,128)S(1)}, f32[104,128]{1,0:T(8,128)S(1)}, f32[104,128]{1,0:T(8,128)S(1)}, f32[104,128]{1,0:T(8,128)S(1)}) custom-call(bf16[2048,128]{1,0:T(8,128)(2,1)S(1)} %get-tuple-element.39.mine, bf16[2048,128]{1,0:T(8,128)(2,1)S(1)} %collective-permute-done.20.theirs, bf16[128,256]{1,0:T(8,128)(2,1)} %w_first.1, ...), custom_call_target="tpu_custom_call" | custom-call | tf_op jit(solution)/shard_map/pallas_call | solution.py:449
  75.1 1.9 %collective-permute-start.21 = (f32[104,128]{1,0:T(8,128)S(1)}, f32[104,128]{1,0:T(8,128)S(1)}, u32[]{:S(2)}, u32[]{:S(2)}) collective-permute-start(f32[104,128]{1,0:T(8,128)S(1)} %get-tuple-element.41), channel_id=1, source_target_pairs={{0,2},{1,3},{2,0},{3,1},{4,6},{5,7},{6,4},{7,5},{8,10},{9,11},{10,... | collective-permute-start | bytes 159752 | tf_op jit(solution)/shard_map/ppermute | solution.py:121
  77.0 1.7 %collective-permute-start.23 = (f32[104,128]{1,0:T(8,128)S(1)}, f32[104,128]{1,0:T(8,128)S(1)}, u32[]{:S(2)}, u32[]{:S(2)}) collective-permute-start(f32[104,128]{1,0:T(8,128)S(1)} %get-tuple-element.43), channel_id=1, source_target_pairs={{0,6},{1,7},{2,4},{3,5},{4,2},{5,3},{6,0},{7,1},{8,14},{9,15},{10,... | collective-permute-start | bytes 159752 | tf_op jit(solution)/shard_map/ppermute | solution.py:121
  79.3 2.2 %collective-permute-done.22 = f32[104,128]{1,0:T(8,128)S(1)} collective-permute-done((f32[104,128]{1,0:T(8,128)S(1)}, f32[104,128]{1,0:T(8,128)S(1)}, u32[]{:S(2)}, u32[]{:S(2)}) %collective-permute-start.22) | collective-permute-done | bytes 53280 | tf_op jit(solution)/shard_map/ppermute | solution.py:121
  82.1 2.8 %collective-permute-start.24 = (f32[104,128]{1,0:T(8,128)S(1)}, f32[104,128]{1,0:T(8,128)S(1)}, u32[]{:S(2)}, u32[]{:S(2)}) collective-permute-start(f32[104,128]{1,0:T(8,128)S(1)} %add_add_fusion.1), channel_id=1, source_target_pairs={{0,8},{1,9},{2,10},{3,11},{4,12},{5,13},{6,14},{7,15},{8,0},{9,1},... | collective-permute-start | bytes 159752 | tf_op jit(solution)/shard_map/ppermute | solution.py:121
  85.0 2.2 %collective-permute-start.25 = (f32[104,128]{1,0:T(8,128)S(1)}, f32[104,128]{1,0:T(8,128)S(1)}, u32[]{:S(2)}, u32[]{:S(2)}) collective-permute-start(f32[104,128]{1,0:T(8,128)S(1)} %add_add_fusion.1), channel_id=1, source_target_pairs={{0,16},{1,17},{2,18},{3,19},{4,20},{5,21},{6,22},{7,23},{8,24},{9,... | collective-permute-start | bytes 159752 | tf_op jit(solution)/shard_map/ppermute | solution.py:121
  87.1 1.4 %collective-permute-start.26 = (f32[104,128]{1,0:T(8,128)S(1)}, f32[104,128]{1,0:T(8,128)S(1)}, u32[]{:S(2)}, u32[]{:S(2)}) collective-permute-start(f32[104,128]{1,0:T(8,128)S(1)} %add_add_fusion.1), channel_id=1, source_target_pairs={{0,24},{1,25},{2,26},{3,27},{4,28},{5,29},{6,30},{7,31},{8,16},{9,... | collective-permute-start | bytes 159752 | tf_op jit(solution)/shard_map/ppermute | solution.py:121
  88.5 2.2 %collective-permute-done.25 = f32[104,128]{1,0:T(8,128)S(1)} collective-permute-done((f32[104,128]{1,0:T(8,128)S(1)}, f32[104,128]{1,0:T(8,128)S(1)}, u32[]{:S(2)}, u32[]{:S(2)}) %collective-permute-start.25) | collective-permute-done | bytes 53280 | tf_op jit(solution)/shard_map/ppermute | solution.py:121
  90.7 2.5 %collective-permute-done.26 = f32[104,128]{1,0:T(8,128)S(1)} collective-permute-done((f32[104,128]{1,0:T(8,128)S(1)}, f32[104,128]{1,0:T(8,128)S(1)}, u32[]{:S(2)}, u32[]{:S(2)}) %collective-permute-start.26) | collective-permute-done | bytes 53280 | tf_op jit(solution)/shard_map/ppermute | solution.py:121
  93.8 2.9 %collective-permute-start.29 = (f32[104,128]{1,0:T(8,128)S(1)}, f32[104,128]{1,0:T(8,128)S(1)}, u32[]{:S(2)}, u32[]{:S(2)}) collective-permute-start(f32[104,128]{1,0:T(8,128)S(1)} %add_add_fusion.refs_0_), channel_id=1, source_target_pairs={{0,6},{1,7},{2,4},{3,5},{4,2},{5,3},{6,0},{7,1},{8,14},{9,15},{10,... | collective-permute-start | bytes 159752 | tf_op jit(solution)/shard_map/ppermute | solution.py:121
  (59 shorter events, 20.5 us)
Async XLA Ops:
  1.8 1.6 %collective-permute-start = (bf16[768,128]{1,0:T(8,128)(2,1)S(1)}, bf16[768,128]{1,0:T(8,128)(2,1)S(1)}, u32[]{:S(2)}, u32[]{:S(2)}) collective-permute-start(bf16[768,128]{1,0:T(8,128)(2,1)S(1)} %shard_map.131), channel_id=1, source_target_pairs={{0,1},{1,0},{2,3},{3,2},{4,5},{5,4},{6,7},{7,6},{8,9},{9,8},{10,11... | collective-permute-start | bytes 589832 | tf_op jit(solution)/shard_map/ppermute | solution.py:121
  3.5 30.0 %collective-permute-start.2 = (bf16[8,12,128,128]{3,2,1,0:T(8,128)(2,1)}, bf16[8,12,128,128]{3,2,1,0:T(8,128)(2,1)}, u32[]{:S(2)}, u32[]{:S(2)}) collective-permute-start(bf16[8,12,128,128]{3,2,1,0:T(8,128)(2,1)} %bitcast.8), channel_id=1, source_target_pairs={{0,1},{1,0},{2,3},{3,2},{4,5},{5,4},{6,7},{7,6},{8,9},{9,8},{10,11... | collective-permute-start | bytes 9437192 | tf_op jit(solution)/shard_map/ppermute | solution.py:121
  3.8 12.4 %collective-permute-start.6 = (bf16[1536,128]{1,0:T(8,128)(2,1)S(1)}, bf16[1536,128]{1,0:T(8,128)(2,1)S(1)}, u32[]{:S(2)}, u32[]{:S(2)}) collective-permute-start(bf16[1536,128]{1,0:T(8,128)(2,1)S(1)} %constant_dynamic-update-slice_fusion.after.rest_0_), channel_id=1, source_target_pairs={{0,8},{1,9},{2,10},{3,11},{4,12},{5,13},{6,14},{7,15},{8,0},{9,1},... | collective-permute-start | bytes 1179656 | tf_op jit(solution)/shard_map/TP1/ppermute | solution.py:121
  6.6 9.6 %collective-permute-start.4 = (bf16[1536,128]{1,0:T(8,128)(2,1)S(1)}, bf16[1536,128]{1,0:T(8,128)(2,1)S(1)}, u32[]{:S(2)}, u32[]{:S(2)}) collective-permute-start(bf16[1536,128]{1,0:T(8,128)(2,1)S(1)} %constant_dynamic-update-slice_fusion.after.rest_0_), channel_id=1, source_target_pairs={{0,4},{1,3},{2,6},{3,1},{4,0},{5,7},{6,2},{7,5},{8,12},{9,11},{10,... | collective-permute-start | bytes 1179656 | tf_op jit(solution)/shard_map/TvO/ppermute | solution.py:121
  9.5 9.0 %collective-permute-start.8 = (bf16[1536,128]{1,0:T(8,128)(2,1)}, bf16[1536,128]{1,0:T(8,128)(2,1)S(1)}, u32[]{:S(2)}, u32[]{:S(2)}) collective-permute-start(bf16[1536,128]{1,0:T(8,128)(2,1)} %copy-done), channel_id=1, source_target_pairs={{8,16},{9,17},{10,18},{11,19},{12,20},{13,21},{14,22},{15,23},{16,... | collective-permute-start | bytes 1179656 | tf_op jit(solution)/shard_map/TP2/ppermute | solution.py:121
  10.2 9.6 %collective-permute-start.3 = (bf16[1536,128]{1,0:T(8,128)(2,1)}, bf16[1536,128]{1,0:T(8,128)(2,1)S(1)}, u32[]{:S(2)}, u32[]{:S(2)}) collective-permute-start(bf16[1536,128]{1,0:T(8,128)(2,1)} %copy-done), channel_id=1, source_target_pairs={{0,2},{1,5},{2,0},{3,7},{4,6},{5,1},{6,4},{7,3},{8,10},{9,13},{10,... | collective-permute-start | bytes 1179656 | tf_op jit(solution)/shard_map/TuO/ppermute | solution.py:121
  16.2 10.5 %collective-permute-start.7 = (bf16[1536,128]{1,0:T(8,128)(2,1)S(1)}, bf16[1536,128]{1,0:T(8,128)(2,1)S(1)}, u32[]{:S(2)}, u32[]{:S(2)}) collective-permute-start(bf16[1536,128]{1,0:T(8,128)(2,1)S(1)} %collective-permute-done.6.rest_1_), channel_id=1, source_target_pairs={{0,2},{1,5},{2,0},{3,7},{4,6},{5,1},{6,4},{7,3},{8,10},{9,13},{10,... | collective-permute-start | bytes 1179656 | tf_op jit(solution)/shard_map/TuA/ppermute | solution.py:121
  18.5 14.9 %collective-permute-start.9 = (bf16[1536,128]{1,0:T(8,128)(2,1)S(1)}, bf16[1536,128]{1,0:T(8,128)(2,1)S(1)}, u32[]{:S(2)}, u32[]{:S(2)}) collective-permute-start(bf16[1536,128]{1,0:T(8,128)(2,1)S(1)} %collective-permute-done.8), channel_id=1, source_target_pairs={{8,0},{9,1},{10,2},{11,3},{12,4},{13,5},{14,6},{15,7},{16,24},{17,... | collective-permute-start | bytes 1179656 | tf_op jit(solution)/shard_map/TP3a/ppermute | solution.py:121
  19.8 13.8 %collective-permute-start.15 = (bf16[1536,128]{1,0:T(8,128)(2,1)S(1)}, bf16[1536,128]{1,0:T(8,128)(2,1)S(1)}, u32[]{:S(2)}, u32[]{:S(2)}) collective-permute-start(bf16[1536,128]{1,0:T(8,128)(2,1)S(1)} %collective-permute-done.6.rest_1_), channel_id=1, source_target_pairs={{8,16},{9,17},{10,18},{11,19},{12,20},{13,21},{14,22},{15,23},{16,... | collective-permute-start | bytes 1179656 | tf_op jit(solution)/shard_map/TP3b/ppermute | solution.py:121
  20.5 13.1 %collective-permute-start.5 = (bf16[1536,128]{1,0:T(8,128)(2,1)S(1)}, bf16[1536,128]{1,0:T(8,128)(2,1)S(1)}, u32[]{:S(2)}, u32[]{:S(2)}) collective-permute-start(bf16[1536,128]{1,0:T(8,128)(2,1)S(1)} %collective-permute-done.3.rest_1_), channel_id=1, source_target_pairs={{0,4},{1,3},{2,6},{3,1},{4,0},{5,7},{6,2},{7,5},{8,12},{9,11},{10,... | collective-permute-start | bytes 1179656 | tf_op jit(solution)/shard_map/TvuO/ppermute | solution.py:121
  26.7 16.6 %collective-permute-start.11 = (bf16[1536,128]{1,0:T(8,128)(2,1)S(1)}, bf16[1536,128]{1,0:T(8,128)(2,1)S(1)}, u32[]{:S(2)}, u32[]{:S(2)}) collective-permute-start(bf16[1536,128]{1,0:T(8,128)(2,1)S(1)} %collective-permute-done.6.rest_1_), channel_id=1, source_target_pairs={{0,4},{1,3},{2,6},{3,1},{4,0},{5,7},{6,2},{7,5},{8,12},{9,11},{10,... | collective-permute-start | bytes 1179656 | tf_op jit(solution)/shard_map/TvA/ppermute | solution.py:121
  33.5 11.1 %collective-permute-start.10 = (bf16[1536,128]{1,0:T(8,128)(2,1)S(1)}, bf16[1536,128]{1,0:T(8,128)(2,1)S(1)}, u32[]{:S(2)}, u32[]{:S(2)}) collective-permute-start(bf16[1536,128]{1,0:T(8,128)(2,1)S(1)} %broadcast_select_fusion.1.rest_1_), channel_id=1, source_target_pairs={{0,2},{1,5},{2,0},{3,7},{4,6},{5,1},{6,4},{7,3},{8,10},{9,13},{10,... | collective-permute-start | bytes 1179656 | tf_op jit(solution)/shard_map/TuB/ppermute | solution.py:121
  33.6 14.7 %collective-permute-start.16 = (bf16[1536,128]{1,0:T(8,128)(2,1)S(1)}, bf16[1536,128]{1,0:T(8,128)(2,1)S(1)}, u32[]{:S(2)}, u32[]{:S(2)}) collective-permute-start(bf16[1536,128]{1,0:T(8,128)(2,1)S(1)} %collective-permute-done.15), channel_id=1, source_target_pairs={{8,0},{9,1},{10,2},{11,3},{12,4},{13,5},{14,6},{15,7},{16,24},{17,... | collective-permute-start | bytes 1179656 | tf_op jit(solution)/shard_map/TP4/ppermute | solution.py:121
  34.9 2.9 %collective-permute-start.1 = (s32[16,128]{1,0:T(8,128)}, s32[16,128]{1,0:T(8,128)S(1)}, u32[]{:S(2)}, u32[]{:S(2)}) collective-permute-start(s32[16,128]{1,0:T(8,128)} %shard_map.132.own_table), channel_id=1, source_target_pairs={{0,1},{1,0},{2,3},{3,2},{4,5},{5,4},{6,7},{7,6},{8,9},{9,8},{10,11... | collective-permute-start | bytes 24584 | tf_op jit(solution)/shard_map/ppermute | solution.py:121
  43.3 7.8 %collective-permute-start.12 = (bf16[1536,128]{1,0:T(8,128)(2,1)S(1)}, bf16[1536,128]{1,0:T(8,128)(2,1)S(1)}, u32[]{:S(2)}, u32[]{:S(2)}) collective-permute-start(bf16[1536,128]{1,0:T(8,128)(2,1)S(1)} %broadcast_select_fusion.1.rest_1_), channel_id=1, source_target_pairs={{0,4},{1,3},{2,6},{3,1},{4,0},{5,7},{6,2},{7,5},{8,12},{9,11},{10,... | collective-permute-start | bytes 1179656 | tf_op jit(solution)/shard_map/TvB/ppermute | solution.py:121
  48.3 11.7 %collective-permute-start.17 = (bf16[1536,128]{1,0:T(8,128)(2,1)S(1)}, bf16[1536,128]{1,0:T(8,128)(2,1)S(1)}, u32[]{:S(2)}, u32[]{:S(2)}) collective-permute-start(bf16[1536,128]{1,0:T(8,128)(2,1)S(1)} %broadcast_select_fusion.rest_2_), channel_id=1, source_target_pairs={{0,2},{1,5},{2,0},{3,7},{4,6},{5,1},{6,4},{7,3},{8,10},{9,13},{10,... | collective-permute-start | bytes 1179656 | tf_op jit(solution)/shard_map/TuC/ppermute | solution.py:121
  51.1 9.8 %collective-permute-start.18 = (bf16[1536,128]{1,0:T(8,128)(2,1)S(1)}, bf16[1536,128]{1,0:T(8,128)(2,1)S(1)}, u32[]{:S(2)}, u32[]{:S(2)}) collective-permute-start(bf16[1536,128]{1,0:T(8,128)(2,1)S(1)} %broadcast_select_fusion.rest_2_), channel_id=1, source_target_pairs={{0,4},{1,3},{2,6},{3,1},{4,0},{5,7},{6,2},{7,5},{8,12},{9,11},{10,... | collective-permute-start | bytes 1179656 | tf_op jit(solution)/shard_map/TvC/ppermute | solution.py:121
  52.4 11.1 %collective-permute-start.13 = (bf16[1536,128]{1,0:T(8,128)(2,1)S(1)}, bf16[1536,128]{1,0:T(8,128)(2,1)S(1)}, u32[]{:S(2)}, u32[]{:S(2)}) collective-permute-start(bf16[1536,128]{1,0:T(8,128)(2,1)S(1)} %collective-permute-done.5.rest_0_), channel_id=1, source_target_pairs={{0,8},{1,9},{2,10},{3,11},{4,12},{5,13},{6,14},{7,15},{8,0},{9,1},... | collective-permute-start | bytes 1179656 | tf_op jit(solution)/shard_map/TvuA/ppermute | solution.py:121
  55.4 8.5 %collective-permute-start.14 = (bf16[1536,128]{1,0:T(8,128)(2,1)S(1)}, bf16[1536,128]{1,0:T(8,128)(2,1)S(1)}, u32[]{:S(2)}, u32[]{:S(2)}) collective-permute-start(bf16[1536,128]{1,0:T(8,128)(2,1)S(1)} %collective-permute-done.10.rest_3_), channel_id=1, source_target_pairs={{0,4},{1,3},{2,6},{3,1},{4,0},{5,7},{6,2},{7,5},{8,12},{9,11},{10,... | collective-permute-start | bytes 1179656 | tf_op jit(solution)/shard_map/TvuB/ppermute | solution.py:121
  60.0 8.2 %collective-permute-start.19 = (bf16[1536,128]{1,0:T(8,128)(2,1)S(1)}, bf16[1536,128]{1,0:T(8,128)(2,1)S(1)}, u32[]{:S(2)}, u32[]{:S(2)}) collective-permute-start(bf16[1536,128]{1,0:T(8,128)(2,1)S(1)} %collective-permute-done.17.rest_3_), channel_id=1, source_target_pairs={{0,4},{1,3},{2,6},{3,1},{4,0},{5,7},{6,2},{7,5},{8,12},{9,11},{10,... | collective-permute-start | bytes 1179656 | tf_op jit(solution)/shard_map/TvuC/ppermute | solution.py:121
  71.2 2.2 %collective-permute-start.20 = (bf16[2048,128]{1,0:T(8,128)(2,1)S(1)}, bf16[2048,128]{1,0:T(8,128)(2,1)S(1)}, u32[]{:S(2)}, u32[]{:S(2)}) collective-permute-start(bf16[2048,128]{1,0:T(8,128)(2,1)S(1)} %get-tuple-element.39.mine), channel_id=1, source_target_pairs={{0,1},{1,0},{2,3},{3,2},{4,5},{5,4},{6,7},{7,6},{8,9},{9,8},{10,11... | collective-permute-start | bytes 1572872 | tf_op jit(solution)/shard_map/ppermute | solution.py:121
  75.1 4.2 %collective-permute-start.21 = (f32[104,128]{1,0:T(8,128)S(1)}, f32[104,128]{1,0:T(8,128)S(1)}, u32[]{:S(2)}, u32[]{:S(2)}) collective-permute-start(f32[104,128]{1,0:T(8,128)S(1)} %get-tuple-element.41), channel_id=1, source_target_pairs={{0,2},{1,3},{2,0},{3,1},{4,6},{5,7},{6,4},{7,5},{8,10},{9,11},{10,... | collective-permute-start | bytes 159752 | tf_op jit(solution)/shard_map/ppermute | solution.py:121
  77.0 4.5 %collective-permute-start.22 = (f32[104,128]{1,0:T(8,128)S(1)}, f32[104,128]{1,0:T(8,128)S(1)}, u32[]{:S(2)}, u32[]{:S(2)}) collective-permute-start(f32[104,128]{1,0:T(8,128)S(1)} %get-tuple-element.42), channel_id=1, source_target_pairs={{0,4},{1,5},{2,6},{3,7},{4,0},{5,1},{6,2},{7,3},{8,12},{9,13},{10,... | collective-permute-start | bytes 159752 | tf_op jit(solution)/shard_map/ppermute | solution.py:121
  77.0 5.1 %collective-permute-start.23 = (f32[104,128]{1,0:T(8,128)S(1)}, f32[104,128]{1,0:T(8,128)S(1)}, u32[]{:S(2)}, u32[]{:S(2)}) collective-permute-start(f32[104,128]{1,0:T(8,128)S(1)} %get-tuple-element.43), channel_id=1, source_target_pairs={{0,6},{1,7},{2,4},{3,5},{4,2},{5,3},{6,0},{7,1},{8,14},{9,15},{10,... | collective-permute-start | bytes 159752 | tf_op jit(solution)/shard_map/ppermute | solution.py:121
  82.1 6.4 %collective-permute-start.24 = (f32[104,128]{1,0:T(8,128)S(1)}, f32[104,128]{1,0:T(8,128)S(1)}, u32[]{:S(2)}, u32[]{:S(2)}) collective-permute-start(f32[104,128]{1,0:T(8,128)S(1)} %add_add_fusion.1), channel_id=1, source_target_pairs={{0,8},{1,9},{2,10},{3,11},{4,12},{5,13},{6,14},{7,15},{8,0},{9,1},... | collective-permute-start | bytes 159752 | tf_op jit(solution)/shard_map/ppermute | solution.py:121
  85.0 5.7 %collective-permute-start.25 = (f32[104,128]{1,0:T(8,128)S(1)}, f32[104,128]{1,0:T(8,128)S(1)}, u32[]{:S(2)}, u32[]{:S(2)}) collective-permute-start(f32[104,128]{1,0:T(8,128)S(1)} %add_add_fusion.1), channel_id=1, source_target_pairs={{0,16},{1,17},{2,18},{3,19},{4,20},{5,21},{6,22},{7,23},{8,24},{9,... | collective-permute-start | bytes 159752 | tf_op jit(solution)/shard_map/ppermute | solution.py:121
  87.1 6.0 %collective-permute-start.26 = (f32[104,128]{1,0:T(8,128)S(1)}, f32[104,128]{1,0:T(8,128)S(1)}, u32[]{:S(2)}, u32[]{:S(2)}) collective-permute-start(f32[104,128]{1,0:T(8,128)S(1)} %add_add_fusion.1), channel_id=1, source_target_pairs={{0,24},{1,25},{2,26},{3,27},{4,28},{5,29},{6,30},{7,31},{8,16},{9,... | collective-permute-start | bytes 159752 | tf_op jit(solution)/shard_map/ppermute | solution.py:121
  93.2 4.2 %collective-permute-start.27 = (f32[104,128]{1,0:T(8,128)S(1)}, f32[104,128]{1,0:T(8,128)S(1)}, u32[]{:S(2)}, u32[]{:S(2)}) collective-permute-start(f32[104,128]{1,0:T(8,128)S(1)} %add_add_fusion.refs_0_), channel_id=1, source_target_pairs={{0,2},{1,3},{2,0},{3,1},{4,6},{5,7},{6,4},{7,5},{8,10},{9,11},{10,... | collective-permute-start | bytes 159752 | tf_op jit(solution)/shard_map/ppermute | solution.py:121
  93.4 4.1 %collective-permute-start.28 = (f32[104,128]{1,0:T(8,128)S(1)}, f32[104,128]{1,0:T(8,128)S(1)}, u32[]{:S(2)}, u32[]{:S(2)}) collective-permute-start(f32[104,128]{1,0:T(8,128)S(1)} %add_add_fusion.refs_0_), channel_id=1, source_target_pairs={{0,4},{1,5},{2,6},{3,7},{4,0},{5,1},{6,2},{7,3},{8,12},{9,13},{10,... | collective-permute-start | bytes 159752 | tf_op jit(solution)/shard_map/ppermute | solution.py:121
  93.8 5.0 %collective-permute-start.29 = (f32[104,128]{1,0:T(8,128)S(1)}, f32[104,128]{1,0:T(8,128)S(1)}, u32[]{:S(2)}, u32[]{:S(2)}) collective-permute-start(f32[104,128]{1,0:T(8,128)S(1)} %add_add_fusion.refs_0_), channel_id=1, source_target_pairs={{0,6},{1,7},{2,4},{3,5},{4,2},{5,3},{6,0},{7,1},{8,14},{9,15},{10,... | collective-permute-start | bytes 159752 | tf_op jit(solution)/shard_map/ppermute | solution.py:121
  96.7 2.1 %collective-permute-start.30 = (f32[104,128]{1,0:T(8,128)S(1)}, f32[104,128]{1,0:T(8,128)S(1)}, u32[]{:S(2)}, u32[]{:S(2)}) collective-permute-start(f32[104,128]{1,0:T(8,128)S(1)} %add_add_fusion.refs_0_), channel_id=1, source_target_pairs={{0,1},{1,0},{2,3},{3,2},{4,5},{5,4},{6,7},{7,6},{8,9},{9,8},{10,11... | collective-permute-start | bytes 159752 | tf_op jit(solution)/shard_map/ppermute | solution.py:121
  97.4 1.5 %collective-permute-start.31 = (f32[104,128]{1,0:T(8,128)S(1)}, f32[104,128]{1,0:T(8,128)S(1)}, u32[]{:S(2)}, u32[]{:S(2)}) collective-permute-start(f32[104,128]{1,0:T(8,128)S(1)} %collective-permute-done.27.refs_1_), channel_id=1, source_target_pairs={{0,1},{1,0},{2,3},{3,2},{4,5},{5,4},{6,7},{7,6},{8,9},{9,8},{10,11... | collective-permute-start | bytes 159752 | tf_op jit(solution)/shard_map/ppermute | solution.py:121
  (6 other events, 46.0 us)

commit v4 on v3

--- a/solution.py
+++ b/solution.py
@@ -202,7 +202,7 @@
     return (d >> 3) ^ core, d & 7
 
 
-UNROLL = 4
+UNROLL = 6
 FLOPS = 300000000
 
 
@@ -434,15 +434,15 @@
     two_b = named("TvB", second_way, slot_b, one_a, two_a, first_acc)
     (acc,) = products("TK1", first_acc, [((1, 1, 0), both_o), ((0, 0, 1), slot_a), ((1, 0, 1), one_a), ((1, 0, 2), one_b)])
     slot_c = named("TP4", z_outward, far, both_o, one_a)
-    slot_c = jnp.where(middle, lax.optimization_barrier((far, acc))[0], slot_c)
+    slot_c = jnp.where(middle, lax.optimization_barrier((far, first_acc))[0], slot_c)
     both_b = named("TvuB", second_way, one_b)
-    both_a = named("TvuA", z_pairs, both_o, two_b)
+    both_a = named("TvuA", z_pairs, both_o, slot_c)
     one_c = named("TuC", first_way, slot_c)
-    two_c = named("TvC", second_way, slot_c, two_b)
+    two_c = named("TvC", second_way, slot_c, two_b, acc)
     (acc,) = products("TK2", acc, [((0, 1, 1), two_a), ((0, 0, 2), slot_b), ((0, 1, 2), two_b)])
     both_c = named("TvuC", second_way, one_c, acc)
-    (acc,) = products("TK3", acc, [((1, 1, 1), both_a), ((1, 1, 2), both_b), ((0, 0, 3), slot_c), ((1, 0, 3), one_c), ((0, 1, 3), two_c)], True)
-    _, summed = products("TK4", acc, [((1, 1, 3), both_c)], True)
+    (acc,) = products("TK3", acc, [((1, 1, 2), both_b), ((0, 0, 3), slot_c), ((1, 0, 3), one_c), ((0, 1, 3), two_c)], True)
+    _, summed = products("TK4", acc, [((1, 1, 1), both_a), ((1, 1, 3), both_c)], True)
     from_sibling = in_vmem(to_sibling(summed))
 
     side = hid // 2

time: 102 us -> 101 us (level)
  waiting for transfers between devices: 33.9 us -> 40 us
  starting transfers between devices: 41.3 us -> 35.7 us
    ppermute x34, waiting for transfers between devices: 33.9 us -> 40 us  [send(): return lax.ppermute(value, ('blk', 'rep'), pairs)]
    ppermute x34, starting transfers between devices: 41.3 us -> 35.7 us  [send(): return lax.ppermute(value, ('blk', 'rep'), pairs)]
  transfers between devices with their start and end apart: 34 -> 34, of which waited for: 20 -> 19; matrix products, arithmetic and copies ran while one was open for 0% -> 0% of each run, Pallas kernels for 16% -> 15%
where the time goes in v4:
time: 101 us
  waiting for transfers between devices  40 us (40%)
  starting transfers between devices  35.7 us (35%)
  Pallas kernels  22.2 us (22%)
  local copies, waits for them, and re-layouts  1.73 us (2%)
    ppermute x34, waiting for transfers between devices, send(): return lax.ppermute(value, ('blk', 'rep'), pairs)  40 us
    ppermute x34, starting transfers between devices, send(): return lax.ppermute(value, ('blk', 'rep'), pairs)  35.7 us
    pallas_call x5, Pallas kernels, gather_call(): pl.pallas_call(functools.partial(gather_kernel, kinds, near), out_shape=o...  16.2 us
    pallas_call x2, Pallas kernels, pack_call(): pl.pallas_call(functools.partial(pack_kernel, away), out_shape=pltpu.VMEM...  2.25 us
  transfers between devices with their start and end apart: 34, of which 19 were waited for; matrix products, arithmetic and copies ran while one was open for 0% of the time, Pallas kernels for 15%

profile of v4, /device:TPU:0, one launch (start us, length us, event | category | flops | bytes accessed | tf_op | source)
XLA Modules:
  0.0 100.7 jit_solution(1330262098687382939)
XLA Ops:
  3.8 2.8 %collective-permute-start.6 = (bf16[1536,128]{1,0:T(8,128)(2,1)S(1)}, bf16[1536,128]{1,0:T(8,128)(2,1)S(1)}, u32[]{:S(2)}, u32[]{:S(2)}) collective-permute-start(bf16[1536,128]{1,0:T(8,128)(2,1)S(1)} %constant_dynamic-update-slice_fusion.after.rest_0_), channel_id=1, source_target_pairs={{0,8},{1,9},{2,10},{3,11},{4,12},{5,13},{6,14},{7,15},{8,0},{9,1},... | collective-permute-start | bytes 1179656 | tf_op jit(solution)/shard_map/TP1/ppermute | solution.py:121
  6.6 1.5 %collective-permute-start.4 = (bf16[1536,128]{1,0:T(8,128)(2,1)S(1)}, bf16[1536,128]{1,0:T(8,128)(2,1)S(1)}, u32[]{:S(2)}, u32[]{:S(2)}) collective-permute-start(bf16[1536,128]{1,0:T(8,128)(2,1)S(1)} %constant_dynamic-update-slice_fusion.after.rest_0_), channel_id=1, source_target_pairs={{0,4},{1,3},{2,6},{3,1},{4,0},{5,7},{6,2},{7,5},{8,12},{9,11},{10,... | collective-permute-start | bytes 1179656 | tf_op jit(solution)/shard_map/TvO/ppermute | solution.py:121
  8.1 1.5 %collective-permute-start.3 = (bf16[1536,128]{1,0:T(8,128)(2,1)S(1)}, bf16[1536,128]{1,0:T(8,128)(2,1)S(1)}, u32[]{:S(2)}, u32[]{:S(2)}) collective-permute-start(bf16[1536,128]{1,0:T(8,128)(2,1)S(1)} %constant_dynamic-update-slice_fusion.after.rest_0_), channel_id=1, source_target_pairs={{0,2},{1,5},{2,0},{3,7},{4,6},{5,1},{6,4},{7,3},{8,10},{9,13},{10,... | collective-permute-start | bytes 1179656 | tf_op jit(solution)/shard_map/TuO/ppermute | solution.py:121
  11.6 4.6 %collective-permute-done.6.rest_1_ = bf16[1536,128]{1,0:T(8,128)(2,1)S(1)} collective-permute-done((bf16[1536,128]{1,0:T(8,128)(2,1)S(1)}, bf16[1536,128]{1,0:T(8,128)(2,1)S(1)}, u32[]{:S(2)}, u32[]{:S(2)}) %collective-permute-start.6) | collective-permute-done | bytes 393248 | tf_op jit(solution)/shard_map/TP1/ppermute | solution.py:121
  16.2 2.2 %collective-permute-done.4.rest_2_ = bf16[1536,128]{1,0:T(8,128)(2,1)S(1)} collective-permute-done((bf16[1536,128]{1,0:T(8,128)(2,1)S(1)}, bf16[1536,128]{1,0:T(8,128)(2,1)S(1)}, u32[]{:S(2)}, u32[]{:S(2)}) %collective-permute-start.4) | collective-permute-done | bytes 393248 | tf_op jit(solution)/shard_map/TvO/ppermute | solution.py:121
  20.1 1.6 %collective-permute-start.5 = (bf16[1536,128]{1,0:T(8,128)(2,1)S(1)}, bf16[1536,128]{1,0:T(8,128)(2,1)S(1)}, u32[]{:S(2)}, u32[]{:S(2)}) collective-permute-start(bf16[1536,128]{1,0:T(8,128)(2,1)S(1)} %collective-permute-done.3.rest_1_), channel_id=1, source_target_pairs={{0,4},{1,3},{2,6},{3,1},{4,0},{5,7},{6,2},{7,5},{8,12},{9,11},{10,... | collective-permute-start | bytes 1179656 | tf_op jit(solution)/shard_map/TvuO/ppermute | solution.py:121
  23.0 7.2 %collective-permute-done.7.rest_2_ = bf16[1536,128]{1,0:T(8,128)(2,1)S(1)} collective-permute-done((bf16[1536,128]{1,0:T(8,128)(2,1)S(1)}, bf16[1536,128]{1,0:T(8,128)(2,1)S(1)}, u32[]{:S(2)}, u32[]{:S(2)}) %collective-permute-start.7) | collective-permute-done | bytes 393248 | tf_op jit(solution)/shard_map/TuA/ppermute | solution.py:121
  30.2 1.5 %collective-permute-start.11 = (bf16[1536,128]{1,0:T(8,128)(2,1)S(1)}, bf16[1536,128]{1,0:T(8,128)(2,1)S(1)}, u32[]{:S(2)}, u32[]{:S(2)}) collective-permute-start(bf16[1536,128]{1,0:T(8,128)(2,1)S(1)} %collective-permute-done.6.rest_1_), channel_id=1, source_target_pairs={{0,4},{1,3},{2,6},{3,1},{4,0},{5,7},{6,2},{7,5},{8,12},{9,11},{10,... | collective-permute-start | bytes 1179656 | tf_op jit(solution)/shard_map/TvA/ppermute | solution.py:121
  34.4 1.6 %collective-permute-start.10 = (bf16[1536,128]{1,0:T(8,128)(2,1)S(1)}, bf16[1536,128]{1,0:T(8,128)(2,1)S(1)}, u32[]{:S(2)}, u32[]{:S(2)}) collective-permute-start(bf16[1536,128]{1,0:T(8,128)(2,1)S(1)} %broadcast_select_fusion.1.rest_1_), channel_id=1, source_target_pairs={{0,2},{1,5},{2,0},{3,7},{4,6},{5,1},{6,4},{7,3},{8,10},{9,13},{10,... | collective-permute-start | bytes 1179656 | tf_op jit(solution)/shard_map/TuB/ppermute | solution.py:121
  37.7 3.5 %TK0.1.start = f32[3,9,128,128]{3,2,1,0:T(8,128)S(1)} custom-call(s32[16,128]{1,0:T(8,128)S(1)} %copy-done.2, s32[16,128]{1,0:T(8,128)S(1)} %collective-permute-done.1.other_table, f32[8,128]{1,0:T(8,128)S(1)} %bitcast.7, bf16[8,12,128,128]{3,2,1,0:T(8,128)(2,1)} %bitcast.9, bf16[8,12,128,128]{3,2,1,0:T(8,128)(2,1)} %collective-permute-done.2.other, ...), custom_call_target="tpu_custom_call" | custom-call | flops 900000000 | bytes 2400000 | tf_op jit(solution)/shard_map/TK0/pallas_call | solution.py:303
  41.2 1.9 %collective-permute-start.12 = (bf16[1536,128]{1,0:T(8,128)(2,1)S(1)}, bf16[1536,128]{1,0:T(8,128)(2,1)S(1)}, u32[]{:S(2)}, u32[]{:S(2)}) collective-permute-start(bf16[1536,128]{1,0:T(8,128)(2,1)S(1)} %broadcast_select_fusion.1.rest_1_), channel_id=1, source_target_pairs={{0,4},{1,3},{2,6},{3,1},{4,0},{5,7},{6,2},{7,5},{8,12},{9,11},{10,... | collective-permute-start | bytes 1179656 | tf_op jit(solution)/shard_map/TvB/ppermute | solution.py:121
  43.9 1.6 %collective-permute-start.16 = (bf16[1536,128]{1,0:T(8,128)(2,1)S(1)}, bf16[1536,128]{1,0:T(8,128)(2,1)S(1)}, u32[]{:S(2)}, u32[]{:S(2)}) collective-permute-start(bf16[1536,128]{1,0:T(8,128)(2,1)S(1)} %broadcast_select_fusion.rest_1_), channel_id=1, source_target_pairs={{0,2},{1,5},{2,0},{3,7},{4,6},{5,1},{6,4},{7,3},{8,10},{9,13},{10,... | collective-permute-start | bytes 1179656 | tf_op jit(solution)/shard_map/TuC/ppermute | solution.py:121
  45.5 3.2 %TK1.1.start = f32[3,9,128,128]{3,2,1,0:T(8,128)S(1)} custom-call(s32[16,128]{1,0:T(8,128)S(1)} %copy-done.2, s32[16,128]{1,0:T(8,128)S(1)} %collective-permute-done.1.other_table, f32[3,9,128,128]{3,2,1,0:T(8,128)S(1)} %TK0.1.start, bf16[8,12,128,128]{3,2,1,0:T(8,128)(2,1)} %bitcast.10, ...), custom_call_target="tpu_custom_call", output_to_operand_aliasing={{}: (2, {})} | custom-call | flops 1200000000 | bytes 3200000 | tf_op jit(solution)/shard_map/TK1/pallas_call | solution.py:303
  48.8 4.3 %collective-permute-done.12.rest_2_ = bf16[1536,128]{1,0:T(8,128)(2,1)S(1)} collective-permute-done((bf16[1536,128]{1,0:T(8,128)(2,1)S(1)}, bf16[1536,128]{1,0:T(8,128)(2,1)S(1)}, u32[]{:S(2)}, u32[]{:S(2)}) %collective-permute-start.12) | collective-permute-done | bytes 393248 | tf_op jit(solution)/shard_map/TvB/ppermute | solution.py:121
  53.1 1.9 %collective-permute-start.17 = (bf16[1536,128]{1,0:T(8,128)(2,1)S(1)}, bf16[1536,128]{1,0:T(8,128)(2,1)S(1)}, u32[]{:S(2)}, u32[]{:S(2)}) collective-permute-start(bf16[1536,128]{1,0:T(8,128)(2,1)S(1)} %broadcast_select_fusion.rest_1_), channel_id=1, source_target_pairs={{0,4},{1,3},{2,6},{3,1},{4,0},{5,7},{6,2},{7,5},{8,12},{9,11},{10,... | collective-permute-start | bytes 1179656 | tf_op jit(solution)/shard_map/TvC/ppermute | solution.py:121
  55.8 2.8 %TK2.1.start = f32[3,9,128,128]{3,2,1,0:T(8,128)S(1)} custom-call(s32[16,128]{1,0:T(8,128)S(1)} %copy-done.2, s32[16,128]{1,0:T(8,128)S(1)} %collective-permute-done.1.other_table, f32[3,9,128,128]{3,2,1,0:T(8,128)S(1)} %TK1.1.start, bf16[8,12,128,128]{3,2,1,0:T(8,128)(2,1)} %bitcast.11, ...), custom_call_target="tpu_custom_call", output_to_operand_aliasing={{}: (2, {})} | custom-call | flops 900000000 | bytes 2400000 | tf_op jit(solution)/shard_map/TK2/pallas_call | solution.py:303
  58.7 1.6 %collective-permute-start.19 = (bf16[1536,128]{1,0:T(8,128)(2,1)S(1)}, bf16[1536,128]{1,0:T(8,128)(2,1)S(1)}, u32[]{:S(2)}, u32[]{:S(2)}) collective-permute-start(bf16[1536,128]{1,0:T(8,128)(2,1)S(1)} %collective-permute-done.16.rest_2_), channel_id=1, source_target_pairs={{0,4},{1,3},{2,6},{3,1},{4,0},{5,7},{6,2},{7,5},{8,12},{9,11},{10,... | collective-permute-start | bytes 1179656 | tf_op jit(solution)/shard_map/TvuC/ppermute | solution.py:121
  60.9 4.2 %collective-permute-done.13.rest_0_ = bf16[1536,128]{1,0:T(8,128)(2,1)S(1)} collective-permute-done((bf16[1536,128]{1,0:T(8,128)(2,1)S(1)}, bf16[1536,128]{1,0:T(8,128)(2,1)S(1)}, u32[]{:S(2)}, u32[]{:S(2)}) %collective-permute-start.13) | collective-permute-done | bytes 393248 | tf_op jit(solution)/shard_map/TvuB/ppermute | solution.py:121
  65.1 3.4 %TK3.1.start = f32[3,9,128,128]{3,2,1,0:T(8,128)S(1)} custom-call(s32[16,128]{1,0:T(8,128)S(1)} %copy-done.2, s32[16,128]{1,0:T(8,128)S(1)} %collective-permute-done.1.other_table, f32[3,9,128,128]{3,2,1,0:T(8,128)S(1)} %TK2.1.start, bf16[8,12,128,128]{3,2,1,0:T(8,128)(2,1)} %bitcast.12, ...), custom_call_target="tpu_custom_call", output_to_operand_aliasing={{}: (2, {})} | custom-call | flops 1200000000 | bytes 3200000 | tf_op jit(solution)/shard_map/TK3/pallas_call | solution.py:303
  69.3 3.3 %TK4.1 = (f32[3,9,128,128]{3,2,1,0:T(8,128)S(1)}, bf16[2048,128]{1,0:T(8,128)(2,1)S(1)}) custom-call(s32[16,128]{1,0:T(8,128)S(1)} %copy-done.2, s32[16,128]{1,0:T(8,128)S(1)} %collective-permute-done.1.other_table, f32[3,9,128,128]{3,2,1,0:T(8,128)S(1)} %TK3.1.start, bf16[8,12,128,128]{3,2,1,0:T(8,128)(2,1)} %bitcast.13, ...), custom_call_target="tpu_custom_call", output_to_operand_aliasing={{0}: (2, {})} | custom-call | flops 600000000 | bytes 1600000 | tf_op jit(solution)/shard_map/TK4/pallas_call | solution.py:303
  72.7 1.9 %collective-permute-done.20.theirs = bf16[2048,128]{1,0:T(8,128)(2,1)S(1)} collective-permute-done((bf16[2048,128]{1,0:T(8,128)(2,1)S(1)}, bf16[2048,128]{1,0:T(8,128)(2,1)S(1)}, u32[]{:S(2)}, u32[]{:S(2)}) %collective-permute-start.20) | collective-permute-done | bytes 524320 | tf_op jit(solution)/shard_map/ppermute | solution.py:121
  74.6 1.6 %shard_map.133 = (f32[104,128]{1,0:T(8,128)S(1)}, f32[104,128]{1,0:T(8,128)S(1)}, f32[104,128]{1,0:T(8,128)S(1)}, f32[104,128]{1,0:T(8,128)S(1)}) custom-call(bf16[2048,128]{1,0:T(8,128)(2,1)S(1)} %get-tuple-element.39.mine, bf16[2048,128]{1,0:T(8,128)(2,1)S(1)} %collective-permute-done.20.theirs, bf16[128,256]{1,0:T(8,128)(2,1)} %w_first.1, ...), custom_call_target="tpu_custom_call" | custom-call | tf_op jit(solution)/shard_map/pallas_call | solution.py:449
  76.3 1.9 %collective-permute-start.22 = (f32[104,128]{1,0:T(8,128)S(1)}, f32[104,128]{1,0:T(8,128)S(1)}, u32[]{:S(2)}, u32[]{:S(2)}) collective-permute-start(f32[104,128]{1,0:T(8,128)S(1)} %get-tuple-element.42), channel_id=1, source_target_pairs={{0,4},{1,5},{2,6},{3,7},{4,0},{5,1},{6,2},{7,3},{8,12},{9,13},{10,... | collective-permute-start | bytes 159752 | tf_op jit(solution)/shard_map/ppermute | solution.py:121
  78.2 1.6 %collective-permute-start.23 = (f32[104,128]{1,0:T(8,128)S(1)}, f32[104,128]{1,0:T(8,128)S(1)}, u32[]{:S(2)}, u32[]{:S(2)}) collective-permute-start(f32[104,128]{1,0:T(8,128)S(1)} %get-tuple-element.43), channel_id=1, source_target_pairs={{0,6},{1,7},{2,4},{3,5},{4,2},{5,3},{6,0},{7,1},{8,14},{9,15},{10,... | collective-permute-start | bytes 159752 | tf_op jit(solution)/shard_map/ppermute | solution.py:121
  80.5 2.8 %collective-permute-done.23 = f32[104,128]{1,0:T(8,128)S(1)} collective-permute-done((f32[104,128]{1,0:T(8,128)S(1)}, f32[104,128]{1,0:T(8,128)S(1)}, u32[]{:S(2)}, u32[]{:S(2)}) %collective-permute-start.23) | collective-permute-done | bytes 53280 | tf_op jit(solution)/shard_map/ppermute | solution.py:121
  84.0 1.6 %collective-permute-start.25 = (f32[104,128]{1,0:T(8,128)S(1)}, f32[104,128]{1,0:T(8,128)S(1)}, u32[]{:S(2)}, u32[]{:S(2)}) collective-permute-start(f32[104,128]{1,0:T(8,128)S(1)} %add_add_fusion.1), channel_id=1, source_target_pairs={{0,16},{1,17},{2,18},{3,19},{4,20},{5,21},{6,22},{7,23},{8,24},{9,... | collective-permute-start | bytes 159752 | tf_op jit(solution)/shard_map/ppermute | solution.py:121
  85.6 2.1 %collective-permute-start.26 = (f32[104,128]{1,0:T(8,128)S(1)}, f32[104,128]{1,0:T(8,128)S(1)}, u32[]{:S(2)}, u32[]{:S(2)}) collective-permute-start(f32[104,128]{1,0:T(8,128)S(1)} %add_add_fusion.1), channel_id=1, source_target_pairs={{0,24},{1,25},{2,26},{3,27},{4,28},{5,29},{6,30},{7,31},{8,16},{9,... | collective-permute-start | bytes 159752 | tf_op jit(solution)/shard_map/ppermute | solution.py:121
  87.7 1.7 %collective-permute-done.25 = f32[104,128]{1,0:T(8,128)S(1)} collective-permute-done((f32[104,128]{1,0:T(8,128)S(1)}, f32[104,128]{1,0:T(8,128)S(1)}, u32[]{:S(2)}, u32[]{:S(2)}) %collective-permute-start.25) | collective-permute-done | bytes 53280 | tf_op jit(solution)/shard_map/ppermute | solution.py:121
  89.4 2.3 %collective-permute-done.26 = f32[104,128]{1,0:T(8,128)S(1)} collective-permute-done((f32[104,128]{1,0:T(8,128)S(1)}, f32[104,128]{1,0:T(8,128)S(1)}, u32[]{:S(2)}, u32[]{:S(2)}) %collective-permute-start.26) | collective-permute-done | bytes 53280 | tf_op jit(solution)/shard_map/ppermute | solution.py:121
  91.7 1.6 %collective-permute-start.27 = (f32[104,128]{1,0:T(8,128)S(1)}, f32[104,128]{1,0:T(8,128)S(1)}, u32[]{:S(2)}, u32[]{:S(2)}) collective-permute-start(f32[104,128]{1,0:T(8,128)S(1)} %add_add_fusion.refs_0_), channel_id=1, source_target_pairs={{0,2},{1,3},{2,0},{3,1},{4,6},{5,7},{6,4},{7,5},{8,10},{9,11},{10,... | collective-permute-start | bytes 159752 | tf_op jit(solution)/shard_map/ppermute | solution.py:121
  93.6 1.6 %collective-permute-start.29 = (f32[104,128]{1,0:T(8,128)S(1)}, f32[104,128]{1,0:T(8,128)S(1)}, u32[]{:S(2)}, u32[]{:S(2)}) collective-permute-start(f32[104,128]{1,0:T(8,128)S(1)} %add_add_fusion.refs_0_), channel_id=1, source_target_pairs={{0,6},{1,7},{2,4},{3,5},{4,2},{5,3},{6,0},{7,1},{8,14},{9,15},{10,... | collective-permute-start | bytes 159752 | tf_op jit(solution)/shard_map/ppermute | solution.py:121
  95.9 1.6 %collective-permute-done.28.refs_2_ = f32[104,128]{1,0:T(8,128)S(1)} collective-permute-done((f32[104,128]{1,0:T(8,128)S(1)}, f32[104,128]{1,0:T(8,128)S(1)}, u32[]{:S(2)}, u32[]{:S(2)}) %collective-permute-start.28) | collective-permute-done | bytes 53280 | tf_op jit(solution)/shard_map/ppermute | solution.py:121
  (59 shorter events, 21.4 us)
Async XLA Ops:
  1.8 1.6 %collective-permute-start = (bf16[768,128]{1,0:T(8,128)(2,1)S(1)}, bf16[768,128]{1,0:T(8,128)(2,1)S(1)}, u32[]{:S(2)}, u32[]{:S(2)}) collective-permute-start(bf16[768,128]{1,0:T(8,128)(2,1)S(1)} %shard_map.131), channel_id=1, source_target_pairs={{0,1},{1,0},{2,3},{3,2},{4,5},{5,4},{6,7},{7,6},{8,9},{9,8},{10,11... | collective-permute-start | bytes 589832 | tf_op jit(solution)/shard_map/ppermute | solution.py:121
  3.5 30.9 %collective-permute-start.2 = (bf16[8,12,128,128]{3,2,1,0:T(8,128)(2,1)}, bf16[8,12,128,128]{3,2,1,0:T(8,128)(2,1)}, u32[]{:S(2)}, u32[]{:S(2)}) collective-permute-start(bf16[8,12,128,128]{3,2,1,0:T(8,128)(2,1)} %bitcast.8), channel_id=1, source_target_pairs={{0,1},{1,0},{2,3},{3,2},{4,5},{5,4},{6,7},{7,6},{8,9},{9,8},{10,11... | collective-permute-start | bytes 9437192 | tf_op jit(solution)/shard_map/ppermute | solution.py:121
  3.8 12.4 %collective-permute-start.6 = (bf16[1536,128]{1,0:T(8,128)(2,1)S(1)}, bf16[1536,128]{1,0:T(8,128)(2,1)S(1)}, u32[]{:S(2)}, u32[]{:S(2)}) collective-permute-start(bf16[1536,128]{1,0:T(8,128)(2,1)S(1)} %constant_dynamic-update-slice_fusion.after.rest_0_), channel_id=1, source_target_pairs={{0,8},{1,9},{2,10},{3,11},{4,12},{5,13},{6,14},{7,15},{8,0},{9,1},... | collective-permute-start | bytes 1179656 | tf_op jit(solution)/shard_map/TP1/ppermute | solution.py:121
  6.6 11.7 %collective-permute-start.4 = (bf16[1536,128]{1,0:T(8,128)(2,1)S(1)}, bf16[1536,128]{1,0:T(8,128)(2,1)S(1)}, u32[]{:S(2)}, u32[]{:S(2)}) collective-permute-start(bf16[1536,128]{1,0:T(8,128)(2,1)S(1)} %constant_dynamic-update-slice_fusion.after.rest_0_), channel_id=1, source_target_pairs={{0,4},{1,3},{2,6},{3,1},{4,0},{5,7},{6,2},{7,5},{8,12},{9,11},{10,... | collective-permute-start | bytes 1179656 | tf_op jit(solution)/shard_map/TvO/ppermute | solution.py:121
  8.1 11.3 %collective-permute-start.3 = (bf16[1536,128]{1,0:T(8,128)(2,1)S(1)}, bf16[1536,128]{1,0:T(8,128)(2,1)S(1)}, u32[]{:S(2)}, u32[]{:S(2)}) collective-permute-start(bf16[1536,128]{1,0:T(8,128)(2,1)S(1)} %constant_dynamic-update-slice_fusion.after.rest_0_), channel_id=1, source_target_pairs={{0,2},{1,5},{2,0},{3,7},{4,6},{5,1},{6,4},{7,3},{8,10},{9,13},{10,... | collective-permute-start | bytes 1179656 | tf_op jit(solution)/shard_map/TuO/ppermute | solution.py:121
  11.0 10.7 %collective-permute-start.8 = (bf16[1536,128]{1,0:T(8,128)(2,1)}, bf16[1536,128]{1,0:T(8,128)(2,1)S(1)}, u32[]{:S(2)}, u32[]{:S(2)}) collective-permute-start(bf16[1536,128]{1,0:T(8,128)(2,1)} %copy-done), channel_id=1, source_target_pairs={{8,16},{9,17},{10,18},{11,19},{12,20},{13,21},{14,22},{15,23},{16,... | collective-permute-start | bytes 1179656 | tf_op jit(solution)/shard_map/TP2/ppermute | solution.py:121
  18.4 11.9 %collective-permute-start.7 = (bf16[1536,128]{1,0:T(8,128)(2,1)S(1)}, bf16[1536,128]{1,0:T(8,128)(2,1)S(1)}, u32[]{:S(2)}, u32[]{:S(2)}) collective-permute-start(bf16[1536,128]{1,0:T(8,128)(2,1)S(1)} %collective-permute-done.6.rest_1_), channel_id=1, source_target_pairs={{0,2},{1,5},{2,0},{3,7},{4,6},{5,1},{6,4},{7,3},{8,10},{9,13},{10,... | collective-permute-start | bytes 1179656 | tf_op jit(solution)/shard_map/TuA/ppermute | solution.py:121
  19.4 10.8 %collective-permute-start.14 = (bf16[1536,128]{1,0:T(8,128)(2,1)S(1)}, bf16[1536,128]{1,0:T(8,128)(2,1)S(1)}, u32[]{:S(2)}, u32[]{:S(2)}) collective-permute-start(bf16[1536,128]{1,0:T(8,128)(2,1)S(1)} %collective-permute-done.6.rest_1_), channel_id=1, source_target_pairs={{8,16},{9,17},{10,18},{11,19},{12,20},{13,21},{14,22},{15,23},{16,... | collective-permute-start | bytes 1179656 | tf_op jit(solution)/shard_map/TP3b/ppermute | solution.py:121
  20.1 11.7 %collective-permute-start.5 = (bf16[1536,128]{1,0:T(8,128)(2,1)S(1)}, bf16[1536,128]{1,0:T(8,128)(2,1)S(1)}, u32[]{:S(2)}, u32[]{:S(2)}) collective-permute-start(bf16[1536,128]{1,0:T(8,128)(2,1)S(1)} %collective-permute-done.3.rest_1_), channel_id=1, source_target_pairs={{0,4},{1,3},{2,6},{3,1},{4,0},{5,7},{6,2},{7,5},{8,12},{9,11},{10,... | collective-permute-start | bytes 1179656 | tf_op jit(solution)/shard_map/TvuO/ppermute | solution.py:121
  21.7 12.7 %collective-permute-start.9 = (bf16[1536,128]{1,0:T(8,128)(2,1)S(1)}, bf16[1536,128]{1,0:T(8,128)(2,1)S(1)}, u32[]{:S(2)}, u32[]{:S(2)}) collective-permute-start(bf16[1536,128]{1,0:T(8,128)(2,1)S(1)} %collective-permute-done.8), channel_id=1, source_target_pairs={{8,0},{9,1},{10,2},{11,3},{12,4},{13,5},{14,6},{15,7},{16,24},{17,... | collective-permute-start | bytes 1179656 | tf_op jit(solution)/shard_map/TP3a/ppermute | solution.py:121
  30.2 5.8 %collective-permute-start.1 = (s32[16,128]{1,0:T(8,128)}, s32[16,128]{1,0:T(8,128)S(1)}, u32[]{:S(2)}, u32[]{:S(2)}) collective-permute-start(s32[16,128]{1,0:T(8,128)} %shard_map.132.own_table), channel_id=1, source_target_pairs={{0,1},{1,0},{2,3},{3,2},{4,5},{5,4},{6,7},{7,6},{8,9},{9,8},{10,11... | collective-permute-start | bytes 24584 | tf_op jit(solution)/shard_map/ppermute | solution.py:121
  30.2 11.0 %collective-permute-start.11 = (bf16[1536,128]{1,0:T(8,128)(2,1)S(1)}, bf16[1536,128]{1,0:T(8,128)(2,1)S(1)}, u32[]{:S(2)}, u32[]{:S(2)}) collective-permute-start(bf16[1536,128]{1,0:T(8,128)(2,1)S(1)} %collective-permute-done.6.rest_1_), channel_id=1, source_target_pairs={{0,4},{1,3},{2,6},{3,1},{4,0},{5,7},{6,2},{7,5},{8,12},{9,11},{10,... | collective-permute-start | bytes 1179656 | tf_op jit(solution)/shard_map/TvA/ppermute | solution.py:121
  31.8 12.1 %collective-permute-start.15 = (bf16[1536,128]{1,0:T(8,128)(2,1)S(1)}, bf16[1536,128]{1,0:T(8,128)(2,1)S(1)}, u32[]{:S(2)}, u32[]{:S(2)}) collective-permute-start(bf16[1536,128]{1,0:T(8,128)(2,1)S(1)} %collective-permute-done.14), channel_id=1, source_target_pairs={{8,0},{9,1},{10,2},{11,3},{12,4},{13,5},{14,6},{15,7},{16,24},{17,... | collective-permute-start | bytes 1179656 | tf_op jit(solution)/shard_map/TP4/ppermute | solution.py:121
  34.4 11.1 %collective-permute-start.10 = (bf16[1536,128]{1,0:T(8,128)(2,1)S(1)}, bf16[1536,128]{1,0:T(8,128)(2,1)S(1)}, u32[]{:S(2)}, u32[]{:S(2)}) collective-permute-start(bf16[1536,128]{1,0:T(8,128)(2,1)S(1)} %broadcast_select_fusion.1.rest_1_), channel_id=1, source_target_pairs={{0,2},{1,5},{2,0},{3,7},{4,6},{5,1},{6,4},{7,3},{8,10},{9,13},{10,... | collective-permute-start | bytes 1179656 | tf_op jit(solution)/shard_map/TuB/ppermute | solution.py:121
  41.2 11.9 %collective-permute-start.12 = (bf16[1536,128]{1,0:T(8,128)(2,1)S(1)}, bf16[1536,128]{1,0:T(8,128)(2,1)S(1)}, u32[]{:S(2)}, u32[]{:S(2)}) collective-permute-start(bf16[1536,128]{1,0:T(8,128)(2,1)S(1)} %broadcast_select_fusion.1.rest_1_), channel_id=1, source_target_pairs={{0,4},{1,3},{2,6},{3,1},{4,0},{5,7},{6,2},{7,5},{8,12},{9,11},{10,... | collective-permute-start | bytes 1179656 | tf_op jit(solution)/shard_map/TvB/ppermute | solution.py:121
  43.9 14.7 %collective-permute-start.16 = (bf16[1536,128]{1,0:T(8,128)(2,1)S(1)}, bf16[1536,128]{1,0:T(8,128)(2,1)S(1)}, u32[]{:S(2)}, u32[]{:S(2)}) collective-permute-start(bf16[1536,128]{1,0:T(8,128)(2,1)S(1)} %broadcast_select_fusion.rest_1_), channel_id=1, source_target_pairs={{0,2},{1,5},{2,0},{3,7},{4,6},{5,1},{6,4},{7,3},{8,10},{9,13},{10,... | collective-permute-start | bytes 1179656 | tf_op jit(solution)/shard_map/TuC/ppermute | solution.py:121
  53.1 7.8 %collective-permute-start.17 = (bf16[1536,128]{1,0:T(8,128)(2,1)S(1)}, bf16[1536,128]{1,0:T(8,128)(2,1)S(1)}, u32[]{:S(2)}, u32[]{:S(2)}) collective-permute-start(bf16[1536,128]{1,0:T(8,128)(2,1)S(1)} %broadcast_select_fusion.rest_1_), channel_id=1, source_target_pairs={{0,4},{1,3},{2,6},{3,1},{4,0},{5,7},{6,2},{7,5},{8,12},{9,11},{10,... | collective-permute-start | bytes 1179656 | tf_op jit(solution)/shard_map/TvC/ppermute | solution.py:121
  55.0 10.1 %collective-permute-start.13 = (bf16[1536,128]{1,0:T(8,128)(2,1)S(1)}, bf16[1536,128]{1,0:T(8,128)(2,1)S(1)}, u32[]{:S(2)}, u32[]{:S(2)}) collective-permute-start(bf16[1536,128]{1,0:T(8,128)(2,1)S(1)} %collective-permute-done.10.rest_3_), channel_id=1, source_target_pairs={{0,4},{1,3},{2,6},{3,1},{4,0},{5,7},{6,2},{7,5},{8,12},{9,11},{10,... | collective-permute-start | bytes 1179656 | tf_op jit(solution)/shard_map/TvuB/ppermute | solution.py:121
  55.1 13.3 %collective-permute-start.18 = (bf16[1536,128]{1,0:T(8,128)(2,1)S(1)}, bf16[1536,128]{1,0:T(8,128)(2,1)S(1)}, u32[]{:S(2)}, u32[]{:S(2)}) collective-permute-start(bf16[1536,128]{1,0:T(8,128)(2,1)S(1)} %collective-permute-done.5.rest_0_), channel_id=1, source_target_pairs={{0,8},{1,9},{2,10},{3,11},{4,12},{5,13},{6,14},{7,15},{8,0},{9,1},... | collective-permute-start | bytes 1179656 | tf_op jit(solution)/shard_map/TvuA/ppermute | solution.py:121
  58.7 10.6 %collective-permute-start.19 = (bf16[1536,128]{1,0:T(8,128)(2,1)S(1)}, bf16[1536,128]{1,0:T(8,128)(2,1)S(1)}, u32[]{:S(2)}, u32[]{:S(2)}) collective-permute-start(bf16[1536,128]{1,0:T(8,128)(2,1)S(1)} %collective-permute-done.16.rest_2_), channel_id=1, source_target_pairs={{0,4},{1,3},{2,6},{3,1},{4,0},{5,7},{6,2},{7,5},{8,12},{9,11},{10,... | collective-permute-start | bytes 1179656 | tf_op jit(solution)/shard_map/TvuC/ppermute | solution.py:121
  72.6 2.0 %collective-permute-start.20 = (bf16[2048,128]{1,0:T(8,128)(2,1)S(1)}, bf16[2048,128]{1,0:T(8,128)(2,1)S(1)}, u32[]{:S(2)}, u32[]{:S(2)}) collective-permute-start(bf16[2048,128]{1,0:T(8,128)(2,1)S(1)} %get-tuple-element.39.mine), channel_id=1, source_target_pairs={{0,1},{1,0},{2,3},{3,2},{4,5},{5,4},{6,7},{7,6},{8,9},{9,8},{10,11... | collective-permute-start | bytes 1572872 | tf_op jit(solution)/shard_map/ppermute | solution.py:121
  76.2 4.2 %collective-permute-start.21 = (f32[104,128]{1,0:T(8,128)S(1)}, f32[104,128]{1,0:T(8,128)S(1)}, u32[]{:S(2)}, u32[]{:S(2)}) collective-permute-start(f32[104,128]{1,0:T(8,128)S(1)} %get-tuple-element.41), channel_id=1, source_target_pairs={{0,2},{1,3},{2,0},{3,1},{4,6},{5,7},{6,4},{7,5},{8,10},{9,11},{10,... | collective-permute-start | bytes 159752 | tf_op jit(solution)/shard_map/ppermute | solution.py:121
  76.3 4.2 %collective-permute-start.22 = (f32[104,128]{1,0:T(8,128)S(1)}, f32[104,128]{1,0:T(8,128)S(1)}, u32[]{:S(2)}, u32[]{:S(2)}) collective-permute-start(f32[104,128]{1,0:T(8,128)S(1)} %get-tuple-element.42), channel_id=1, source_target_pairs={{0,4},{1,5},{2,6},{3,7},{4,0},{5,1},{6,2},{7,3},{8,12},{9,13},{10,... | collective-permute-start | bytes 159752 | tf_op jit(solution)/shard_map/ppermute | solution.py:121
  78.2 5.0 %collective-permute-start.23 = (f32[104,128]{1,0:T(8,128)S(1)}, f32[104,128]{1,0:T(8,128)S(1)}, u32[]{:S(2)}, u32[]{:S(2)}) collective-permute-start(f32[104,128]{1,0:T(8,128)S(1)} %get-tuple-element.43), channel_id=1, source_target_pairs={{0,6},{1,7},{2,4},{3,5},{4,2},{5,3},{6,0},{7,1},{8,14},{9,15},{10,... | collective-permute-start | bytes 159752 | tf_op jit(solution)/shard_map/ppermute | solution.py:121
  83.2 4.5 %collective-permute-start.24 = (f32[104,128]{1,0:T(8,128)S(1)}, f32[104,128]{1,0:T(8,128)S(1)}, u32[]{:S(2)}, u32[]{:S(2)}) collective-permute-start(f32[104,128]{1,0:T(8,128)S(1)} %add_add_fusion.1), channel_id=1, source_target_pairs={{0,8},{1,9},{2,10},{3,11},{4,12},{5,13},{6,14},{7,15},{8,0},{9,1},... | collective-permute-start | bytes 159752 | tf_op jit(solution)/shard_map/ppermute | solution.py:121
  84.0 5.4 %collective-permute-start.25 = (f32[104,128]{1,0:T(8,128)S(1)}, f32[104,128]{1,0:T(8,128)S(1)}, u32[]{:S(2)}, u32[]{:S(2)}) collective-permute-start(f32[104,128]{1,0:T(8,128)S(1)} %add_add_fusion.1), channel_id=1, source_target_pairs={{0,16},{1,17},{2,18},{3,19},{4,20},{5,21},{6,22},{7,23},{8,24},{9,... | collective-permute-start | bytes 159752 | tf_op jit(solution)/shard_map/ppermute | solution.py:121
  85.6 6.0 %collective-permute-start.26 = (f32[104,128]{1,0:T(8,128)S(1)}, f32[104,128]{1,0:T(8,128)S(1)}, u32[]{:S(2)}, u32[]{:S(2)}) collective-permute-start(f32[104,128]{1,0:T(8,128)S(1)} %add_add_fusion.1), channel_id=1, source_target_pairs={{0,24},{1,25},{2,26},{3,27},{4,28},{5,29},{6,30},{7,31},{8,16},{9,... | collective-permute-start | bytes 159752 | tf_op jit(solution)/shard_map/ppermute | solution.py:121
  91.7 4.2 %collective-permute-start.27 = (f32[104,128]{1,0:T(8,128)S(1)}, f32[104,128]{1,0:T(8,128)S(1)}, u32[]{:S(2)}, u32[]{:S(2)}) collective-permute-start(f32[104,128]{1,0:T(8,128)S(1)} %add_add_fusion.refs_0_), channel_id=1, source_target_pairs={{0,2},{1,3},{2,0},{3,1},{4,6},{5,7},{6,4},{7,5},{8,10},{9,11},{10,... | collective-permute-start | bytes 159752 | tf_op jit(solution)/shard_map/ppermute | solution.py:121
  93.3 4.1 %collective-permute-start.28 = (f32[104,128]{1,0:T(8,128)S(1)}, f32[104,128]{1,0:T(8,128)S(1)}, u32[]{:S(2)}, u32[]{:S(2)}) collective-permute-start(f32[104,128]{1,0:T(8,128)S(1)} %add_add_fusion.refs_0_), channel_id=1, source_target_pairs={{0,4},{1,5},{2,6},{3,7},{4,0},{5,1},{6,2},{7,3},{8,12},{9,13},{10,... | collective-permute-start | bytes 159752 | tf_op jit(solution)/shard_map/ppermute | solution.py:121
  93.6 5.0 %collective-permute-start.29 = (f32[104,128]{1,0:T(8,128)S(1)}, f32[104,128]{1,0:T(8,128)S(1)}, u32[]{:S(2)}, u32[]{:S(2)}) collective-permute-start(f32[104,128]{1,0:T(8,128)S(1)} %add_add_fusion.refs_0_), channel_id=1, source_target_pairs={{0,6},{1,7},{2,4},{3,5},{4,2},{5,3},{6,0},{7,1},{8,14},{9,15},{10,... | collective-permute-start | bytes 159752 | tf_op jit(solution)/shard_map/ppermute | solution.py:121
  95.2 3.4 %collective-permute-start.30 = (f32[104,128]{1,0:T(8,128)S(1)}, f32[104,128]{1,0:T(8,128)S(1)}, u32[]{:S(2)}, u32[]{:S(2)}) collective-permute-start(f32[104,128]{1,0:T(8,128)S(1)} %add_add_fusion.refs_0_), channel_id=1, source_target_pairs={{0,1},{1,0},{2,3},{3,2},{4,5},{5,4},{6,7},{7,6},{8,9},{9,8},{10,11... | collective-permute-start | bytes 159752 | tf_op jit(solution)/shard_map/ppermute | solution.py:121
  95.9 2.8 %collective-permute-start.31 = (f32[104,128]{1,0:T(8,128)S(1)}, f32[104,128]{1,0:T(8,128)S(1)}, u32[]{:S(2)}, u32[]{:S(2)}) collective-permute-start(f32[104,128]{1,0:T(8,128)S(1)} %collective-permute-done.27.refs_1_), channel_id=1, source_target_pairs={{0,1},{1,0},{2,3},{3,2},{4,5},{5,4},{6,7},{7,6},{8,9},{9,8},{10,11... | collective-permute-start | bytes 159752 | tf_op jit(solution)/shard_map/ppermute | solution.py:121
  (6 other events, 45.7 us)

commit v5 on v4

--- a/solution.py
+++ b/solution.py
@@ -423,7 +423,7 @@
     slot_a = named("TP1", z_pairs, panel)
     one_o = named("TuO", first_way, panel)
     two_o = named("TvO", second_way, panel)
-    near = named("TP2", z_middle, later)
+    near = named("TP2", z_middle, panel)
     both_o = named("TvuO", second_way, one_o)
     far = named("TP3b", z_middle, slot_a, one_o)
     one_a = named("TuA", first_way, slot_a, two_o)

time: 101 us -> 101 us (level)
  waiting for transfers between devices: 40 us -> 38.4 us
  starting transfers between devices: 35.7 us -> 37 us
    ppermute x34, waiting for transfers between devices: 40 us -> 38.4 us  [send(): return lax.ppermute(value, ('blk', 'rep'), pairs)]
    ppermute x34, starting transfers between devices: 35.7 us -> 37 us  [send(): return lax.ppermute(value, ('blk', 'rep'), pairs)]
where the time goes in v5:
time: 101 us; the launch traced here: 100 us
  waiting for transfers between devices  38.4 us (38%)
  starting transfers between devices  37 us (37%)
  Pallas kernels  22 us (22%)
  local copies, waits for them, and re-layouts  1.73 us (2%)
    ppermute x34, waiting for transfers between devices, send(): return lax.ppermute(value, ('blk', 'rep'), pairs)  38.4 us
    ppermute x34, starting transfers between devices, send(): return lax.ppermute(value, ('blk', 'rep'), pairs)  37 us
    pallas_call x5, Pallas kernels, gather_call(): pl.pallas_call(functools.partial(gather_kernel, kinds, near), out_shape=o...  16 us
    pallas_call x2, Pallas kernels, pack_call(): pl.pallas_call(functools.partial(pack_kernel, away), out_shape=pltpu.VMEM...  2.25 us
  transfers between devices with their start and end apart: 34, of which 19 were waited for; matrix products, arithmetic and copies ran while one was open for 0% of the time, Pallas kernels for 15%

profile of v5, /device:TPU:0, one launch (start us, length us, event | category | flops | bytes accessed | tf_op | source)
XLA Modules:
  0.0 100.1 jit_solution(8501048568539277234)
XLA Ops:
  3.8 2.8 %collective-permute-start.6 = (bf16[1536,128]{1,0:T(8,128)(2,1)S(1)}, bf16[1536,128]{1,0:T(8,128)(2,1)S(1)}, u32[]{:S(2)}, u32[]{:S(2)}) collective-permute-start(bf16[1536,128]{1,0:T(8,128)(2,1)S(1)} %constant_dynamic-update-slice_fusion.after.rest_0_), channel_id=1, source_target_pairs={{0,8},{1,9},{2,10},{3,11},{4,12},{5,13},{6,14},{7,15},{8,0},{9,1},... | collective-permute-start | bytes 1179656 | tf_op jit(solution)/shard_map/TP1/ppermute | solution.py:121
  6.6 1.5 %collective-permute-start.4 = (bf16[1536,128]{1,0:T(8,128)(2,1)S(1)}, bf16[1536,128]{1,0:T(8,128)(2,1)S(1)}, u32[]{:S(2)}, u32[]{:S(2)}) collective-permute-start(bf16[1536,128]{1,0:T(8,128)(2,1)S(1)} %constant_dynamic-update-slice_fusion.after.rest_0_), channel_id=1, source_target_pairs={{0,4},{1,3},{2,6},{3,1},{4,0},{5,7},{6,2},{7,5},{8,12},{9,11},{10,... | collective-permute-start | bytes 1179656 | tf_op jit(solution)/shard_map/TvO/ppermute | solution.py:121
  8.1 1.5 %collective-permute-start.3 = (bf16[1536,128]{1,0:T(8,128)(2,1)S(1)}, bf16[1536,128]{1,0:T(8,128)(2,1)S(1)}, u32[]{:S(2)}, u32[]{:S(2)}) collective-permute-start(bf16[1536,128]{1,0:T(8,128)(2,1)S(1)} %constant_dynamic-update-slice_fusion.after.rest_0_), channel_id=1, source_target_pairs={{0,2},{1,5},{2,0},{3,7},{4,6},{5,1},{6,4},{7,3},{8,10},{9,13},{10,... | collective-permute-start | bytes 1179656 | tf_op jit(solution)/shard_map/TuO/ppermute | solution.py:121
  10.3 5.9 %collective-permute-done.6.rest_1_ = bf16[1536,128]{1,0:T(8,128)(2,1)S(1)} collective-permute-done((bf16[1536,128]{1,0:T(8,128)(2,1)S(1)}, bf16[1536,128]{1,0:T(8,128)(2,1)S(1)}, u32[]{:S(2)}, u32[]{:S(2)}) %collective-permute-start.6) | collective-permute-done | bytes 393248 | tf_op jit(solution)/shard_map/TP1/ppermute | solution.py:121
  16.2 2.2 %collective-permute-done.4.rest_2_ = bf16[1536,128]{1,0:T(8,128)(2,1)S(1)} collective-permute-done((bf16[1536,128]{1,0:T(8,128)(2,1)S(1)}, bf16[1536,128]{1,0:T(8,128)(2,1)S(1)}, u32[]{:S(2)}, u32[]{:S(2)}) %collective-permute-start.4) | collective-permute-done | bytes 393248 | tf_op jit(solution)/shard_map/TvO/ppermute | solution.py:121
  20.1 1.6 %collective-permute-start.5 = (bf16[1536,128]{1,0:T(8,128)(2,1)S(1)}, bf16[1536,128]{1,0:T(8,128)(2,1)S(1)}, u32[]{:S(2)}, u32[]{:S(2)}) collective-permute-start(bf16[1536,128]{1,0:T(8,128)(2,1)S(1)} %collective-permute-done.3.rest_1_), channel_id=1, source_target_pairs={{0,4},{1,3},{2,6},{3,1},{4,0},{5,7},{6,2},{7,5},{8,12},{9,11},{10,... | collective-permute-start | bytes 1179656 | tf_op jit(solution)/shard_map/TvuO/ppermute | solution.py:121
  24.3 5.9 %collective-permute-done.7.rest_2_ = bf16[1536,128]{1,0:T(8,128)(2,1)S(1)} collective-permute-done((bf16[1536,128]{1,0:T(8,128)(2,1)S(1)}, bf16[1536,128]{1,0:T(8,128)(2,1)S(1)}, u32[]{:S(2)}, u32[]{:S(2)}) %collective-permute-start.7) | collective-permute-done | bytes 393248 | tf_op jit(solution)/shard_map/TuA/ppermute | solution.py:121
  30.2 1.5 %collective-permute-start.11 = (bf16[1536,128]{1,0:T(8,128)(2,1)S(1)}, bf16[1536,128]{1,0:T(8,128)(2,1)S(1)}, u32[]{:S(2)}, u32[]{:S(2)}) collective-permute-start(bf16[1536,128]{1,0:T(8,128)(2,1)S(1)} %collective-permute-done.6.rest_1_), channel_id=1, source_target_pairs={{0,4},{1,3},{2,6},{3,1},{4,0},{5,7},{6,2},{7,5},{8,12},{9,11},{10,... | collective-permute-start | bytes 1179656 | tf_op jit(solution)/shard_map/TvA/ppermute | solution.py:121
  34.2 1.8 %collective-permute-start.10 = (bf16[1536,128]{1,0:T(8,128)(2,1)S(1)}, bf16[1536,128]{1,0:T(8,128)(2,1)S(1)}, u32[]{:S(2)}, u32[]{:S(2)}) collective-permute-start(bf16[1536,128]{1,0:T(8,128)(2,1)S(1)} %broadcast_select_fusion.1.rest_1_), channel_id=1, source_target_pairs={{0,2},{1,5},{2,0},{3,7},{4,6},{5,1},{6,4},{7,3},{8,10},{9,13},{10,... | collective-permute-start | bytes 1179656 | tf_op jit(solution)/shard_map/TuB/ppermute | solution.py:121
  37.7 3.2 %TK0.1.start = f32[3,9,128,128]{3,2,1,0:T(8,128)S(1)} custom-call(s32[16,128]{1,0:T(8,128)S(1)} %copy-done.2, s32[16,128]{1,0:T(8,128)S(1)} %collective-permute-done.1.other_table, f32[8,128]{1,0:T(8,128)S(1)} %bitcast.7, bf16[8,12,128,128]{3,2,1,0:T(8,128)(2,1)} %bitcast.9, bf16[8,12,128,128]{3,2,1,0:T(8,128)(2,1)} %collective-permute-done.2.other, ...), custom_call_target="tpu_custom_call" | custom-call | flops 900000000 | bytes 2400000 | tf_op jit(solution)/shard_map/TK0/pallas_call | solution.py:303
  41.0 1.7 %collective-permute-start.12 = (bf16[1536,128]{1,0:T(8,128)(2,1)S(1)}, bf16[1536,128]{1,0:T(8,128)(2,1)S(1)}, u32[]{:S(2)}, u32[]{:S(2)}) collective-permute-start(bf16[1536,128]{1,0:T(8,128)(2,1)S(1)} %broadcast_select_fusion.1.rest_1_), channel_id=1, source_target_pairs={{0,4},{1,3},{2,6},{3,1},{4,0},{5,7},{6,2},{7,5},{8,12},{9,11},{10,... | collective-permute-start | bytes 1179656 | tf_op jit(solution)/shard_map/TvB/ppermute | solution.py:121
  43.9 1.6 %collective-permute-start.16 = (bf16[1536,128]{1,0:T(8,128)(2,1)S(1)}, bf16[1536,128]{1,0:T(8,128)(2,1)S(1)}, u32[]{:S(2)}, u32[]{:S(2)}) collective-permute-start(bf16[1536,128]{1,0:T(8,128)(2,1)S(1)} %broadcast_select_fusion.rest_1_), channel_id=1, source_target_pairs={{0,2},{1,5},{2,0},{3,7},{4,6},{5,1},{6,4},{7,3},{8,10},{9,13},{10,... | collective-permute-start | bytes 1179656 | tf_op jit(solution)/shard_map/TuC/ppermute | solution.py:121
  45.5 3.5 %TK1.1.start = f32[3,9,128,128]{3,2,1,0:T(8,128)S(1)} custom-call(s32[16,128]{1,0:T(8,128)S(1)} %copy-done.3, s32[16,128]{1,0:T(8,128)S(1)} %collective-permute-done.1.other_table, f32[3,9,128,128]{3,2,1,0:T(8,128)S(1)} %TK0.1.start, bf16[8,12,128,128]{3,2,1,0:T(8,128)(2,1)} %bitcast.10, ...), custom_call_target="tpu_custom_call", output_to_operand_aliasing={{}: (2, {})} | custom-call | flops 1200000000 | bytes 3200000 | tf_op jit(solution)/shard_map/TK1/pallas_call | solution.py:303
  49.1 3.1 %collective-permute-done.12.rest_2_ = bf16[1536,128]{1,0:T(8,128)(2,1)S(1)} collective-permute-done((bf16[1536,128]{1,0:T(8,128)(2,1)S(1)}, bf16[1536,128]{1,0:T(8,128)(2,1)S(1)}, u32[]{:S(2)}, u32[]{:S(2)}) %collective-permute-start.12) | collective-permute-done | bytes 393248 | tf_op jit(solution)/shard_map/TvB/ppermute | solution.py:121
  52.2 1.6 %collective-permute-start.17 = (bf16[1536,128]{1,0:T(8,128)(2,1)S(1)}, bf16[1536,128]{1,0:T(8,128)(2,1)S(1)}, u32[]{:S(2)}, u32[]{:S(2)}) collective-permute-start(bf16[1536,128]{1,0:T(8,128)(2,1)S(1)} %broadcast_select_fusion.rest_1_), channel_id=1, source_target_pairs={{0,4},{1,3},{2,6},{3,1},{4,0},{5,7},{6,2},{7,5},{8,12},{9,11},{10,... | collective-permute-start | bytes 1179656 | tf_op jit(solution)/shard_map/TvC/ppermute | solution.py:121
  55.5 2.8 %TK2.1.start = f32[3,9,128,128]{3,2,1,0:T(8,128)S(1)} custom-call(s32[16,128]{1,0:T(8,128)S(1)} %copy-done.3, s32[16,128]{1,0:T(8,128)S(1)} %collective-permute-done.1.other_table, f32[3,9,128,128]{3,2,1,0:T(8,128)S(1)} %TK1.1.start, bf16[8,12,128,128]{3,2,1,0:T(8,128)(2,1)} %bitcast.11, ...), custom_call_target="tpu_custom_call", output_to_operand_aliasing={{}: (2, {})} | custom-call | flops 900000000 | bytes 2400000 | tf_op jit(solution)/shard_map/TK2/pallas_call | solution.py:303
  58.3 2.1 %collective-permute-start.19 = (bf16[1536,128]{1,0:T(8,128)(2,1)S(1)}, bf16[1536,128]{1,0:T(8,128)(2,1)S(1)}, u32[]{:S(2)}, u32[]{:S(2)}) collective-permute-start(bf16[1536,128]{1,0:T(8,128)(2,1)S(1)} %collective-permute-done.16.rest_2_), channel_id=1, source_target_pairs={{0,4},{1,3},{2,6},{3,1},{4,0},{5,7},{6,2},{7,5},{8,12},{9,11},{10,... | collective-permute-start | bytes 1179656 | tf_op jit(solution)/shard_map/TvuC/ppermute | solution.py:121
  60.4 3.8 %collective-permute-done.13.rest_0_ = bf16[1536,128]{1,0:T(8,128)(2,1)S(1)} collective-permute-done((bf16[1536,128]{1,0:T(8,128)(2,1)S(1)}, bf16[1536,128]{1,0:T(8,128)(2,1)S(1)}, u32[]{:S(2)}, u32[]{:S(2)}) %collective-permute-start.13) | collective-permute-done | bytes 393248 | tf_op jit(solution)/shard_map/TvuB/ppermute | solution.py:121
  64.2 3.2 %TK3.1.start = f32[3,9,128,128]{3,2,1,0:T(8,128)S(1)} custom-call(s32[16,128]{1,0:T(8,128)S(1)} %copy-done.3, s32[16,128]{1,0:T(8,128)S(1)} %collective-permute-done.1.other_table, f32[3,9,128,128]{3,2,1,0:T(8,128)S(1)} %TK2.1.start, bf16[8,12,128,128]{3,2,1,0:T(8,128)(2,1)} %bitcast.12, ...), custom_call_target="tpu_custom_call", output_to_operand_aliasing={{}: (2, {})} | custom-call | flops 1200000000 | bytes 3200000 | tf_op jit(solution)/shard_map/TK3/pallas_call | solution.py:303
  68.4 3.3 %TK4.1 = (f32[3,9,128,128]{3,2,1,0:T(8,128)S(1)}, bf16[2048,128]{1,0:T(8,128)(2,1)S(1)}) custom-call(s32[16,128]{1,0:T(8,128)S(1)} %copy-done.3, s32[16,128]{1,0:T(8,128)S(1)} %collective-permute-done.1.other_table, f32[3,9,128,128]{3,2,1,0:T(8,128)S(1)} %TK3.1.start, bf16[8,12,128,128]{3,2,1,0:T(8,128)(2,1)} %bitcast.13, ...), custom_call_target="tpu_custom_call", output_to_operand_aliasing={{0}: (2, {})} | custom-call | flops 600000000 | bytes 1600000 | tf_op jit(solution)/shard_map/TK4/pallas_call | solution.py:303
  71.8 1.9 %collective-permute-done.20.theirs = bf16[2048,128]{1,0:T(8,128)(2,1)S(1)} collective-permute-done((bf16[2048,128]{1,0:T(8,128)(2,1)S(1)}, bf16[2048,128]{1,0:T(8,128)(2,1)S(1)}, u32[]{:S(2)}, u32[]{:S(2)}) %collective-permute-start.20) | collective-permute-done | bytes 524320 | tf_op jit(solution)/shard_map/ppermute | solution.py:121
  73.6 1.6 %shard_map.133 = (f32[104,128]{1,0:T(8,128)S(1)}, f32[104,128]{1,0:T(8,128)S(1)}, f32[104,128]{1,0:T(8,128)S(1)}, f32[104,128]{1,0:T(8,128)S(1)}) custom-call(bf16[2048,128]{1,0:T(8,128)(2,1)S(1)} %get-tuple-element.37.mine, bf16[2048,128]{1,0:T(8,128)(2,1)S(1)} %collective-permute-done.20.theirs, bf16[128,256]{1,0:T(8,128)(2,1)} %w_first.1, ...), custom_call_target="tpu_custom_call" | custom-call | tf_op jit(solution)/shard_map/pallas_call | solution.py:449
  75.4 1.6 %collective-permute-start.22 = (f32[104,128]{1,0:T(8,128)S(1)}, f32[104,128]{1,0:T(8,128)S(1)}, u32[]{:S(2)}, u32[]{:S(2)}) collective-permute-start(f32[104,128]{1,0:T(8,128)S(1)} %get-tuple-element.40), channel_id=1, source_target_pairs={{0,4},{1,5},{2,6},{3,7},{4,0},{5,1},{6,2},{7,3},{8,12},{9,13},{10,... | collective-permute-start | bytes 159752 | tf_op jit(solution)/shard_map/ppermute | solution.py:121
  77.0 1.9 %collective-permute-start.23 = (f32[104,128]{1,0:T(8,128)S(1)}, f32[104,128]{1,0:T(8,128)S(1)}, u32[]{:S(2)}, u32[]{:S(2)}) collective-permute-start(f32[104,128]{1,0:T(8,128)S(1)} %get-tuple-element.41), channel_id=1, source_target_pairs={{0,6},{1,7},{2,4},{3,5},{4,2},{5,3},{6,0},{7,1},{8,14},{9,15},{10,... | collective-permute-start | bytes 159752 | tf_op jit(solution)/shard_map/ppermute | solution.py:121
  79.7 2.3 %collective-permute-done.23 = f32[104,128]{1,0:T(8,128)S(1)} collective-permute-done((f32[104,128]{1,0:T(8,128)S(1)}, f32[104,128]{1,0:T(8,128)S(1)}, u32[]{:S(2)}, u32[]{:S(2)}) %collective-permute-start.23) | collective-permute-done | bytes 53280 | tf_op jit(solution)/shard_map/ppermute | solution.py:121
  83.2 2.1 %collective-permute-start.25 = (f32[104,128]{1,0:T(8,128)S(1)}, f32[104,128]{1,0:T(8,128)S(1)}, u32[]{:S(2)}, u32[]{:S(2)}) collective-permute-start(f32[104,128]{1,0:T(8,128)S(1)} %add_add_fusion.1), channel_id=1, source_target_pairs={{0,16},{1,17},{2,18},{3,19},{4,20},{5,21},{6,22},{7,23},{8,24},{9,... | collective-permute-start | bytes 159752 | tf_op jit(solution)/shard_map/ppermute | solution.py:121
  85.3 1.4 %collective-permute-start.26 = (f32[104,128]{1,0:T(8,128)S(1)}, f32[104,128]{1,0:T(8,128)S(1)}, u32[]{:S(2)}, u32[]{:S(2)}) collective-permute-start(f32[104,128]{1,0:T(8,128)S(1)} %add_add_fusion.1), channel_id=1, source_target_pairs={{0,24},{1,25},{2,26},{3,27},{4,28},{5,29},{6,30},{7,31},{8,16},{9,... | collective-permute-start | bytes 159752 | tf_op jit(solution)/shard_map/ppermute | solution.py:121
  86.7 2.2 %collective-permute-done.25 = f32[104,128]{1,0:T(8,128)S(1)} collective-permute-done((f32[104,128]{1,0:T(8,128)S(1)}, f32[104,128]{1,0:T(8,128)S(1)}, u32[]{:S(2)}, u32[]{:S(2)}) %collective-permute-start.25) | collective-permute-done | bytes 53280 | tf_op jit(solution)/shard_map/ppermute | solution.py:121
  88.9 2.4 %collective-permute-done.26 = f32[104,128]{1,0:T(8,128)S(1)} collective-permute-done((f32[104,128]{1,0:T(8,128)S(1)}, f32[104,128]{1,0:T(8,128)S(1)}, u32[]{:S(2)}, u32[]{:S(2)}) %collective-permute-start.26) | collective-permute-done | bytes 53280 | tf_op jit(solution)/shard_map/ppermute | solution.py:121
  91.4 1.5 %collective-permute-start.27 = (f32[104,128]{1,0:T(8,128)S(1)}, f32[104,128]{1,0:T(8,128)S(1)}, u32[]{:S(2)}, u32[]{:S(2)}) collective-permute-start(f32[104,128]{1,0:T(8,128)S(1)} %add_add_fusion.refs_0_), channel_id=1, source_target_pairs={{0,2},{1,3},{2,0},{3,1},{4,6},{5,7},{6,4},{7,5},{8,10},{9,11},{10,... | collective-permute-start | bytes 159752 | tf_op jit(solution)/shard_map/ppermute | solution.py:121
  93.0 1.9 %collective-permute-start.29 = (f32[104,128]{1,0:T(8,128)S(1)}, f32[104,128]{1,0:T(8,128)S(1)}, u32[]{:S(2)}, u32[]{:S(2)}) collective-permute-start(f32[104,128]{1,0:T(8,128)S(1)} %add_add_fusion.refs_0_), channel_id=1, source_target_pairs={{0,6},{1,7},{2,4},{3,5},{4,2},{5,3},{6,0},{7,1},{8,14},{9,15},{10,... | collective-permute-start | bytes 159752 | tf_op jit(solution)/shard_map/ppermute | solution.py:121
  95.6 1.4 %collective-permute-done.28.refs_2_ = f32[104,128]{1,0:T(8,128)S(1)} collective-permute-done((f32[104,128]{1,0:T(8,128)S(1)}, f32[104,128]{1,0:T(8,128)S(1)}, u32[]{:S(2)}, u32[]{:S(2)}) %collective-permute-start.28) | collective-permute-done | bytes 53280 | tf_op jit(solution)/shard_map/ppermute | solution.py:121
  (61 shorter events, 22.6 us)
Async XLA Ops:
  1.8 1.6 %collective-permute-start = (bf16[768,128]{1,0:T(8,128)(2,1)S(1)}, bf16[768,128]{1,0:T(8,128)(2,1)S(1)}, u32[]{:S(2)}, u32[]{:S(2)}) collective-permute-start(bf16[768,128]{1,0:T(8,128)(2,1)S(1)} %shard_map.131), channel_id=1, source_target_pairs={{0,1},{1,0},{2,3},{3,2},{4,5},{5,4},{6,7},{7,6},{8,9},{9,8},{10,11... | collective-permute-start | bytes 589832 | tf_op jit(solution)/shard_map/ppermute | solution.py:121
  3.5 30.7 %collective-permute-start.2 = (bf16[8,12,128,128]{3,2,1,0:T(8,128)(2,1)}, bf16[8,12,128,128]{3,2,1,0:T(8,128)(2,1)}, u32[]{:S(2)}, u32[]{:S(2)}) collective-permute-start(bf16[8,12,128,128]{3,2,1,0:T(8,128)(2,1)} %bitcast.8), channel_id=1, source_target_pairs={{0,1},{1,0},{2,3},{3,2},{4,5},{5,4},{6,7},{7,6},{8,9},{9,8},{10,11... | collective-permute-start | bytes 9437192 | tf_op jit(solution)/shard_map/ppermute | solution.py:121
  3.8 12.4 %collective-permute-start.6 = (bf16[1536,128]{1,0:T(8,128)(2,1)S(1)}, bf16[1536,128]{1,0:T(8,128)(2,1)S(1)}, u32[]{:S(2)}, u32[]{:S(2)}) collective-permute-start(bf16[1536,128]{1,0:T(8,128)(2,1)S(1)} %constant_dynamic-update-slice_fusion.after.rest_0_), channel_id=1, source_target_pairs={{0,8},{1,9},{2,10},{3,11},{4,12},{5,13},{6,14},{7,15},{8,0},{9,1},... | collective-permute-start | bytes 1179656 | tf_op jit(solution)/shard_map/TP1/ppermute | solution.py:121
  6.6 11.7 %collective-permute-start.4 = (bf16[1536,128]{1,0:T(8,128)(2,1)S(1)}, bf16[1536,128]{1,0:T(8,128)(2,1)S(1)}, u32[]{:S(2)}, u32[]{:S(2)}) collective-permute-start(bf16[1536,128]{1,0:T(8,128)(2,1)S(1)} %constant_dynamic-update-slice_fusion.after.rest_0_), channel_id=1, source_target_pairs={{0,4},{1,3},{2,6},{3,1},{4,0},{5,7},{6,2},{7,5},{8,12},{9,11},{10,... | collective-permute-start | bytes 1179656 | tf_op jit(solution)/shard_map/TvO/ppermute | solution.py:121
  8.1 11.3 %collective-permute-start.3 = (bf16[1536,128]{1,0:T(8,128)(2,1)S(1)}, bf16[1536,128]{1,0:T(8,128)(2,1)S(1)}, u32[]{:S(2)}, u32[]{:S(2)}) collective-permute-start(bf16[1536,128]{1,0:T(8,128)(2,1)S(1)} %constant_dynamic-update-slice_fusion.after.rest_0_), channel_id=1, source_target_pairs={{0,2},{1,5},{2,0},{3,7},{4,6},{5,1},{6,4},{7,3},{8,10},{9,13},{10,... | collective-permute-start | bytes 1179656 | tf_op jit(solution)/shard_map/TuO/ppermute | solution.py:121
  9.6 12.0 %collective-permute-start.8 = (bf16[1536,128]{1,0:T(8,128)(2,1)S(1)}, bf16[1536,128]{1,0:T(8,128)(2,1)S(1)}, u32[]{:S(2)}, u32[]{:S(2)}) collective-permute-start(bf16[1536,128]{1,0:T(8,128)(2,1)S(1)} %constant_dynamic-update-slice_fusion.after.rest_0_), channel_id=1, source_target_pairs={{8,16},{9,17},{10,18},{11,19},{12,20},{13,21},{14,22},{15,23},{16,... | collective-permute-start | bytes 1179656 | tf_op jit(solution)/shard_map/TP2/ppermute | solution.py:121
  18.4 11.9 %collective-permute-start.7 = (bf16[1536,128]{1,0:T(8,128)(2,1)S(1)}, bf16[1536,128]{1,0:T(8,128)(2,1)S(1)}, u32[]{:S(2)}, u32[]{:S(2)}) collective-permute-start(bf16[1536,128]{1,0:T(8,128)(2,1)S(1)} %collective-permute-done.6.rest_1_), channel_id=1, source_target_pairs={{0,2},{1,5},{2,0},{3,7},{4,6},{5,1},{6,4},{7,3},{8,10},{9,13},{10,... | collective-permute-start | bytes 1179656 | tf_op jit(solution)/shard_map/TuA/ppermute | solution.py:121
  19.4 10.8 %collective-permute-start.14 = (bf16[1536,128]{1,0:T(8,128)(2,1)S(1)}, bf16[1536,128]{1,0:T(8,128)(2,1)S(1)}, u32[]{:S(2)}, u32[]{:S(2)}) collective-permute-start(bf16[1536,128]{1,0:T(8,128)(2,1)S(1)} %collective-permute-done.6.rest_1_), channel_id=1, source_target_pairs={{8,16},{9,17},{10,18},{11,19},{12,20},{13,21},{14,22},{15,23},{16,... | collective-permute-start | bytes 1179656 | tf_op jit(solution)/shard_map/TP3b/ppermute | solution.py:121
  20.1 11.7 %collective-permute-start.5 = (bf16[1536,128]{1,0:T(8,128)(2,1)S(1)}, bf16[1536,128]{1,0:T(8,128)(2,1)S(1)}, u32[]{:S(2)}, u32[]{:S(2)}) collective-permute-start(bf16[1536,128]{1,0:T(8,128)(2,1)S(1)} %collective-permute-done.3.rest_1_), channel_id=1, source_target_pairs={{0,4},{1,3},{2,6},{3,1},{4,0},{5,7},{6,2},{7,5},{8,12},{9,11},{10,... | collective-permute-start | bytes 1179656 | tf_op jit(solution)/shard_map/TvuO/ppermute | solution.py:121
  21.7 12.5 %collective-permute-start.9 = (bf16[1536,128]{1,0:T(8,128)(2,1)S(1)}, bf16[1536,128]{1,0:T(8,128)(2,1)S(1)}, u32[]{:S(2)}, u32[]{:S(2)}) collective-permute-start(bf16[1536,128]{1,0:T(8,128)(2,1)S(1)} %collective-permute-done.8), channel_id=1, source_target_pairs={{8,0},{9,1},{10,2},{11,3},{12,4},{13,5},{14,6},{15,7},{16,24},{17,... | collective-permute-start | bytes 1179656 | tf_op jit(solution)/shard_map/TP3a/ppermute | solution.py:121
  30.2 5.8 %collective-permute-start.1 = (s32[16,128]{1,0:T(8,128)}, s32[16,128]{1,0:T(8,128)S(1)}, u32[]{:S(2)}, u32[]{:S(2)}) collective-permute-start(s32[16,128]{1,0:T(8,128)} %shard_map.132.own_table), channel_id=1, source_target_pairs={{0,1},{1,0},{2,3},{3,2},{4,5},{5,4},{6,7},{7,6},{8,9},{9,8},{10,11... | collective-permute-start | bytes 24584 | tf_op jit(solution)/shard_map/ppermute | solution.py:121
  30.2 10.7 %collective-permute-start.11 = (bf16[1536,128]{1,0:T(8,128)(2,1)S(1)}, bf16[1536,128]{1,0:T(8,128)(2,1)S(1)}, u32[]{:S(2)}, u32[]{:S(2)}) collective-permute-start(bf16[1536,128]{1,0:T(8,128)(2,1)S(1)} %collective-permute-done.6.rest_1_), channel_id=1, source_target_pairs={{0,4},{1,3},{2,6},{3,1},{4,0},{5,7},{6,2},{7,5},{8,12},{9,11},{10,... | collective-permute-start | bytes 1179656 | tf_op jit(solution)/shard_map/TvA/ppermute | solution.py:121
  31.8 12.1 %collective-permute-start.15 = (bf16[1536,128]{1,0:T(8,128)(2,1)S(1)}, bf16[1536,128]{1,0:T(8,128)(2,1)S(1)}, u32[]{:S(2)}, u32[]{:S(2)}) collective-permute-start(bf16[1536,128]{1,0:T(8,128)(2,1)S(1)} %collective-permute-done.14), channel_id=1, source_target_pairs={{8,0},{9,1},{10,2},{11,3},{12,4},{13,5},{14,6},{15,7},{16,24},{17,... | collective-permute-start | bytes 1179656 | tf_op jit(solution)/shard_map/TP4/ppermute | solution.py:121
  34.2 11.3 %collective-permute-start.10 = (bf16[1536,128]{1,0:T(8,128)(2,1)S(1)}, bf16[1536,128]{1,0:T(8,128)(2,1)S(1)}, u32[]{:S(2)}, u32[]{:S(2)}) collective-permute-start(bf16[1536,128]{1,0:T(8,128)(2,1)S(1)} %broadcast_select_fusion.1.rest_1_), channel_id=1, source_target_pairs={{0,2},{1,5},{2,0},{3,7},{4,6},{5,1},{6,4},{7,3},{8,10},{9,13},{10,... | collective-permute-start | bytes 1179656 | tf_op jit(solution)/shard_map/TuB/ppermute | solution.py:121
  41.0 11.2 %collective-permute-start.12 = (bf16[1536,128]{1,0:T(8,128)(2,1)S(1)}, bf16[1536,128]{1,0:T(8,128)(2,1)S(1)}, u32[]{:S(2)}, u32[]{:S(2)}) collective-permute-start(bf16[1536,128]{1,0:T(8,128)(2,1)S(1)} %broadcast_select_fusion.1.rest_1_), channel_id=1, source_target_pairs={{0,4},{1,3},{2,6},{3,1},{4,0},{5,7},{6,2},{7,5},{8,12},{9,11},{10,... | collective-permute-start | bytes 1179656 | tf_op jit(solution)/shard_map/TvB/ppermute | solution.py:121
  43.9 14.3 %collective-permute-start.16 = (bf16[1536,128]{1,0:T(8,128)(2,1)S(1)}, bf16[1536,128]{1,0:T(8,128)(2,1)S(1)}, u32[]{:S(2)}, u32[]{:S(2)}) collective-permute-start(bf16[1536,128]{1,0:T(8,128)(2,1)S(1)} %broadcast_select_fusion.rest_1_), channel_id=1, source_target_pairs={{0,2},{1,5},{2,0},{3,7},{4,6},{5,1},{6,4},{7,3},{8,10},{9,13},{10,... | collective-permute-start | bytes 1179656 | tf_op jit(solution)/shard_map/TuC/ppermute | solution.py:121
  52.2 8.2 %collective-permute-start.17 = (bf16[1536,128]{1,0:T(8,128)(2,1)S(1)}, bf16[1536,128]{1,0:T(8,128)(2,1)S(1)}, u32[]{:S(2)}, u32[]{:S(2)}) collective-permute-start(bf16[1536,128]{1,0:T(8,128)(2,1)S(1)} %broadcast_select_fusion.rest_1_), channel_id=1, source_target_pairs={{0,4},{1,3},{2,6},{3,1},{4,0},{5,7},{6,2},{7,5},{8,12},{9,11},{10,... | collective-permute-start | bytes 1179656 | tf_op jit(solution)/shard_map/TvC/ppermute | solution.py:121
  53.8 10.4 %collective-permute-start.13 = (bf16[1536,128]{1,0:T(8,128)(2,1)S(1)}, bf16[1536,128]{1,0:T(8,128)(2,1)S(1)}, u32[]{:S(2)}, u32[]{:S(2)}) collective-permute-start(bf16[1536,128]{1,0:T(8,128)(2,1)S(1)} %collective-permute-done.10.rest_3_), channel_id=1, source_target_pairs={{0,4},{1,3},{2,6},{3,1},{4,0},{5,7},{6,2},{7,5},{8,12},{9,11},{10,... | collective-permute-start | bytes 1179656 | tf_op jit(solution)/shard_map/TvuB/ppermute | solution.py:121
  54.2 13.2 %collective-permute-start.18 = (bf16[1536,128]{1,0:T(8,128)(2,1)S(1)}, bf16[1536,128]{1,0:T(8,128)(2,1)S(1)}, u32[]{:S(2)}, u32[]{:S(2)}) collective-permute-start(bf16[1536,128]{1,0:T(8,128)(2,1)S(1)} %collective-permute-done.5.rest_0_), channel_id=1, source_target_pairs={{0,8},{1,9},{2,10},{3,11},{4,12},{5,13},{6,14},{7,15},{8,0},{9,1},... | collective-permute-start | bytes 1179656 | tf_op jit(solution)/shard_map/TvuA/ppermute | solution.py:121
  58.3 10.1 %collective-permute-start.19 = (bf16[1536,128]{1,0:T(8,128)(2,1)S(1)}, bf16[1536,128]{1,0:T(8,128)(2,1)S(1)}, u32[]{:S(2)}, u32[]{:S(2)}) collective-permute-start(bf16[1536,128]{1,0:T(8,128)(2,1)S(1)} %collective-permute-done.16.rest_2_), channel_id=1, source_target_pairs={{0,4},{1,3},{2,6},{3,1},{4,0},{5,7},{6,2},{7,5},{8,12},{9,11},{10,... | collective-permute-start | bytes 1179656 | tf_op jit(solution)/shard_map/TvuC/ppermute | solution.py:121
  71.7 2.0 %collective-permute-start.20 = (bf16[2048,128]{1,0:T(8,128)(2,1)S(1)}, bf16[2048,128]{1,0:T(8,128)(2,1)S(1)}, u32[]{:S(2)}, u32[]{:S(2)}) collective-permute-start(bf16[2048,128]{1,0:T(8,128)(2,1)S(1)} %get-tuple-element.37.mine), channel_id=1, source_target_pairs={{0,1},{1,0},{2,3},{3,2},{4,5},{5,4},{6,7},{7,6},{8,9},{9,8},{10,11... | collective-permute-start | bytes 1572872 | tf_op jit(solution)/shard_map/ppermute | solution.py:121
  75.3 4.4 %collective-permute-start.21 = (f32[104,128]{1,0:T(8,128)S(1)}, f32[104,128]{1,0:T(8,128)S(1)}, u32[]{:S(2)}, u32[]{:S(2)}) collective-permute-start(f32[104,128]{1,0:T(8,128)S(1)} %get-tuple-element.39), channel_id=1, source_target_pairs={{0,2},{1,3},{2,0},{3,1},{4,6},{5,7},{6,4},{7,5},{8,10},{9,11},{10,... | collective-permute-start | bytes 159752 | tf_op jit(solution)/shard_map/ppermute | solution.py:121
  75.4 4.3 %collective-permute-start.22 = (f32[104,128]{1,0:T(8,128)S(1)}, f32[104,128]{1,0:T(8,128)S(1)}, u32[]{:S(2)}, u32[]{:S(2)}) collective-permute-start(f32[104,128]{1,0:T(8,128)S(1)} %get-tuple-element.40), channel_id=1, source_target_pairs={{0,4},{1,5},{2,6},{3,7},{4,0},{5,1},{6,2},{7,3},{8,12},{9,13},{10,... | collective-permute-start | bytes 159752 | tf_op jit(solution)/shard_map/ppermute | solution.py:121
  77.0 5.0 %collective-permute-start.23 = (f32[104,128]{1,0:T(8,128)S(1)}, f32[104,128]{1,0:T(8,128)S(1)}, u32[]{:S(2)}, u32[]{:S(2)}) collective-permute-start(f32[104,128]{1,0:T(8,128)S(1)} %get-tuple-element.41), channel_id=1, source_target_pairs={{0,6},{1,7},{2,4},{3,5},{4,2},{5,3},{6,0},{7,1},{8,14},{9,15},{10,... | collective-permute-start | bytes 159752 | tf_op jit(solution)/shard_map/ppermute | solution.py:121
  82.0 4.7 %collective-permute-start.24 = (f32[104,128]{1,0:T(8,128)S(1)}, f32[104,128]{1,0:T(8,128)S(1)}, u32[]{:S(2)}, u32[]{:S(2)}) collective-permute-start(f32[104,128]{1,0:T(8,128)S(1)} %add_add_fusion.1), channel_id=1, source_target_pairs={{0,8},{1,9},{2,10},{3,11},{4,12},{5,13},{6,14},{7,15},{8,0},{9,1},... | collective-permute-start | bytes 159752 | tf_op jit(solution)/shard_map/ppermute | solution.py:121
  83.2 5.7 %collective-permute-start.25 = (f32[104,128]{1,0:T(8,128)S(1)}, f32[104,128]{1,0:T(8,128)S(1)}, u32[]{:S(2)}, u32[]{:S(2)}) collective-permute-start(f32[104,128]{1,0:T(8,128)S(1)} %add_add_fusion.1), channel_id=1, source_target_pairs={{0,16},{1,17},{2,18},{3,19},{4,20},{5,21},{6,22},{7,23},{8,24},{9,... | collective-permute-start | bytes 159752 | tf_op jit(solution)/shard_map/ppermute | solution.py:121
  85.3 6.0 %collective-permute-start.26 = (f32[104,128]{1,0:T(8,128)S(1)}, f32[104,128]{1,0:T(8,128)S(1)}, u32[]{:S(2)}, u32[]{:S(2)}) collective-permute-start(f32[104,128]{1,0:T(8,128)S(1)} %add_add_fusion.1), channel_id=1, source_target_pairs={{0,24},{1,25},{2,26},{3,27},{4,28},{5,29},{6,30},{7,31},{8,16},{9,... | collective-permute-start | bytes 159752 | tf_op jit(solution)/shard_map/ppermute | solution.py:121
  91.4 4.2 %collective-permute-start.27 = (f32[104,128]{1,0:T(8,128)S(1)}, f32[104,128]{1,0:T(8,128)S(1)}, u32[]{:S(2)}, u32[]{:S(2)}) collective-permute-start(f32[104,128]{1,0:T(8,128)S(1)} %add_add_fusion.refs_0_), channel_id=1, source_target_pairs={{0,2},{1,3},{2,0},{3,1},{4,6},{5,7},{6,4},{7,5},{8,10},{9,11},{10,... | collective-permute-start | bytes 159752 | tf_op jit(solution)/shard_map/ppermute | solution.py:121
  92.8 4.1 %collective-permute-start.28 = (f32[104,128]{1,0:T(8,128)S(1)}, f32[104,128]{1,0:T(8,128)S(1)}, u32[]{:S(2)}, u32[]{:S(2)}) collective-permute-start(f32[104,128]{1,0:T(8,128)S(1)} %add_add_fusion.refs_0_), channel_id=1, source_target_pairs={{0,4},{1,5},{2,6},{3,7},{4,0},{5,1},{6,2},{7,3},{8,12},{9,13},{10,... | collective-permute-start | bytes 159752 | tf_op jit(solution)/shard_map/ppermute | solution.py:121
  93.0 5.0 %collective-permute-start.29 = (f32[104,128]{1,0:T(8,128)S(1)}, f32[104,128]{1,0:T(8,128)S(1)}, u32[]{:S(2)}, u32[]{:S(2)}) collective-permute-start(f32[104,128]{1,0:T(8,128)S(1)} %add_add_fusion.refs_0_), channel_id=1, source_target_pairs={{0,6},{1,7},{2,4},{3,5},{4,2},{5,3},{6,0},{7,1},{8,14},{9,15},{10,... | collective-permute-start | bytes 159752 | tf_op jit(solution)/shard_map/ppermute | solution.py:121
  94.9 3.1 %collective-permute-start.30 = (f32[104,128]{1,0:T(8,128)S(1)}, f32[104,128]{1,0:T(8,128)S(1)}, u32[]{:S(2)}, u32[]{:S(2)}) collective-permute-start(f32[104,128]{1,0:T(8,128)S(1)} %add_add_fusion.refs_0_), channel_id=1, source_target_pairs={{0,1},{1,0},{2,3},{3,2},{4,5},{5,4},{6,7},{7,6},{8,9},{9,8},{10,11... | collective-permute-start | bytes 159752 | tf_op jit(solution)/shard_map/ppermute | solution.py:121
  95.6 2.5 %collective-permute-start.31 = (f32[104,128]{1,0:T(8,128)S(1)}, f32[104,128]{1,0:T(8,128)S(1)}, u32[]{:S(2)}, u32[]{:S(2)}) collective-permute-start(f32[104,128]{1,0:T(8,128)S(1)} %collective-permute-done.27.refs_1_), channel_id=1, source_target_pairs={{0,1},{1,0},{2,3},{3,2},{4,5},{5,4},{6,7},{7,6},{8,9},{9,8},{10,11... | collective-permute-start | bytes 159752 | tf_op jit(solution)/shard_map/ppermute | solution.py:121
  (7 other events, 66.9 us)
